TPU v7x, 32 devices: a whole 2x2x4 slice. The times are simulated.
32 devices in a mesh: dp: 8 (over y, x, core), mp: 4 (over z).
Axes of the slice: x: 2, y: 2, z: 4, core: 2. Of those that a mesh axis runs over, the one named last changes fastest.
Arguments:
- tokens_in: bfloat16 [1024, 5120], P('dp'), may hold values from -6 to 6
- cotangent: bfloat16 [1024, 10240], P('dp', 'mp'), may hold values from -6 to 6
- old_weights: bfloat16 [112, 128, 128], P('mp'), may hold values from -0.25 to 0.25
- old_first: float32 [112, 16384], P('mp', 'dp'), may hold values from -6 to 6
- old_second: float32 [112, 16384], P('mp', 'dp'), may hold values from 0.25 to 4
- new_coords: int32 [80, 2], replicated, may hold values from 0 to 79, as said below
- moved_to: int32 [112], replicated, may hold values from -1 to 79, as said below
Outputs:
- activated: bfloat16 [1024, 10240], P('dp', 'mp')
- input_grads: bfloat16 [1024, 5120], P('dp', 'mp')
- new_weights: bfloat16 [80, 128, 128], P('mp')
- new_first: float32 [80, 16384], P('mp', 'dp')
- new_second: float32 [80, 16384], P('mp', 'dp')
Inputs may be any that keep to these rules, and one draw needn't show every extreme that they name: new_coords[b] is (row block, column block) of new slot b, owned by mp index b // 20; no two slots share a cell. Call the column blocks of one index of mp a band; no owner has more than 11 blocks in one band, and in every draw some band holds exactly 11 blocks of every owner. moved_to[o] is the new slot that old slot o (held by mp index o // 28) moves to, or -1 where the old block is pruned or the slot is empty. Each new slot is named at most once; new slots that no old slot names are regrown. At most 7 blocks move from one old owner to one new owner; in every draw every new owner receives exactly 7 from some old owner, and some new owner receives 20 blocks in all.
All inputs are finite; a program needn't handle non-finite values.
Results may differ from a plain program's by a relative error of at most 0.0055.
Values may be sent and summed in bfloat16 or wider, within the bound.
No kernel may reach another device: no remote copies, remote signals or barrier semaphores. Data moves between devices by JAX's collectives and lax.ppermute only.
A program may use at most 64 MiB of HBM per device.

v0:
```python
import functools
import math

import jax
import jax.numpy as jnp
from jax import lax
from jax.experimental import pallas as pl
from jax.experimental.pallas import tpu as pltpu
from jax.sharding import PartitionSpec as P


BETA_ONE = 0.9
BETA_TWO = 0.95
LEARN_RATE = 0.01
ADAM_EPSILON = 0.05
SQRT_2_OVER_PI = math.sqrt(2.0 / math.pi)


VMEM = pl.BlockSpec(memory_space=pltpu.VMEM)
SMEM = pl.BlockSpec(memory_space=pltpu.SMEM)


def call(kernel, out_shape, in_specs, out_specs, scratch):
    return pl.pallas_call(
        kernel, out_shape=out_shape, in_specs=in_specs, out_specs=out_specs, scratch_shapes=scratch
    )


def shape(dims, dtype):
    return jax.ShapeDtypeStruct(dims, dtype)


def wrap(value, count):
    return jnp.where(value < 0, value + count, value)


def which_group(value, group, count):
    found = jnp.int32(0)
    for edge in range(1, count):
        found = found + (value >= edge * group).astype(jnp.int32)
    return found


def plan_kernel(cfg, here, coords, moved, first, second, *rest):
    n, per, cap, ms, bs, bw, pad = cfg
    table = rest[0]
    packs = rest[1 : 1 + n]
    src, out_slot, counts = rest[1 + n :]
    total = n * per
    slots = n * bs
    me = here[0]

    def fill(ref, base, size, value):
        def put(i, _):
            ref[base + i] = jnp.int32(value)
            return 0

        lax.fori_loop(0, size, put, 0)

    fill(src, 0, total, -1)
    fill(out_slot, 0, n * ms, 0)
    fill(table, 0, slots, -1)
    fill(table, slots, 2 * slots, 0)
    fill(table, 3 * slots, 3 * per, -1)

    for p in range(n):
        for i in range(n):
            counts[i] = jnp.int32(0)
        rel = wrap(me - p, n)

        def old_slot(j, _):
            o = p * cap + j
            t = moved[o]

            @pl.when(t >= 0)
            def _():
                dest = which_group(t, per, n)
                src[t] = rel * cap + j
                k = counts[dest]
                counts[dest] = k + 1

                @pl.when(me == p)
                def _():
                    out_slot[wrap(dest - me, n) * ms + k] = j

                @pl.when(dest == me)
                def _():
                    table[3 * slots + 2 * per + t - me * per] = rel * pad + k

            return 0

        lax.fori_loop(0, cap, old_slot, 0)

    for w in range(n):
        for i in range(n):
            counts[i] = jnp.int32(0)

        def new_slot(j, _):
            b = w * per + j
            col = coords[1, b]
            band = which_group(col, bw, n)
            k = counts[band]
            counts[band] = k + 1

            @pl.when(band == me)
            def _():
                q = w * bs + k
                table[q] = src[b]
                table[slots + q] = coords[0, b]
                table[2 * slots + q] = col - me * bw

            @pl.when(me == w)
            def _():
                table[3 * slots + j] = src[b]
                table[3 * slots + per + j] = wrap(me - band, n) * bs + k

            return 0

        lax.fori_loop(0, per, new_slot, 0)

    for s in range(n):
        for k in range(ms):
            row = out_slot[s * ms + k]
            packs[s][0, k : k + 1, :] = first[pl.ds(row, 1), :]
            packs[s][1, k : k + 1, :] = second[pl.ds(row, 1), :]
        if pad > ms:
            packs[s][:, ms:pad, :] = jnp.zeros((2, pad - ms, first.shape[1]), jnp.float32)


def select_kernel(cfg, table, *rest):
    n, per, cap, bs = cfg
    shares = rest[:n]
    picked, mine, pool = rest[n:]
    slots = n * bs
    for s in range(n):
        pool[s * cap : (s + 1) * cap] = shares[s][...]

    def pick(out, base):
        def one(i, _):
            at = table[base + i]
            row = pool[jnp.maximum(at, 0)]
            out[i] = jnp.where(at >= 0, row, jnp.zeros_like(row))
            return 0

        return one

    lax.fori_loop(0, slots, pick(picked, 0), 0, unroll=4)
    lax.fori_loop(0, per, pick(mine, 3 * slots), 0, unroll=4)


def forward_kernel(cfg, here, table, tokens, cotangent, *rest):
    n, bs, bw, blk, parts = cfg
    weights_in = rest[:parts]
    rest = rest[parts:]
    activated, slopes = rest[:2]
    far = rest[2 : 1 + n]
    own = rest[1 + n]
    weights, products, hidden, backs, grads = rest[2 + n :]
    slots = n * bs
    me = here[0]
    if parts == 1:
        weights = weights_in[0]
    else:
        rows = blk // parts
        d = here[1]
        for s in range(parts):
            weights[:, pl.ds(pl.multiple_of((d ^ s) * rows, rows), rows), :] = weights_in[s][...]

    def col_at(index):
        return pl.ds(pl.multiple_of(index * blk, blk), blk)

    def product(w, _):
        for k in range(bs):
            q = w * bs + k
            products[q] = jnp.dot(
                tokens[:, col_at(table[slots + q])],
                weights[q],
                preferred_element_type=jnp.float32,
            ).astype(jnp.bfloat16)
        return 0

    lax.fori_loop(0, n, product, 0)
    hidden[...] = jnp.zeros_like(hidden)

    def gather_hidden(q, _):
        at = col_at(table[2 * slots + q])
        hidden[:, at] = hidden[:, at] + products[q].astype(jnp.float32)
        return 0

    lax.fori_loop(0, slots, gather_hidden, 0)

    def pointwise(c, _):
        at = col_at(c)
        v = hidden[:, at]
        square = v * v
        t = jnp.tanh(SQRT_2_OVER_PI * (v + 0.044715 * (square * v)))
        half = 0.5 * (1.0 + t)
        activated[:, at] = (v * half).astype(jnp.bfloat16)
        slope = half + 0.5 * v * ((1.0 - t) * (1.0 + t)) * (
            SQRT_2_OVER_PI * (1.0 + (3.0 * 0.044715) * square)
        )
        slopes[:, at] = (cotangent[:, at].astype(jnp.float32) * slope).astype(jnp.bfloat16)
        return 0

    lax.fori_loop(0, bw, pointwise, 0)

    def back(w, _):
        for k in range(bs):
            q = w * bs + k
            backs[q] = lax.dot_general(
                slopes[:, col_at(table[2 * slots + q])],
                weights[q],
                (((1,), (1,)), ((), ())),
                preferred_element_type=jnp.float32,
            )
        return 0

    lax.fori_loop(0, n, back, 0)
    grads[...] = jnp.zeros_like(grads)

    def gather_back(q, _):
        at = col_at(table[slots + q])
        grads[:, at] = grads[:, at] + backs[q]
        return 0

    lax.fori_loop(0, slots, gather_back, 0)
    width = own.shape[1]

    def band_of(s):
        band = me + s
        band = jnp.where(band >= n, band - n, band)
        return grads[:, pl.ds(pl.multiple_of(band * width, blk), width)]

    own[...] = band_of(0)
    for s in range(1, n):
        far[s - 1][...] = band_of(s).astype(jnp.bfloat16)


def grad_kernel(cfg, here, table, tokens, slopes, *rest):
    n, bs, blk, parts = cfg
    outs = rest[:parts]
    partial = rest[parts]
    slots = n * bs

    def col_at(index):
        return pl.ds(pl.multiple_of(index * blk, blk), blk)

    target = outs[0] if parts == 1 else partial

    def one(w, _):
        for k in range(bs):
            q = w * bs + k
            target[q] = lax.dot_general(
                tokens[:, col_at(table[slots + q])],
                slopes[:, col_at(table[2 * slots + q])],
                (((0,), (0,)), ((), ())),
                preferred_element_type=jnp.float32,
            ).astype(jnp.bfloat16)
        return 0

    lax.fori_loop(0, n, one, 0)
    if parts > 1:
        rows = blk // parts
        d = here[1]
        for s in range(parts):
            outs[s][...] = partial[:, pl.ds(pl.multiple_of((d ^ s) * rows, rows), rows), :]


def pair_kernel(half, *refs):
    for j in range(half):
        total = refs[j][...].astype(jnp.float32) + refs[half + j][...].astype(jnp.float32)
        refs[2 * half + j][...] = total.astype(jnp.bfloat16)


def total_kernel(cfg, here, *rest):
    n, bs, count = cfg
    terms = rest[:count]
    outs = rest[count : count + n]
    pool = rest[count + n]
    me = here[0]
    total = terms[0][...].astype(jnp.float32)
    for term in terms[1:]:
        total = total + term[...].astype(jnp.float32)
    pool[...] = total.astype(jnp.bfloat16)
    for s in range(n):
        band = me + s
        band = jnp.where(band >= n, band - n, band)
        outs[s][...] = pool[pl.ds(band * bs, bs)]


def adam_kernel(cfg, table, mine, *rest):
    n, per, bs, pad, rows, scale = cfg
    grads = rest[:n]
    moments = rest[n : 2 * n]
    first_out, second_out, weight_out = rest[2 * n : 2 * n + 3]
    pool, moved, grad, weight, first, second = rest[2 * n + 3 :]
    slots = n * bs
    lanes = mine.shape[2]
    for s in range(n):
        pool[s * bs : (s + 1) * bs] = grads[s][...]
        moved[:, s * pad : (s + 1) * pad, :] = moments[s][...]

    for i in range(per):
        grad[i * rows : (i + 1) * rows, :] = (
            pool[table[3 * slots + per + i]].astype(jnp.float32) * scale
        )
        weight[i * rows : (i + 1) * rows, :] = mine[i].astype(jnp.float32)
        at = table[3 * slots + 2 * per + i]
        row = jnp.maximum(at, 0)
        old_first = moved[0, pl.ds(row, 1), :]
        old_second = moved[1, pl.ds(row, 1), :]
        first[i : i + 1, :] = jnp.where(at >= 0, old_first, jnp.zeros_like(old_first))
        second[i : i + 1, :] = jnp.where(at >= 0, old_second, jnp.zeros_like(old_second))

    for r in range(rows):
        at = slice(r * lanes, (r + 1) * lanes)
        strided = pl.ds(r, per, stride=rows)
        g = grad[strided, :]
        first_new = BETA_ONE * first[:, at] + (1.0 - BETA_ONE) * g
        second_new = BETA_TWO * second[:, at] + (1.0 - BETA_TWO) * g * g
        first_out[:, at] = first_new
        second_out[:, at] = second_new
        weight[strided, :] = weight[strided, :] - LEARN_RATE * first_new / (
            jnp.sqrt(second_new) + ADAM_EPSILON
        )
    for i in range(per):
        weight_out[i] = weight[i * rows : (i + 1) * rows, :].astype(jnp.bfloat16)


def join_kernel(parts, here, *rest):
    out = rest[parts]
    rows = rest[0].shape[1]
    d = here[1]
    for s in range(parts):
        out[:, pl.ds(pl.multiple_of((d ^ s) * rows, rows), rows), :] = rest[s][...]


def sum_kernel(own, *rest):
    total = own[...]
    for term in rest[:-1]:
        total = total + term[...].astype(jnp.float32)
    rest[-1][...] = total.astype(jnp.bfloat16)


def swap(value, bits, parts):
    return lax.ppermute(value, "dp", [(i, i ^ bits) for i in range(parts)])


def shift(value, step, n):
    return lax.ppermute(value, "mp", [(i, (i + step) % n) for i in range(n)])


def plane_gather(value, parts):
    pieces = [value] + [None] * (parts - 1)
    for s in range(2, parts, 2):
        pieces[s] = swap(value, s, parts)
    for s in range(0, parts, 2):
        pieces[s + 1] = swap(pieces[s], 1, parts)
    return pieces


def step(tokens_in, cotangent, old_weights, old_first, old_second, new_coords, moved_to):
    n = lax.axis_size("mp")
    parts = lax.axis_size("dp")
    me = lax.axis_index("mp")
    d = lax.axis_index("dp")
    cap, blk = old_weights.shape[:2]
    total = new_coords.shape[0]
    per = total // n
    shard = old_first.shape[1]
    rows = blk // parts
    tok, width = tokens_in.shape
    bw = cotangent.shape[1] // blk
    ms = cap // n
    pad = -(-ms // 8) * 8
    bs = 2 * per // n + 1
    slots = n * bs
    direct = rows % 16 == 0 and parts & (parts - 1) == 0
    bf16, f32 = jnp.bfloat16, jnp.float32
    here = jnp.stack([me, d]).astype(jnp.int32)

    share = lax.dynamic_slice_in_dim(old_weights, d * rows, rows, 1)
    shares = [share] + [shift(share, s, n) for s in range(1, n)]

    plan = call(
        functools.partial(plan_kernel, (n, per, cap, ms, bs, bw, pad)),
        [shape((3 * slots + 3 * per,), jnp.int32)] + [shape((2, pad, shard), f32)] * n,
        [SMEM, SMEM, SMEM, VMEM, VMEM],
        [SMEM] + [VMEM] * n,
        [
            pltpu.SMEM((total,), jnp.int32),
            pltpu.SMEM((n * ms,), jnp.int32),
            pltpu.SMEM((n,), jnp.int32),
        ],
    )(here, new_coords.T, moved_to, old_first, old_second)
    table, packs = plan[0], plan[1:]

    picked, mine = call(
        functools.partial(select_kernel, (n, per, cap, bs)),
        [shape((slots, rows, blk), bf16), shape((per, rows, blk), bf16)],
        [SMEM] + [VMEM] * n,
        [VMEM, VMEM],
        [pltpu.VMEM((n * cap, rows, blk), bf16)],
    )(table, *shares)

    if direct:
        pieces = plane_gather(picked, parts)
    else:
        gathered = lax.all_gather(picked, "dp", axis=0)
        pieces = [gathered.transpose(1, 0, 2, 3).reshape(slots, blk, blk)]

    packs = list(lax.optimization_barrier(tuple(packs) + (picked,)))[:n]
    moments = [packs[0]] + [shift(packs[s], s, n) for s in range(1, n)]

    results = call(
        functools.partial(forward_kernel, (n, bs, bw, blk, len(pieces))),
        [shape((tok, bw * blk), bf16)] * 2
        + [shape((tok, width // n), bf16)] * (n - 1)
        + [shape((tok, width // n), f32)],
        [SMEM, SMEM, VMEM, VMEM] + [VMEM] * len(pieces),
        [VMEM] * (n + 2),
        [
            pltpu.VMEM((slots, blk, blk), bf16),
            pltpu.VMEM((slots, tok, blk), bf16),
            pltpu.VMEM((tok, bw * blk), f32),
            pltpu.VMEM((slots, tok, blk), f32),
            pltpu.VMEM((tok, width), f32),
        ],
    )(here, table, tokens_in, cotangent, *pieces)
    activated, slopes = results[:2]
    far, own = results[2 : 1 + n], results[1 + n]
    back_terms = [shift(far[s - 1], s, n) for s in range(1, n)]

    count = parts if direct else 1
    partials = call(
        functools.partial(grad_kernel, (n, bs, blk, count)),
        [shape((slots, blk // count, blk), bf16)] * count,
        [SMEM, SMEM, VMEM, VMEM],
        [VMEM] * count,
        [pltpu.VMEM((slots, blk, blk), bf16)],
    )(here, table, tokens_in, slopes)

    if direct:
        half = parts // 2
        even = [partials[2 * j] for j in range(half)]
        crossed = [swap(partials[2 * j + 1], 1, parts) for j in range(half)]
        paired = call(
            functools.partial(pair_kernel, half),
            [shape((slots, rows, blk), bf16)] * half,
            [VMEM] * parts,
            [VMEM] * half,
            [],
        )(*even, *crossed)
        terms = [paired[0]] + [swap(paired[j], 2 * j, parts) for j in range(1, half)]
    else:
        spread = partials[0].reshape(slots, parts, rows, blk).transpose(1, 0, 2, 3)
        spread = lax.all_to_all(spread, "dp", split_axis=0, concat_axis=0, tiled=True)
        terms = [jnp.sum(spread.astype(f32), axis=0)]

    owner_grads = call(
        functools.partial(total_kernel, (n, bs, len(terms))),
        [shape((bs, rows, blk), bf16)] * n,
        [SMEM] + [VMEM] * len(terms),
        [VMEM] * n,
        [pltpu.VMEM((slots, rows, blk), bf16)],
    )(here, *terms)
    arrived = [owner_grads[0]] + [shift(owner_grads[s], s, n) for s in range(1, n)]

    first_new, second_new, weight_share = call(
        functools.partial(
            adam_kernel, (n, per, bs, pad, rows, 1.0 / math.sqrt(tok * parts))
        ),
        [shape((per, shard), f32)] * 2 + [shape((per, rows, blk), bf16)],
        [SMEM, VMEM] + [VMEM] * (2 * n),
        [VMEM] * 3,
        [
            pltpu.VMEM((slots, rows, blk), bf16),
            pltpu.VMEM((2, n * pad, shard), f32),
            pltpu.VMEM((per * rows, blk), f32),
            pltpu.VMEM((per * rows, blk), f32),
            pltpu.VMEM((per, shard), f32),
            pltpu.VMEM((per, shard), f32),
        ],
    )(table, mine, *arrived, *moments)

    if direct:
        weights_out = call(
            functools.partial(join_kernel, parts),
            shape((per, blk, blk), bf16),
            [SMEM] + [VMEM] * parts,
            VMEM,
            [],
        )(here, *plane_gather(weight_share, parts))
    else:
        weights_out = lax.all_gather(weight_share, "dp", axis=1, tiled=True)

    grad_inputs = call(
        sum_kernel, shape((tok, width // n), bf16), [VMEM] * n, VMEM, []
    )(own, *back_terms)
    return (activated, grad_inputs, weights_out, first_new, second_new)


def solution(mesh):
    in_specs = (
        P("dp", None),
        P("dp", "mp"),
        P("mp", None, None),
        P("mp", "dp"),
        P("mp", "dp"),
        P(),
        P(),
    )
    out_specs = (P("dp", "mp"), P("dp", "mp"), P("mp", None, None), P("mp", "dp"), P("mp", "dp"))
    return jax.shard_map(step, mesh=mesh, in_specs=in_specs, out_specs=out_specs, check_vma=False)
```

profile of v0, /device:TPU:0, one launch (start us, length us, event | category | flops | bytes accessed | tf_op | source)
XLA Modules:
  0.0 122.0 jit_solution(17316701609250656040)
XLA Ops:
  0.7 1.2 copy-done
  1.8 5.1 %collective-permute-start.2 = (bf16[28,16,128]{2,1,0:T(8,128)(2,1)S(1)}, bf16[28,16,128]{2,1,0:T(8,128)(2,1)S(1)}, u32[]{:S(2)}, u32[]{:S(2)}) collective-permute-start(bf16[28,16,128]{2,1,0:T(8,128)(2,1)S(1)} %constant_dynamic-slice_fusion.rest_0_), channel_id=1, source_target_pairs={{0,3},{1,0},{2,1},{3,2},{4,7},{5,4},{6,5},{7,6},{8,11},{9,8},{10,9... | collective-permute-start | bytes 344072 | tf_op jit(solution)/shard_map/ppermute | solution.py:350
  7.0 1.0 collective-permute-start
  8.0 0.6 pad_add_fusion.here
  8.6 7.8 %shard_map.110 = (s32[192]{0:T(256)}, f32[2,8,2048]{2,1,0:T(8,128)}, f32[2,8,2048]{2,1,0:T(8,128)}, f32[2,8,2048]{2,1,0:T(8,128)}, f32[2,8,2048]{2,1,0:T(8,128)}) custom-call(s32[2]{0:T(128)} %pad_add_fusion.here, s32[2,80]{1,0:T(2,128)} %bitcast.3, s32[112]{0:T(128)} %moved.1, f32[28,2048]{1,0:T(8,128)} %first.1, f32[28,2048]{1,0:T(8,128)} %second.1), custom_call_target="tpu_custom_call" | custom-call | tf_op jit(solution)/shard_map/pallas_call | solution.py:385
  16.5 0.5 collective-permute-done.1.rest_2_
  17.1 0.5 copy-done.23
  17.6 2.0 %shard_map.111 = (bf16[44,16,128]{2,1,0:T(8,128)(2,1)}, bf16[20,16,128]{2,1,0:T(8,128)(2,1)}) custom-call(s32[192]{0:T(256)} %get-tuple-element.41.table, bf16[28,16,128]{2,1,0:T(8,128)(2,1)} %copy-done.1, bf16[28,16,128]{2,1,0:T(8,128)(2,1)} %copy-done.24, bf16[28,16,128]{2,1,0:T(8,128)(2,1)} %copy-done.23, bf16[28,16,128]{2,1,0:T(8,128)(2,1)} %copy-done.22), custom_call_target="tpu_custom_call" | custom-call | tf_op jit(solution)/shard_map/pallas_call | solution.py:398
  19.7 2.4 %collective-permute-start.8 = (bf16[44,16,128]{2,1,0:T(8,128)(2,1)}, bf16[44,16,128]{2,1,0:T(8,128)(2,1)S(1)}, u32[]{:S(2)}, u32[]{:S(2)}) collective-permute-start(bf16[44,16,128]{2,1,0:T(8,128)(2,1)} %get-tuple-element.42.rest_0_), channel_id=1, source_target_pairs={{0,24},{4,28},{8,16},{12,20},{16,8},{20,12},{24,0},{28,4},{1,25},{... | collective-permute-start | bytes 540680 | tf_op jit(solution)/shard_map/ppermute | solution.py:346
  22.1 0.5 collective-permute-start.6
  22.6 0.5 collective-permute-start.4
  23.2 4.9 %collective-permute-done.8.rest_6_ = bf16[44,16,128]{2,1,0:T(8,128)(2,1)S(1)} collective-permute-done((bf16[44,16,128]{2,1,0:T(8,128)(2,1)}, bf16[44,16,128]{2,1,0:T(8,128)(2,1)S(1)}, u32[]{:S(2)}, u32[]{:S(2)}) %collective-permute-start.8) | collective-permute-done | bytes 180256 | tf_op jit(solution)/shard_map/ppermute | solution.py:346
  28.1 2.4 %collective-permute-done.6.rest_4_ = bf16[44,16,128]{2,1,0:T(8,128)(2,1)S(1)} collective-permute-done((bf16[44,16,128]{2,1,0:T(8,128)(2,1)}, bf16[44,16,128]{2,1,0:T(8,128)(2,1)S(1)}, u32[]{:S(2)}, u32[]{:S(2)}) %collective-permute-start.6) | collective-permute-done | bytes 180256 | tf_op jit(solution)/shard_map/ppermute | solution.py:346
  30.6 0.4 collective-permute-start.5
  31.1 0.9 collective-permute-done.7.rest_5_
  31.9 0.3 collective-permute-done.5.rest_3_
  32.2 0.4 copy-done.17
  32.6 0.7 copy-done.18
  33.3 9.2 %shard_map.112 = (bf16[128,2560]{1,0:T(8,128)(2,1)}, bf16[128,2560]{1,0:T(8,128)(2,1)}, bf16[128,1280]{1,0:T(8,128)(2,1)}, bf16[128,1280]{1,0:T(8,128)(2,1)}, bf...) custom-call(s32[2]{0:T(128)} %pad_add_fusion.here, s32[192]{0:T(256)} %get-tuple-element.41.table, bf16[128,5120]{1,0:T(8,128)(2,1)} %tokens.3, ...), custom_call_target="tpu_custom_call" | custom-call | tf_op jit(solution)/shard_map/pallas_call | solution.py:415
  42.5 4.2 %shard_map.114 = (bf16[44,16,128]{2,1,0:T(8,128)(2,1)}, bf16[44,16,128]{2,1,0:T(8,128)(2,1)}, bf16[44,16,128]{2,1,0:T(8,128)(2,1)}, bf16[44,16,128]{2,1,0:T(8,12...) custom-call(s32[2]{0:T(128)} %pad_add_fusion.here, ...), custom_call_target="tpu_custom_call" | custom-call | tf_op jit(solution)/shard_map/pallas_call | solution.py:435
  46.7 0.1 collective-permute-start.13
  46.8 0.4 collective-permute-start.14
  47.2 0.1 collective-permute-start.15
  47.3 0.4 collective-permute-start.16
  47.7 0.6 collective-permute-done.13.refs_4_
  48.3 0.3 collective-permute-done.14.refs_5_
  48.6 0.3 collective-permute-done.15.refs_6_
  48.8 0.3 collective-permute-done.16.refs_7_
  49.1 0.2 copy-done.9
  49.2 0.2 copy-done.10
  49.5 0.3 copy-done.11
  49.7 2.3 %shard_map.115 = (bf16[44,16,128]{2,1,0:T(8,128)(2,1)}, bf16[44,16,128]{2,1,0:T(8,128)(2,1)}, bf16[44,16,128]{2,1,0:T(8,128)(2,1)}, bf16[44,16,128]{2,1,0:T(8,128)(2,1)}) custom-call(bf16[44,16,128]{2,1,0:T(8,128)(2,1)} %get-tuple-element.50.refs_0_, bf16[44,16,128]{2,1,0:T(8,128)(2,1)} %get-tuple-element.51.refs_1_, ...), custom_call_target="tpu_custom_call" | custom-call | tf_op jit(solution)/shard_map/pallas_call | solution.py:447
  52.1 1.5 %collective-permute-start.17 = (bf16[44,16,128]{2,1,0:T(8,128)(2,1)}, bf16[44,16,128]{2,1,0:T(8,128)(2,1)S(1)}, u32[]{:S(2)}, u32[]{:S(2)}) collective-permute-start(bf16[44,16,128]{2,1,0:T(8,128)(2,1)} %get-tuple-element.59), channel_id=1, source_target_pairs={{0,8},{4,12},{8,0},{12,4},{16,24},{20,28},{24,16},{28,20},{1,9},{5... | collective-permute-start | bytes 540680 | tf_op jit(solution)/shard_map/ppermute | solution.py:346
  53.6 1.6 %collective-permute-start.23 = (f32[2,8,2048]{2,1,0:T(8,128)S(1)}, f32[2,8,2048]{2,1,0:T(8,128)S(1)}, u32[]{:S(2)}, u32[]{:S(2)}) collective-permute-start(f32[2,8,2048]{2,1,0:T(8,128)S(1)} %copy-done.37), channel_id=1, source_target_pairs={{0,1},{1,2},{2,3},{3,0},{4,5},{5,6},{6,7},{7,4},{8,9},{9,10},{10,1... | collective-permute-start | bytes 393224 | tf_op jit(solution)/shard_map/ppermute | solution.py:350
  55.1 0.8 collective-permute-start.18
  55.9 1.2 collective-permute-start.19
  57.1 1.3 %collective-permute-start.10 = (bf16[128,1280]{1,0:T(8,128)(2,1)}, bf16[128,1280]{1,0:T(8,128)(2,1)S(1)}, u32[]{:S(2)}, u32[]{:S(2)}) collective-permute-start(bf16[128,1280]{1,0:T(8,128)(2,1)} %get-tuple-element.45), channel_id=1, source_target_pairs={{0,1},{1,2},{2,3},{3,0},{4,5},{5,6},{6,7},{7,4},{8,9},{9,10},{10,1... | collective-permute-start | bytes 983048 | tf_op jit(solution)/shard_map/ppermute | solution.py:350
  58.4 2.3 %collective-permute-done.23.rest_5_ = f32[2,8,2048]{2,1,0:T(8,128)S(1)} collective-permute-done((f32[2,8,2048]{2,1,0:T(8,128)S(1)}, f32[2,8,2048]{2,1,0:T(8,128)S(1)}, u32[]{:S(2)}, u32[]{:S(2)}) %collective-permute-start.23) | collective-permute-done | bytes 131104 | tf_op jit(solution)/shard_map/ppermute | solution.py:350
  60.7 1.4 %collective-permute-start.11 = (bf16[128,1280]{1,0:T(8,128)(2,1)S(1)}, bf16[128,1280]{1,0:T(8,128)(2,1)S(1)}, u32[]{:S(2)}, u32[]{:S(2)}) collective-permute-start(bf16[128,1280]{1,0:T(8,128)(2,1)S(1)} %copy-done.36), channel_id=1, source_target_pairs={{0,2},{1,3},{2,0},{3,1},{4,6},{5,7},{6,4},{7,5},{8,10},{9,11},{10,... | collective-permute-start | bytes 983048 | tf_op jit(solution)/shard_map/ppermute | solution.py:350
  62.2 1.5 %collective-permute-start.24 = (f32[2,8,2048]{2,1,0:T(8,128)}, f32[2,8,2048]{2,1,0:T(8,128)S(1)}, u32[]{:S(2)}, u32[]{:S(2)}) collective-permute-start(f32[2,8,2048]{2,1,0:T(8,128)} %get-tuple-element.72), channel_id=1, source_target_pairs={{0,2},{1,3},{2,0},{3,1},{4,6},{5,7},{6,4},{7,5},{8,10},{9,11},{10,... | collective-permute-start | bytes 393224 | tf_op jit(solution)/shard_map/ppermute | solution.py:350
  63.7 1.7 %collective-permute-done.18.rest_2_ = bf16[44,16,128]{2,1,0:T(8,128)(2,1)S(1)} collective-permute-done((bf16[44,16,128]{2,1,0:T(8,128)(2,1)}, bf16[44,16,128]{2,1,0:T(8,128)(2,1)S(1)}, u32[]{:S(2)}, u32[]{:S(2)}) %collective-permute-start.18) | collective-permute-done | bytes 180256 | tf_op jit(solution)/shard_map/ppermute | solution.py:346
  65.4 2.2 %collective-permute-start.25 = (f32[2,8,2048]{2,1,0:T(8,128)}, f32[2,8,2048]{2,1,0:T(8,128)S(1)}, u32[]{:S(2)}, u32[]{:S(2)}) collective-permute-start(f32[2,8,2048]{2,1,0:T(8,128)} %get-tuple-element.73), channel_id=1, source_target_pairs={{0,3},{1,0},{2,1},{3,2},{4,7},{5,4},{6,5},{7,6},{8,11},{9,8},{10,9... | collective-permute-start | bytes 393224 | tf_op jit(solution)/shard_map/ppermute | solution.py:350
  67.6 0.5 collective-permute-start.12
  68.1 0.2 copy-done.7
  68.3 2.0 %shard_map.116 = (bf16[11,16,128]{2,1,0:T(8,128)(2,1)}, bf16[11,16,128]{2,1,0:T(8,128)(2,1)}, bf16[11,16,128]{2,1,0:T(8,128)(2,1)}, bf16[11,16,128]{2,1,0:T(8,128)(2,1)}) custom-call(s32[2]{0:T(128)} %pad_add_fusion.here, bf16[44,16,128]{2,1,0:T(8,128)(2,1)} %get-tuple-element.58.rest_0_, bf16[44,16,128]{2,1,0:T(8,128)(2,1)} %copy-done.5, ...), custom_call_target="tpu_custom_call" | custom-call | tf_op jit(solution)/shard_map/pallas_call | solution.py:460
  70.3 17.4 %collective-permute-done.24.rest_6_ = f32[2,8,2048]{2,1,0:T(8,128)S(1)} collective-permute-done((f32[2,8,2048]{2,1,0:T(8,128)}, f32[2,8,2048]{2,1,0:T(8,128)S(1)}, u32[]{:S(2)}, u32[]{:S(2)}) %collective-permute-start.24) | collective-permute-done | bytes 131104 | tf_op jit(solution)/shard_map/ppermute | solution.py:350
  87.7 8.4 %collective-permute-start.20 = (bf16[11,16,128]{2,1,0:T(8,128)(2,1)}, bf16[11,16,128]{2,1,0:T(8,128)(2,1)S(1)}, u32[]{:S(2)}, u32[]{:S(2)}) collective-permute-start(bf16[11,16,128]{2,1,0:T(8,128)(2,1)} %get-tuple-element.63), channel_id=1, source_target_pairs={{0,1},{1,2},{2,3},{3,0},{4,5},{5,6},{6,7},{7,4},{8,9},{9,10},{10,1... | collective-permute-start | bytes 135176 | tf_op jit(solution)/shard_map/ppermute | solution.py:350
  96.1 3.3 %collective-permute-start.21 = (bf16[11,16,128]{2,1,0:T(8,128)(2,1)}, bf16[11,16,128]{2,1,0:T(8,128)(2,1)S(1)}, u32[]{:S(2)}, u32[]{:S(2)}) collective-permute-start(bf16[11,16,128]{2,1,0:T(8,128)(2,1)} %get-tuple-element.64), channel_id=1, source_target_pairs={{0,2},{1,3},{2,0},{3,1},{4,6},{5,7},{6,4},{7,5},{8,10},{9,11},{10,... | collective-permute-start | bytes 135176 | tf_op jit(solution)/shard_map/ppermute | solution.py:350
  99.3 1.7 %collective-permute-done.20.rest_1_ = bf16[11,16,128]{2,1,0:T(8,128)(2,1)S(1)} collective-permute-done((bf16[11,16,128]{2,1,0:T(8,128)(2,1)}, bf16[11,16,128]{2,1,0:T(8,128)(2,1)S(1)}, u32[]{:S(2)}, u32[]{:S(2)}) %collective-permute-start.20) | collective-permute-done | bytes 45088 | tf_op jit(solution)/shard_map/ppermute | solution.py:350
  101.0 2.0 %collective-permute-start.22 = (bf16[11,16,128]{2,1,0:T(8,128)(2,1)}, bf16[11,16,128]{2,1,0:T(8,128)(2,1)S(1)}, u32[]{:S(2)}, u32[]{:S(2)}) collective-permute-start(bf16[11,16,128]{2,1,0:T(8,128)(2,1)} %get-tuple-element.65), channel_id=1, source_target_pairs={{0,3},{1,0},{2,1},{3,2},{4,7},{5,4},{6,5},{7,6},{8,11},{9,8},{10,9... | collective-permute-start | bytes 135176 | tf_op jit(solution)/shard_map/ppermute | solution.py:350
  103.0 2.3 %collective-permute-done.22.rest_3_ = bf16[11,16,128]{2,1,0:T(8,128)(2,1)S(1)} collective-permute-done((bf16[11,16,128]{2,1,0:T(8,128)(2,1)}, bf16[11,16,128]{2,1,0:T(8,128)(2,1)S(1)}, u32[]{:S(2)}, u32[]{:S(2)}) %collective-permute-start.22) | collective-permute-done | bytes 45088 | tf_op jit(solution)/shard_map/ppermute | solution.py:350
  105.3 0.6 copy-done.34
  105.9 2.3 %shard_map.117 = (f32[20,2048]{1,0:T(8,128)}, f32[20,2048]{1,0:T(8,128)}, bf16[20,16,128]{2,1,0:T(8,128)(2,1)}) custom-call(s32[192]{0:T(256)} %get-tuple-element.41.table, bf16[20,16,128]{2,1,0:T(8,128)(2,1)} %get-tuple-element.48.mine, bf16[11,16,128]{2,1,0:T(8,128)(2,1)} %get-tuple-element.62.rest_0_, bf16[11,16,128]{2,1,0:T(8,128)(2,1)} %copy-done.32, ...), custom_call_target="tpu_custom_call" | custom-call | tf_op jit(solution)/shard_map/pallas_call | solution.py:469
  108.2 1.7 %collective-permute-start.31 = (bf16[20,16,128]{2,1,0:T(8,128)(2,1)}, bf16[20,16,128]{2,1,0:T(8,128)(2,1)S(1)}, u32[]{:S(2)}, u32[]{:S(2)}) collective-permute-start(bf16[20,16,128]{2,1,0:T(8,128)(2,1)} %get-tuple-element.74.rest_0_), channel_id=1, source_target_pairs={{0,24},{4,28},{8,16},{12,20},{16,8},{20,12},{24,0},{28,4},{1,25},{... | collective-permute-start | bytes 245768 | tf_op jit(solution)/shard_map/ppermute | solution.py:346
  110.0 0.9 collective-permute-start.29
  110.9 0.8 collective-permute-start.27
  111.7 2.0 %collective-permute-done.31.rest_6_ = bf16[20,16,128]{2,1,0:T(8,128)(2,1)S(1)} collective-permute-done((bf16[20,16,128]{2,1,0:T(8,128)(2,1)}, bf16[20,16,128]{2,1,0:T(8,128)(2,1)S(1)}, u32[]{:S(2)}, u32[]{:S(2)}) %collective-permute-start.31) | collective-permute-done | bytes 81952 | tf_op jit(solution)/shard_map/ppermute | solution.py:346
  113.8 0.9 collective-permute-done.29.rest_4_
  114.7 0.9 collective-permute-done.27.rest_2_
  115.6 0.7 copy-done.4
  116.3 2.2 %shard_map.113 = bf16[128,1280]{1,0:T(8,128)(2,1)} custom-call(f32[128,1280]{1,0:T(8,128)} %get-tuple-element.44.own, bf16[128,1280]{1,0:T(8,128)(2,1)} %copy-done.2, bf16[128,1280]{1,0:T(8,128)(2,1)} %copy-done.3, bf16[128,1280]{1,0:T(8,128)(2,1)} %copy-done.4), custom_call_target="tpu_custom_call" | custom-call | tf_op jit(solution)/shard_map/pallas_call | solution.py:497
  118.6 0.6 copy-done.28
  119.3 0.6 copy-done.31
  119.9 2.1 %shard_map.118 = bf16[20,128,128]{2,1,0:T(8,128)(2,1)} custom-call(s32[2]{0:T(128)} %pad_add_fusion.here, bf16[20,16,128]{2,1,0:T(8,128)(2,1)} %get-tuple-element.74.rest_0_, bf16[20,16,128]{2,1,0:T(8,128)(2,1)} %copy-done.28, bf16[20,16,128]{2,1,0:T(8,128)(2,1)} %copy-done.27, bf16[20,16,128]{2,1,0:T(8,128)(2,1)} %copy-done.31, ...), custom_call_target="tpu_custom_call" | custom-call | tf_op jit(solution)/shard_map/pallas_call | solution.py:487
  (89 shorter events, 0.5 us)
Async XLA Ops:
  0.6 1.2 copy-start
  1.8 15.1 %copy-start.1 = (bf16[28,16,128]{2,1,0:T(8,128)(2,1)}, bf16[28,16,128]{2,1,0:T(8,128)(2,1)S(1)}, u32[]{:S(2)}) copy-start(bf16[28,16,128]{2,1,0:T(8,128)(2,1)S(1)} %constant_dynamic-slice_fusion.rest_0_) | copy-start | bytes 344068
  1.8 14.6 %collective-permute-start.2 = (bf16[28,16,128]{2,1,0:T(8,128)(2,1)S(1)}, bf16[28,16,128]{2,1,0:T(8,128)(2,1)S(1)}, u32[]{:S(2)}, u32[]{:S(2)}) collective-permute-start(bf16[28,16,128]{2,1,0:T(8,128)(2,1)S(1)} %constant_dynamic-slice_fusion.rest_0_), channel_id=1, source_target_pairs={{0,3},{1,0},{2,1},{3,2},{4,7},{5,4},{6,5},{7,6},{8,11},{9,8},{10,9... | collective-permute-start | bytes 344072 | tf_op jit(solution)/shard_map/ppermute | solution.py:350
  7.0 10.0 %collective-permute-start.1 = (bf16[28,16,128]{2,1,0:T(8,128)(2,1)S(1)}, bf16[28,16,128]{2,1,0:T(8,128)(2,1)S(1)}, u32[]{:S(2)}, u32[]{:S(2)}) collective-permute-start(bf16[28,16,128]{2,1,0:T(8,128)(2,1)S(1)} %constant_dynamic-slice_fusion.rest_0_), channel_id=1, source_target_pairs={{0,2},{1,3},{2,0},{3,1},{4,6},{5,7},{6,4},{7,5},{8,10},{9,11},{10,... | collective-permute-start | bytes 344072 | tf_op jit(solution)/shard_map/ppermute | solution.py:350
  7.0 10.0 %collective-permute-start = (bf16[28,16,128]{2,1,0:T(8,128)(2,1)S(1)}, bf16[28,16,128]{2,1,0:T(8,128)(2,1)S(1)}, u32[]{:S(2)}, u32[]{:S(2)}) collective-permute-start(bf16[28,16,128]{2,1,0:T(8,128)(2,1)S(1)} %constant_dynamic-slice_fusion.rest_0_), channel_id=1, source_target_pairs={{0,1},{1,2},{2,3},{3,0},{4,5},{5,6},{6,7},{7,4},{8,9},{9,10},{10,1... | collective-permute-start | bytes 344072 | tf_op jit(solution)/shard_map/ppermute | solution.py:350
  17.0 0.7 copy-start.24
  19.7 8.4 %collective-permute-start.8 = (bf16[44,16,128]{2,1,0:T(8,128)(2,1)}, bf16[44,16,128]{2,1,0:T(8,128)(2,1)S(1)}, u32[]{:S(2)}, u32[]{:S(2)}) collective-permute-start(bf16[44,16,128]{2,1,0:T(8,128)(2,1)} %get-tuple-element.42.rest_0_), channel_id=1, source_target_pairs={{0,24},{4,28},{8,16},{12,20},{16,8},{20,12},{24,0},{28,4},{1,25},{... | collective-permute-start | bytes 540680 | tf_op jit(solution)/shard_map/ppermute | solution.py:346
  22.1 8.4 %collective-permute-start.6 = (bf16[44,16,128]{2,1,0:T(8,128)(2,1)}, bf16[44,16,128]{2,1,0:T(8,128)(2,1)S(1)}, u32[]{:S(2)}, u32[]{:S(2)}) collective-permute-start(bf16[44,16,128]{2,1,0:T(8,128)(2,1)} %get-tuple-element.42.rest_0_), channel_id=1, source_target_pairs={{0,16},{4,20},{8,24},{12,28},{16,0},{20,4},{24,8},{28,12},{1,17},{... | collective-permute-start | bytes 540680 | tf_op jit(solution)/shard_map/ppermute | solution.py:346
  22.6 8.0 %collective-permute-start.4 = (bf16[44,16,128]{2,1,0:T(8,128)(2,1)}, bf16[44,16,128]{2,1,0:T(8,128)(2,1)S(1)}, u32[]{:S(2)}, u32[]{:S(2)}) collective-permute-start(bf16[44,16,128]{2,1,0:T(8,128)(2,1)} %get-tuple-element.42.rest_0_), channel_id=1, source_target_pairs={{0,8},{4,12},{8,0},{12,4},{16,24},{20,28},{24,16},{28,20},{1,9},{5... | collective-permute-start | bytes 540680 | tf_op jit(solution)/shard_map/ppermute | solution.py:346
  23.2 7.9 %collective-permute-start.3 = (bf16[44,16,128]{2,1,0:T(8,128)(2,1)}, bf16[44,16,128]{2,1,0:T(8,128)(2,1)S(1)}, u32[]{:S(2)}, u32[]{:S(2)}) collective-permute-start(bf16[44,16,128]{2,1,0:T(8,128)(2,1)} %get-tuple-element.42.rest_0_), channel_id=1, source_target_pairs={{0,4},{4,0},{8,12},{12,8},{16,20},{20,16},{24,28},{28,24},{1,5},{5... | collective-permute-start | bytes 540680 | tf_op jit(solution)/shard_map/ppermute | solution.py:346
  28.1 4.1 %copy-start.12 = (bf16[44,16,128]{2,1,0:T(8,128)(2,1)}, bf16[44,16,128]{2,1,0:T(8,128)(2,1)S(1)}, u32[]{:S(2)}) copy-start(bf16[44,16,128]{2,1,0:T(8,128)(2,1)S(1)} %collective-permute-done.8.rest_6_) | copy-start | bytes 540676
  28.1 3.0 %collective-permute-start.9 = (bf16[44,16,128]{2,1,0:T(8,128)(2,1)S(1)}, bf16[44,16,128]{2,1,0:T(8,128)(2,1)S(1)}, u32[]{:S(2)}, u32[]{:S(2)}) collective-permute-start(bf16[44,16,128]{2,1,0:T(8,128)(2,1)S(1)} %collective-permute-done.8.rest_6_), channel_id=1, source_target_pairs={{0,4},{4,0},{8,12},{12,8},{16,20},{20,16},{24,28},{28,24},{1,5},{5... | collective-permute-start | bytes 540680 | tf_op jit(solution)/shard_map/ppermute | solution.py:346
  30.5 1.7 %copy-start.13 = (bf16[44,16,128]{2,1,0:T(8,128)(2,1)}, bf16[44,16,128]{2,1,0:T(8,128)(2,1)S(1)}, u32[]{:S(2)}) copy-start(bf16[44,16,128]{2,1,0:T(8,128)(2,1)S(1)} %collective-permute-done.6.rest_4_) | copy-start | bytes 540676
  30.5 1.4 %collective-permute-start.7 = (bf16[44,16,128]{2,1,0:T(8,128)(2,1)S(1)}, bf16[44,16,128]{2,1,0:T(8,128)(2,1)S(1)}, u32[]{:S(2)}, u32[]{:S(2)}) collective-permute-start(bf16[44,16,128]{2,1,0:T(8,128)(2,1)S(1)} %collective-permute-done.6.rest_4_), channel_id=1, source_target_pairs={{0,4},{4,0},{8,12},{12,8},{16,20},{20,16},{24,28},{28,24},{1,5},{5... | collective-permute-start | bytes 540680 | tf_op jit(solution)/shard_map/ppermute | solution.py:346
  30.6 1.6 %copy-start.14 = (bf16[44,16,128]{2,1,0:T(8,128)(2,1)}, bf16[44,16,128]{2,1,0:T(8,128)(2,1)S(1)}, u32[]{:S(2)}) copy-start(bf16[44,16,128]{2,1,0:T(8,128)(2,1)S(1)} %collective-permute-done.4.rest_2_) | copy-start | bytes 540676
  30.6 1.6 %collective-permute-start.5 = (bf16[44,16,128]{2,1,0:T(8,128)(2,1)S(1)}, bf16[44,16,128]{2,1,0:T(8,128)(2,1)S(1)}, u32[]{:S(2)}, u32[]{:S(2)}) collective-permute-start(bf16[44,16,128]{2,1,0:T(8,128)(2,1)S(1)} %collective-permute-done.4.rest_2_), channel_id=1, source_target_pairs={{0,4},{4,0},{8,12},{12,8},{16,20},{20,16},{24,28},{28,24},{1,5},{5... | collective-permute-start | bytes 540680 | tf_op jit(solution)/shard_map/ppermute | solution.py:346
  31.0 1.2 copy-start.15
  31.0 1.2 copy-start.16
  31.9 0.7 copy-start.17
  32.6 0.7 copy-start.18
  42.5 11.1 %copy-start.37 = (f32[2,8,2048]{2,1,0:T(8,128)S(1)}, f32[2,8,2048]{2,1,0:T(8,128)}, u32[]{:S(2)}) copy-start(f32[2,8,2048]{2,1,0:T(8,128)} %get-tuple-element.71) | copy-start | bytes 393220
  42.5 18.3 %copy-start.36 = (bf16[128,1280]{1,0:T(8,128)(2,1)S(1)}, bf16[128,1280]{1,0:T(8,128)(2,1)}, u32[]{:S(2)}) copy-start(bf16[128,1280]{1,0:T(8,128)(2,1)} %get-tuple-element.46) | copy-start | bytes 983044
  42.5 25.1 %copy-start.35 = (bf16[128,1280]{1,0:T(8,128)(2,1)S(1)}, bf16[128,1280]{1,0:T(8,128)(2,1)}, u32[]{:S(2)}) copy-start(bf16[128,1280]{1,0:T(8,128)(2,1)} %get-tuple-element.47) | copy-start | bytes 983044
  46.7 1.6 %collective-permute-start.13 = (bf16[44,16,128]{2,1,0:T(8,128)(2,1)}, bf16[44,16,128]{2,1,0:T(8,128)(2,1)S(1)}, u32[]{:S(2)}, u32[]{:S(2)}) collective-permute-start(bf16[44,16,128]{2,1,0:T(8,128)(2,1)} %get-tuple-element.54), channel_id=1, source_target_pairs={{0,4},{4,0},{8,12},{12,8},{16,20},{20,16},{24,28},{28,24},{1,5},{5... | collective-permute-start | bytes 540680 | tf_op jit(solution)/shard_map/ppermute | solution.py:346
  46.8 1.7 %collective-permute-start.14 = (bf16[44,16,128]{2,1,0:T(8,128)(2,1)}, bf16[44,16,128]{2,1,0:T(8,128)(2,1)S(1)}, u32[]{:S(2)}, u32[]{:S(2)}) collective-permute-start(bf16[44,16,128]{2,1,0:T(8,128)(2,1)} %get-tuple-element.55), channel_id=1, source_target_pairs={{0,4},{4,0},{8,12},{12,8},{16,20},{20,16},{24,28},{28,24},{1,5},{5... | collective-permute-start | bytes 540680 | tf_op jit(solution)/shard_map/ppermute | solution.py:346
  47.2 1.6 %collective-permute-start.15 = (bf16[44,16,128]{2,1,0:T(8,128)(2,1)}, bf16[44,16,128]{2,1,0:T(8,128)(2,1)S(1)}, u32[]{:S(2)}, u32[]{:S(2)}) collective-permute-start(bf16[44,16,128]{2,1,0:T(8,128)(2,1)} %get-tuple-element.56), channel_id=1, source_target_pairs={{0,4},{4,0},{8,12},{12,8},{16,20},{20,16},{24,28},{28,24},{1,5},{5... | collective-permute-start | bytes 540680 | tf_op jit(solution)/shard_map/ppermute | solution.py:346
  47.3 1.8 %collective-permute-start.16 = (bf16[44,16,128]{2,1,0:T(8,128)(2,1)}, bf16[44,16,128]{2,1,0:T(8,128)(2,1)S(1)}, u32[]{:S(2)}, u32[]{:S(2)}) collective-permute-start(bf16[44,16,128]{2,1,0:T(8,128)(2,1)} %get-tuple-element.57), channel_id=1, source_target_pairs={{0,4},{4,0},{8,12},{12,8},{16,20},{20,16},{24,28},{28,24},{1,5},{5... | collective-permute-start | bytes 540680 | tf_op jit(solution)/shard_map/ppermute | solution.py:346
  48.3 0.8 copy-start.8
  48.6 0.7 copy-start.9
  49.1 0.7 copy-start.11
  52.1 10.1 %collective-permute-start.17 = (bf16[44,16,128]{2,1,0:T(8,128)(2,1)}, bf16[44,16,128]{2,1,0:T(8,128)(2,1)S(1)}, u32[]{:S(2)}, u32[]{:S(2)}) collective-permute-start(bf16[44,16,128]{2,1,0:T(8,128)(2,1)} %get-tuple-element.59), channel_id=1, source_target_pairs={{0,8},{4,12},{8,0},{12,4},{16,24},{20,28},{24,16},{28,20},{1,9},{5... | collective-permute-start | bytes 540680 | tf_op jit(solution)/shard_map/ppermute | solution.py:346
  53.6 7.2 %collective-permute-start.23 = (f32[2,8,2048]{2,1,0:T(8,128)S(1)}, f32[2,8,2048]{2,1,0:T(8,128)S(1)}, u32[]{:S(2)}, u32[]{:S(2)}) collective-permute-start(f32[2,8,2048]{2,1,0:T(8,128)S(1)} %copy-done.37), channel_id=1, source_target_pairs={{0,1},{1,2},{2,3},{3,0},{4,5},{5,6},{6,7},{7,4},{8,9},{9,10},{10,1... | collective-permute-start | bytes 393224 | tf_op jit(solution)/shard_map/ppermute | solution.py:350
  55.1 10.2 %collective-permute-start.18 = (bf16[44,16,128]{2,1,0:T(8,128)(2,1)}, bf16[44,16,128]{2,1,0:T(8,128)(2,1)S(1)}, u32[]{:S(2)}, u32[]{:S(2)}) collective-permute-start(bf16[44,16,128]{2,1,0:T(8,128)(2,1)} %get-tuple-element.60), channel_id=1, source_target_pairs={{0,16},{4,20},{8,24},{12,28},{16,0},{20,4},{24,8},{28,12},{1,17},{... | collective-permute-start | bytes 540680 | tf_op jit(solution)/shard_map/ppermute | solution.py:346
  55.9 11.7 %collective-permute-start.19 = (bf16[44,16,128]{2,1,0:T(8,128)(2,1)}, bf16[44,16,128]{2,1,0:T(8,128)(2,1)S(1)}, u32[]{:S(2)}, u32[]{:S(2)}) collective-permute-start(bf16[44,16,128]{2,1,0:T(8,128)(2,1)} %get-tuple-element.61), channel_id=1, source_target_pairs={{0,24},{4,28},{8,16},{12,20},{16,8},{20,12},{24,0},{28,4},{1,25},{... | collective-permute-start | bytes 540680 | tf_op jit(solution)/shard_map/ppermute | solution.py:346
  57.1 53.8 %collective-permute-start.10 = (bf16[128,1280]{1,0:T(8,128)(2,1)}, bf16[128,1280]{1,0:T(8,128)(2,1)S(1)}, u32[]{:S(2)}, u32[]{:S(2)}) collective-permute-start(bf16[128,1280]{1,0:T(8,128)(2,1)} %get-tuple-element.45), channel_id=1, source_target_pairs={{0,1},{1,2},{2,3},{3,0},{4,5},{5,6},{6,7},{7,4},{8,9},{9,10},{10,1... | collective-permute-start | bytes 983048 | tf_op jit(solution)/shard_map/ppermute | solution.py:350
  60.7 44.6 %copy-start.19 = (f32[2,8,2048]{2,1,0:T(8,128)}, f32[2,8,2048]{2,1,0:T(8,128)S(1)}, u32[]{:S(2)}) copy-start(f32[2,8,2048]{2,1,0:T(8,128)S(1)} %collective-permute-done.23.rest_5_) | copy-start | bytes 393220
  60.7 51.0 %collective-permute-start.11 = (bf16[128,1280]{1,0:T(8,128)(2,1)S(1)}, bf16[128,1280]{1,0:T(8,128)(2,1)S(1)}, u32[]{:S(2)}, u32[]{:S(2)}) collective-permute-start(bf16[128,1280]{1,0:T(8,128)(2,1)S(1)} %copy-done.36), channel_id=1, source_target_pairs={{0,2},{1,3},{2,0},{3,1},{4,6},{5,7},{6,4},{7,5},{8,10},{9,11},{10,... | collective-permute-start | bytes 983048 | tf_op jit(solution)/shard_map/ppermute | solution.py:350
  62.2 5.9 %copy-start.5 = (bf16[44,16,128]{2,1,0:T(8,128)(2,1)}, bf16[44,16,128]{2,1,0:T(8,128)(2,1)S(1)}, u32[]{:S(2)}) copy-start(bf16[44,16,128]{2,1,0:T(8,128)(2,1)S(1)} %collective-permute-done.17.rest_1_) | copy-start | bytes 540676
  62.2 25.5 %collective-permute-start.24 = (f32[2,8,2048]{2,1,0:T(8,128)}, f32[2,8,2048]{2,1,0:T(8,128)S(1)}, u32[]{:S(2)}, u32[]{:S(2)}) collective-permute-start(f32[2,8,2048]{2,1,0:T(8,128)} %get-tuple-element.72), channel_id=1, source_target_pairs={{0,2},{1,3},{2,0},{3,1},{4,6},{5,7},{6,4},{7,5},{8,10},{9,11},{10,... | collective-permute-start | bytes 393224 | tf_op jit(solution)/shard_map/ppermute | solution.py:350
  65.4 2.7 %copy-start.6 = (bf16[44,16,128]{2,1,0:T(8,128)(2,1)}, bf16[44,16,128]{2,1,0:T(8,128)(2,1)S(1)}, u32[]{:S(2)}) copy-start(bf16[44,16,128]{2,1,0:T(8,128)(2,1)S(1)} %collective-permute-done.18.rest_2_) | copy-start | bytes 540676
  65.4 30.7 %collective-permute-start.25 = (f32[2,8,2048]{2,1,0:T(8,128)}, f32[2,8,2048]{2,1,0:T(8,128)S(1)}, u32[]{:S(2)}, u32[]{:S(2)}) collective-permute-start(f32[2,8,2048]{2,1,0:T(8,128)} %get-tuple-element.73), channel_id=1, source_target_pairs={{0,3},{1,0},{2,1},{3,2},{4,7},{5,4},{6,5},{7,6},{8,11},{9,8},{10,9... | collective-permute-start | bytes 393224 | tf_op jit(solution)/shard_map/ppermute | solution.py:350
  67.6 0.7 copy-start.7
  67.6 48.0 %collective-permute-start.12 = (bf16[128,1280]{1,0:T(8,128)(2,1)S(1)}, bf16[128,1280]{1,0:T(8,128)(2,1)S(1)}, u32[]{:S(2)}, u32[]{:S(2)}) collective-permute-start(bf16[128,1280]{1,0:T(8,128)(2,1)S(1)} %copy-done.35), channel_id=1, source_target_pairs={{0,3},{1,0},{2,1},{3,2},{4,7},{5,4},{6,5},{7,6},{8,11},{9,8},{10,9... | collective-permute-start | bytes 983048 | tf_op jit(solution)/shard_map/ppermute | solution.py:350
  87.7 17.6 %copy-start.20 = (f32[2,8,2048]{2,1,0:T(8,128)}, f32[2,8,2048]{2,1,0:T(8,128)S(1)}, u32[]{:S(2)}) copy-start(f32[2,8,2048]{2,1,0:T(8,128)S(1)} %collective-permute-done.24.rest_6_) | copy-start | bytes 393220
  87.7 13.3 %collective-permute-start.20 = (bf16[11,16,128]{2,1,0:T(8,128)(2,1)}, bf16[11,16,128]{2,1,0:T(8,128)(2,1)S(1)}, u32[]{:S(2)}, u32[]{:S(2)}) collective-permute-start(bf16[11,16,128]{2,1,0:T(8,128)(2,1)} %get-tuple-element.63), channel_id=1, source_target_pairs={{0,1},{1,2},{2,3},{3,0},{4,5},{5,6},{6,7},{7,4},{8,9},{9,10},{10,1... | collective-permute-start | bytes 135176 | tf_op jit(solution)/shard_map/ppermute | solution.py:350
  96.1 9.2 %copy-start.21 = (f32[2,8,2048]{2,1,0:T(8,128)}, f32[2,8,2048]{2,1,0:T(8,128)S(1)}, u32[]{:S(2)}) copy-start(f32[2,8,2048]{2,1,0:T(8,128)S(1)} %collective-permute-done.25.rest_7_) | copy-start | bytes 393220
  96.1 7.0 %collective-permute-start.21 = (bf16[11,16,128]{2,1,0:T(8,128)(2,1)}, bf16[11,16,128]{2,1,0:T(8,128)(2,1)S(1)}, u32[]{:S(2)}, u32[]{:S(2)}) collective-permute-start(bf16[11,16,128]{2,1,0:T(8,128)(2,1)} %get-tuple-element.64), channel_id=1, source_target_pairs={{0,2},{1,3},{2,0},{3,1},{4,6},{5,7},{6,4},{7,5},{8,10},{9,11},{10,... | collective-permute-start | bytes 135176 | tf_op jit(solution)/shard_map/ppermute | solution.py:350
  101.0 4.3 %copy-start.32 = (bf16[11,16,128]{2,1,0:T(8,128)(2,1)}, bf16[11,16,128]{2,1,0:T(8,128)(2,1)S(1)}, u32[]{:S(2)}) copy-start(bf16[11,16,128]{2,1,0:T(8,128)(2,1)S(1)} %collective-permute-done.20.rest_1_) | copy-start | bytes 135172
  101.0 4.3 %collective-permute-start.22 = (bf16[11,16,128]{2,1,0:T(8,128)(2,1)}, bf16[11,16,128]{2,1,0:T(8,128)(2,1)S(1)}, u32[]{:S(2)}, u32[]{:S(2)}) collective-permute-start(bf16[11,16,128]{2,1,0:T(8,128)(2,1)} %get-tuple-element.65), channel_id=1, source_target_pairs={{0,3},{1,0},{2,1},{3,2},{4,7},{5,4},{6,5},{7,6},{8,11},{9,8},{10,9... | collective-permute-start | bytes 135176 | tf_op jit(solution)/shard_map/ppermute | solution.py:350
  103.0 2.3 %copy-start.33 = (bf16[11,16,128]{2,1,0:T(8,128)(2,1)}, bf16[11,16,128]{2,1,0:T(8,128)(2,1)S(1)}, u32[]{:S(2)}) copy-start(bf16[11,16,128]{2,1,0:T(8,128)(2,1)S(1)} %collective-permute-done.21.rest_2_) | copy-start | bytes 135172
  108.2 5.6 %collective-permute-start.31 = (bf16[20,16,128]{2,1,0:T(8,128)(2,1)}, bf16[20,16,128]{2,1,0:T(8,128)(2,1)S(1)}, u32[]{:S(2)}, u32[]{:S(2)}) collective-permute-start(bf16[20,16,128]{2,1,0:T(8,128)(2,1)} %get-tuple-element.74.rest_0_), channel_id=1, source_target_pairs={{0,24},{4,28},{8,16},{12,20},{16,8},{20,12},{24,0},{28,4},{1,25},{... | collective-permute-start | bytes 245768 | tf_op jit(solution)/shard_map/ppermute | solution.py:346
  110.0 4.7 %collective-permute-start.29 = (bf16[20,16,128]{2,1,0:T(8,128)(2,1)}, bf16[20,16,128]{2,1,0:T(8,128)(2,1)S(1)}, u32[]{:S(2)}, u32[]{:S(2)}) collective-permute-start(bf16[20,16,128]{2,1,0:T(8,128)(2,1)} %get-tuple-element.74.rest_0_), channel_id=1, source_target_pairs={{0,16},{4,20},{8,24},{12,28},{16,0},{20,4},{24,8},{28,12},{1,17},{... | collective-permute-start | bytes 245768 | tf_op jit(solution)/shard_map/ppermute | solution.py:346
  110.9 4.7 %copy-start.2 = (bf16[128,1280]{1,0:T(8,128)(2,1)}, bf16[128,1280]{1,0:T(8,128)(2,1)S(1)}, u32[]{:S(2)}) copy-start(bf16[128,1280]{1,0:T(8,128)(2,1)S(1)} %collective-permute-done.10.rest_0_) | copy-start | bytes 983044
  110.9 4.7 %collective-permute-start.27 = (bf16[20,16,128]{2,1,0:T(8,128)(2,1)}, bf16[20,16,128]{2,1,0:T(8,128)(2,1)S(1)}, u32[]{:S(2)}, u32[]{:S(2)}) collective-permute-start(bf16[20,16,128]{2,1,0:T(8,128)(2,1)} %get-tuple-element.74.rest_0_), channel_id=1, source_target_pairs={{0,8},{4,12},{8,0},{12,4},{16,24},{20,28},{24,16},{28,20},{1,9},{5... | collective-permute-start | bytes 245768 | tf_op jit(solution)/shard_map/ppermute | solution.py:346
  111.7 3.9 %copy-start.3 = (bf16[128,1280]{1,0:T(8,128)(2,1)}, bf16[128,1280]{1,0:T(8,128)(2,1)S(1)}, u32[]{:S(2)}) copy-start(bf16[128,1280]{1,0:T(8,128)(2,1)S(1)} %collective-permute-done.11.rest_1_) | copy-start | bytes 983044
  111.7 6.8 %collective-permute-start.26 = (bf16[20,16,128]{2,1,0:T(8,128)(2,1)}, bf16[20,16,128]{2,1,0:T(8,128)(2,1)S(1)}, u32[]{:S(2)}, u32[]{:S(2)}) collective-permute-start(bf16[20,16,128]{2,1,0:T(8,128)(2,1)} %get-tuple-element.74.rest_0_), channel_id=1, source_target_pairs={{0,4},{4,0},{8,12},{12,8},{16,20},{20,16},{24,28},{28,24},{1,5},{5... | collective-permute-start | bytes 245768 | tf_op jit(solution)/shard_map/ppermute | solution.py:346
  113.8 4.8 %copy-start.25 = (bf16[20,16,128]{2,1,0:T(8,128)(2,1)}, bf16[20,16,128]{2,1,0:T(8,128)(2,1)S(1)}, u32[]{:S(2)}) copy-start(bf16[20,16,128]{2,1,0:T(8,128)(2,1)S(1)} %collective-permute-done.31.rest_6_) | copy-start | bytes 245764
  113.8 4.8 %collective-permute-start.32 = (bf16[20,16,128]{2,1,0:T(8,128)(2,1)S(1)}, bf16[20,16,128]{2,1,0:T(8,128)(2,1)S(1)}, u32[]{:S(2)}, u32[]{:S(2)}) collective-permute-start(bf16[20,16,128]{2,1,0:T(8,128)(2,1)S(1)} %collective-permute-done.31.rest_6_), channel_id=1, source_target_pairs={{0,4},{4,0},{8,12},{12,8},{16,20},{20,16},{24,28},{28,24},{1,5},{5... | collective-permute-start | bytes 245768 | tf_op jit(solution)/shard_map/ppermute | solution.py:346
  114.7 4.0 %copy-start.26 = (bf16[20,16,128]{2,1,0:T(8,128)(2,1)}, bf16[20,16,128]{2,1,0:T(8,128)(2,1)S(1)}, u32[]{:S(2)}) copy-start(bf16[20,16,128]{2,1,0:T(8,128)(2,1)S(1)} %collective-permute-done.29.rest_4_) | copy-start | bytes 245764
  114.7 3.9 %collective-permute-start.30 = (bf16[20,16,128]{2,1,0:T(8,128)(2,1)S(1)}, bf16[20,16,128]{2,1,0:T(8,128)(2,1)S(1)}, u32[]{:S(2)}, u32[]{:S(2)}) collective-permute-start(bf16[20,16,128]{2,1,0:T(8,128)(2,1)S(1)} %collective-permute-done.29.rest_4_), channel_id=1, source_target_pairs={{0,4},{4,0},{8,12},{12,8},{16,20},{20,16},{24,28},{28,24},{1,5},{5... | collective-permute-start | bytes 245768 | tf_op jit(solution)/shard_map/ppermute | solution.py:346
  115.6 3.1 %copy-start.27 = (bf16[20,16,128]{2,1,0:T(8,128)(2,1)}, bf16[20,16,128]{2,1,0:T(8,128)(2,1)S(1)}, u32[]{:S(2)}) copy-start(bf16[20,16,128]{2,1,0:T(8,128)(2,1)S(1)} %collective-permute-done.27.rest_2_) | copy-start | bytes 245764
  115.6 3.0 %collective-permute-start.28 = (bf16[20,16,128]{2,1,0:T(8,128)(2,1)S(1)}, bf16[20,16,128]{2,1,0:T(8,128)(2,1)S(1)}, u32[]{:S(2)}, u32[]{:S(2)}) collective-permute-start(bf16[20,16,128]{2,1,0:T(8,128)(2,1)S(1)} %collective-permute-done.27.rest_2_), channel_id=1, source_target_pairs={{0,4},{4,0},{8,12},{12,8},{16,20},{20,16},{24,28},{28,24},{1,5},{5... | collective-permute-start | bytes 245768 | tf_op jit(solution)/shard_map/ppermute | solution.py:346
  115.6 0.7 copy-start.4
  118.6 0.7 copy-start.30
  (7 other events, 4.5 us)
where the time goes:
time: 122 us
  starting transfers between devices  40.2 us (33%)
  waiting for transfers between devices  39.7 us (33%)
  Pallas kernels  34.2 us (28%)
  local copies, waits for them, and re-layouts  6.45 us (5%)
    ppermute x12, starting transfers between devices, shift(): return lax.ppermute(value, 'mp', [(i, (i + step) % n) for i in range(n)])  28.3 us
    ppermute x12, waiting for transfers between devices, shift(): return lax.ppermute(value, 'mp', [(i, (i + step) % n) for i in range(n)])  24.2 us
    ppermute x21, waiting for transfers between devices, swap(): return lax.ppermute(value, 'dp', [(i, i ^ bits) for i in range(parts)])  15.5 us
    ppermute x21, starting transfers between devices, swap(): return lax.ppermute(value, 'dp', [(i, i ^ bits) for i in range(parts)])  11.9 us
    pallas_call x1, Pallas kernels, step(): call(functools.partial(forward_kernel, (n, bs, bw, blk, len(pieces))), [s...  9.18 us
    pallas_call x1, Pallas kernels, step(): call(functools.partial(plan_kernel, (n, per, cap, ms, bs, bw, pad)), [sha...  7.78 us
    unnamed x76, local copies, waits for them, and re-layouts  6.43 us
    pallas_call x1, Pallas kernels, step(): call(functools.partial(grad_kernel, (n, bs, blk, count)), [shape((slots,...  4.19 us
  transfers between devices with their start and end apart: 33, of which 18 were waited for; matrix products, arithmetic and copies ran while one was open for 1% of the time, Pallas kernels for 12%

commit v1 on v0

--- a/solution.py
+++ b/solution.py
@@ -16,14 +16,30 @@
 SQRT_2_OVER_PI = math.sqrt(2.0 / math.pi)
 
 
+ROOM_BYTES = 4 << 20
+
 VMEM = pl.BlockSpec(memory_space=pltpu.VMEM)
 SMEM = pl.BlockSpec(memory_space=pltpu.SMEM)
 
 
+def size_of(item):
+    return math.prod(item.shape) * jnp.dtype(item.dtype).itemsize
+
+
 def call(kernel, out_shape, in_specs, out_specs, scratch):
-    return pl.pallas_call(
-        kernel, out_shape=out_shape, in_specs=in_specs, out_specs=out_specs, scratch_shapes=scratch
-    )
+    def run(*args):
+        outs = out_shape if isinstance(out_shape, list) else [out_shape]
+        room = sum(size_of(x) for x in (*args, *outs)) + sum(size_of(x) for x in scratch)
+        return pl.pallas_call(
+            kernel,
+            out_shape=out_shape,
+            in_specs=in_specs,
+            out_specs=out_specs,
+            scratch_shapes=scratch,
+            compiler_params=pltpu.CompilerParams(vmem_limit_bytes=room + ROOM_BYTES),
+        )(*args)
+
+    return run
 
 
 def shape(dims, dtype):

time: 122 us -> 110 us (0.902)
  Pallas kernels: 34.2 us -> 21.9 us
  waiting for transfers between devices: 39.7 us -> 41.4 us
    pallas_call x9, Pallas kernels: 34.2 us -> 21.9 us  [run(): pl.pallas_call(kernel, out_shape=out_shape, in_specs=in_specs, out_specs=...]
    ppermute x12, waiting for transfers between devices: 24.2 us -> 25.7 us  [shift(): return lax.ppermute(value, 'mp', [(i, (i + step) % n) for i in range(n)])]
    unnamed x76 -> x14, local copies, waits for them, and re-layouts: 6.43 us -> 5.71 us
  transfers between devices with their start and end apart: 33 -> 33, of which waited for: 18 -> 18; matrix products, arithmetic and copies ran while one was open for 1% -> 0% of each run, Pallas kernels for 12% -> 9%
where the time goes in v1:
time: 110 us; the launch traced here: 109 us
  waiting for transfers between devices  41.4 us (38%)
  starting transfers between devices  39.5 us (36%)
  Pallas kernels  21.9 us (20%)
  local copies, waits for them, and re-layouts  5.73 us (5%)
    ppermute x12, starting transfers between devices, shift(): return lax.ppermute(value, 'mp', [(i, (i + step) % n) for i in range(n)])  27.3 us
    ppermute x12, waiting for transfers between devices, shift(): return lax.ppermute(value, 'mp', [(i, (i + step) % n) for i in range(n)])  25.7 us
    pallas_call x9, Pallas kernels, run(): pl.pallas_call(kernel, out_shape=out_shape, in_specs=in_specs, out_specs=...  21.9 us
    ppermute x21, waiting for transfers between devices, swap(): return lax.ppermute(value, 'dp', [(i, i ^ bits) for i in range(parts)])  15.7 us
    ppermute x21, starting transfers between devices, swap(): return lax.ppermute(value, 'dp', [(i, i ^ bits) for i in range(parts)])  12.1 us
    unnamed x14, local copies, waits for them, and re-layouts  5.71 us
  transfers between devices with their start and end apart: 33, of which 18 were waited for; matrix products, arithmetic and copies ran while one was open for 0% of the time, Pallas kernels for 9%

profile of v1, /device:TPU:0, one launch (start us, length us, event | category | flops | bytes accessed | tf_op | source)
XLA Modules:
  0.0 109.4 jit_solution(2932257408255685014)
XLA Ops:
  0.6 0.0 copy-start
  0.7 1.2 %copy-done = bf16[28,128,128]{2,1,0:T(8,128)(2,1)S(1)} copy-done((bf16[28,128,128]{2,1,0:T(8,128)(2,1)S(1)}, bf16[28,128,128]{2,1,0:T(8,128)(2,1)}, u32[]{:S(2)}) %copy-start) | copy-done | bytes 917528
  1.8 5.1 %collective-permute-start.2 = (bf16[28,16,128]{2,1,0:T(8,128)(2,1)S(1)}, bf16[28,16,128]{2,1,0:T(8,128)(2,1)S(1)}, u32[]{:S(2)}, u32[]{:S(2)}) collective-permute-start(bf16[28,16,128]{2,1,0:T(8,128)(2,1)S(1)} %constant_dynamic-slice_fusion.rest_0_), channel_id=1, source_target_pairs={{0,3},{1,0},{2,1},{3,2},{4,7},{5,4},{6,5},{7,6},{8,11},{9,8},{10,9... | collective-permute-start | bytes 344072 | tf_op jit(solution)/shard_map/ppermute | solution.py:366
  7.0 0.0 collective-permute-start.1
  7.0 1.0 collective-permute-start
  8.0 0.1 pad_add_fusion.here
  8.1 0.9 copy-done.3
  9.0 0.9 copy-done.4
  10.0 0.7 copy-done.5
  10.6 0.7 copy-done.6
  11.3 7.1 %shard_map.110 = (s32[192]{0:T(256)S(1)}, f32[2,8,2048]{2,1,0:T(8,128)S(1)}, f32[2,8,2048]{2,1,0:T(8,128)S(1)}, f32[2,8,2048]{2,1,0:T(8,128)S(1)}, f32[2,8,2048]{2,1,0:T(8,128)S(1)}) custom-call(s32[2]{0:T(128)S(1)} %pad_add_fusion.here, s32[2,80]{1,0:T(2,128)S(1)} %bitcast.3, s32[112]{0:T(128)S(1)} %copy-done.6, f32[28,2048]{1,0:T(8,128)S(1)} %copy-done.3, ...), custom_call_target="tpu_custom_call" | custom-call | tf_op jit(solution)/shard_map/pallas_call | solution.py:33
  18.4 0.0 collective-permute-done.1.rest_2_
  18.4 0.0 collective-permute-done.rest_1_
  18.4 0.8 shard_map.111
  19.2 2.5 %collective-permute-start.8 = (bf16[44,16,128]{2,1,0:T(8,128)(2,1)S(1)}, bf16[44,16,128]{2,1,0:T(8,128)(2,1)S(1)}, u32[]{:S(2)}, u32[]{:S(2)}) collective-permute-start(bf16[44,16,128]{2,1,0:T(8,128)(2,1)S(1)} %get-tuple-element.42.rest_0_), channel_id=1, source_target_pairs={{0,24},{4,28},{8,16},{12,20},{16,8},{20,12},{24,0},{28,4},{1,25},{... | collective-permute-start | bytes 540680 | tf_op jit(solution)/shard_map/ppermute | solution.py:362
  21.7 0.5 collective-permute-start.6
  22.3 0.5 collective-permute-start.4
  22.8 0.0 collective-permute-start.3
  22.8 4.4 %collective-permute-done.8.rest_6_ = bf16[44,16,128]{2,1,0:T(8,128)(2,1)S(1)} collective-permute-done((bf16[44,16,128]{2,1,0:T(8,128)(2,1)S(1)}, bf16[44,16,128]{2,1,0:T(8,128)(2,1)S(1)}, u32[]{:S(2)}, u32[]{:S(2)}) %collective-permute-start.8) | collective-permute-done | bytes 180256 | tf_op jit(solution)/shard_map/ppermute | solution.py:362
  27.2 2.4 %collective-permute-done.6.rest_4_ = bf16[44,16,128]{2,1,0:T(8,128)(2,1)S(1)} collective-permute-done((bf16[44,16,128]{2,1,0:T(8,128)(2,1)S(1)}, bf16[44,16,128]{2,1,0:T(8,128)(2,1)S(1)}, u32[]{:S(2)}, u32[]{:S(2)}) %collective-permute-start.6) | collective-permute-done | bytes 180256 | tf_op jit(solution)/shard_map/ppermute | solution.py:362
  29.5 0.1 collective-permute-done.4.rest_2_
  29.6 0.4 collective-permute-start.5
  30.0 0.9 collective-permute-done.7.rest_5_
  30.9 0.3 collective-permute-done.5.rest_3_
  31.2 1.3 %copy-done.1 = bf16[128,5120]{1,0:T(8,128)(2,1)S(1)} copy-done((bf16[128,5120]{1,0:T(8,128)(2,1)S(1)}, bf16[128,5120]{1,0:T(8,128)(2,1)}, u32[]{:S(2)}) %copy-start.1) | copy-done | bytes 1310744
  32.5 7.0 %shard_map.112 = (bf16[128,2560]{1,0:T(8,128)(2,1)}, bf16[128,2560]{1,0:T(8,128)(2,1)S(1)}, bf16[128,1280]{1,0:T(8,128)(2,1)S(1)}, bf16[128,1280]{1,0:T(8,128)(2...) custom-call(s32[2]{0:T(128)S(1)} %pad_add_fusion.here, s32[192]{0:T(256)S(1)} %get-tuple-element.41.table, ...), custom_call_target="tpu_custom_call" | custom-call | tf_op jit(solution)/shard_map/pallas_call | solution.py:33
  39.6 2.1 %shard_map.114 = (bf16[44,16,128]{2,1,0:T(8,128)(2,1)S(1)}, bf16[44,16,128]{2,1,0:T(8,128)(2,1)S(1)}, bf16[44,16,128]{2,1,0:T(8,128)(2,1)S(1)}, bf16[44,16,128]{...) custom-call(s32[2]{0:T(128)S(1)} %pad_add_fusion.here, ...), custom_call_target="tpu_custom_call" | custom-call | tf_op jit(solution)/shard_map/pallas_call | solution.py:33
  41.7 0.3 collective-permute-start.13
  42.0 0.3 collective-permute-start.14
  42.2 0.3 collective-permute-start.15
  42.5 0.3 collective-permute-start.16
  42.7 0.4 collective-permute-done.13.refs_4_
  43.1 0.3 collective-permute-done.14.refs_5_
  43.4 0.3 collective-permute-done.15.refs_6_
  43.7 0.3 collective-permute-done.16.refs_7_
  43.9 0.2 shard_map.115
  44.1 1.6 %collective-permute-start.17 = (bf16[44,16,128]{2,1,0:T(8,128)(2,1)S(1)}, bf16[44,16,128]{2,1,0:T(8,128)(2,1)S(1)}, u32[]{:S(2)}, u32[]{:S(2)}) collective-permute-start(bf16[44,16,128]{2,1,0:T(8,128)(2,1)S(1)} %get-tuple-element.59), channel_id=1, source_target_pairs={{0,8},{4,12},{8,0},{12,4},{16,24},{20,28},{24,16},{28,20},{1,9},{5... | collective-permute-start | bytes 540680 | tf_op jit(solution)/shard_map/ppermute | solution.py:362
  45.6 2.4 %collective-permute-start.23 = (f32[2,8,2048]{2,1,0:T(8,128)S(1)}, f32[2,8,2048]{2,1,0:T(8,128)S(1)}, u32[]{:S(2)}, u32[]{:S(2)}) collective-permute-start(f32[2,8,2048]{2,1,0:T(8,128)S(1)} %get-tuple-element.71), channel_id=1, source_target_pairs={{0,1},{1,2},{2,3},{3,0},{4,5},{5,6},{6,7},{7,4},{8,9},{9,10},{10,1... | collective-permute-start | bytes 393224 | tf_op jit(solution)/shard_map/ppermute | solution.py:366
  48.1 0.8 collective-permute-start.18
  48.9 1.2 %collective-permute-start.19 = (bf16[44,16,128]{2,1,0:T(8,128)(2,1)S(1)}, bf16[44,16,128]{2,1,0:T(8,128)(2,1)S(1)}, u32[]{:S(2)}, u32[]{:S(2)}) collective-permute-start(bf16[44,16,128]{2,1,0:T(8,128)(2,1)S(1)} %get-tuple-element.61), channel_id=1, source_target_pairs={{0,24},{4,28},{8,16},{12,20},{16,8},{20,12},{24,0},{28,4},{1,25},{... | collective-permute-start | bytes 540680 | tf_op jit(solution)/shard_map/ppermute | solution.py:362
  50.1 0.3 collective-permute-start.10
  50.4 2.4 %collective-permute-done.23.rest_5_ = f32[2,8,2048]{2,1,0:T(8,128)S(1)} collective-permute-done((f32[2,8,2048]{2,1,0:T(8,128)S(1)}, f32[2,8,2048]{2,1,0:T(8,128)S(1)}, u32[]{:S(2)}, u32[]{:S(2)}) %collective-permute-start.23) | collective-permute-done | bytes 131104 | tf_op jit(solution)/shard_map/ppermute | solution.py:366
  52.8 0.5 collective-permute-start.11
  53.4 2.4 %collective-permute-start.24 = (f32[2,8,2048]{2,1,0:T(8,128)S(1)}, f32[2,8,2048]{2,1,0:T(8,128)S(1)}, u32[]{:S(2)}, u32[]{:S(2)}) collective-permute-start(f32[2,8,2048]{2,1,0:T(8,128)S(1)} %get-tuple-element.72), channel_id=1, source_target_pairs={{0,2},{1,3},{2,0},{3,1},{4,6},{5,7},{6,4},{7,5},{8,10},{9,11},{10,... | collective-permute-start | bytes 393224 | tf_op jit(solution)/shard_map/ppermute | solution.py:366
  55.7 2.3 %collective-permute-done.18.rest_2_ = bf16[44,16,128]{2,1,0:T(8,128)(2,1)S(1)} collective-permute-done((bf16[44,16,128]{2,1,0:T(8,128)(2,1)S(1)}, bf16[44,16,128]{2,1,0:T(8,128)(2,1)S(1)}, u32[]{:S(2)}, u32[]{:S(2)}) %collective-permute-start.18) | collective-permute-done | bytes 180256 | tf_op jit(solution)/shard_map/ppermute | solution.py:362
  58.1 1.4 %collective-permute-start.25 = (f32[2,8,2048]{2,1,0:T(8,128)S(1)}, f32[2,8,2048]{2,1,0:T(8,128)S(1)}, u32[]{:S(2)}, u32[]{:S(2)}) collective-permute-start(f32[2,8,2048]{2,1,0:T(8,128)S(1)} %get-tuple-element.73), channel_id=1, source_target_pairs={{0,3},{1,0},{2,1},{3,2},{4,7},{5,4},{6,5},{7,6},{8,11},{9,8},{10,9... | collective-permute-start | bytes 393224 | tf_op jit(solution)/shard_map/ppermute | solution.py:366
  59.5 1.3 %collective-permute-start.12 = (bf16[128,1280]{1,0:T(8,128)(2,1)S(1)}, bf16[128,1280]{1,0:T(8,128)(2,1)S(1)}, u32[]{:S(2)}, u32[]{:S(2)}) collective-permute-start(bf16[128,1280]{1,0:T(8,128)(2,1)S(1)} %get-tuple-element.47), channel_id=1, source_target_pairs={{0,3},{1,0},{2,1},{3,2},{4,7},{5,4},{6,5},{7,6},{8,11},{9,8},{10,9... | collective-permute-start | bytes 983048 | tf_op jit(solution)/shard_map/ppermute | solution.py:366
  60.8 0.7 shard_map.116
  61.5 18.9 %collective-permute-done.24.rest_6_ = f32[2,8,2048]{2,1,0:T(8,128)S(1)} collective-permute-done((f32[2,8,2048]{2,1,0:T(8,128)S(1)}, f32[2,8,2048]{2,1,0:T(8,128)S(1)}, u32[]{:S(2)}, u32[]{:S(2)}) %collective-permute-start.24) | collective-permute-done | bytes 131104 | tf_op jit(solution)/shard_map/ppermute | solution.py:366
  80.4 7.9 %collective-permute-start.20 = (bf16[11,16,128]{2,1,0:T(8,128)(2,1)S(1)}, bf16[11,16,128]{2,1,0:T(8,128)(2,1)S(1)}, u32[]{:S(2)}, u32[]{:S(2)}) collective-permute-start(bf16[11,16,128]{2,1,0:T(8,128)(2,1)S(1)} %get-tuple-element.63), channel_id=1, source_target_pairs={{0,1},{1,2},{2,3},{3,0},{4,5},{5,6},{6,7},{7,4},{8,9},{9,10},{10,1... | collective-permute-start | bytes 135176 | tf_op jit(solution)/shard_map/ppermute | solution.py:366
  88.3 3.4 %collective-permute-start.21 = (bf16[11,16,128]{2,1,0:T(8,128)(2,1)S(1)}, bf16[11,16,128]{2,1,0:T(8,128)(2,1)S(1)}, u32[]{:S(2)}, u32[]{:S(2)}) collective-permute-start(bf16[11,16,128]{2,1,0:T(8,128)(2,1)S(1)} %get-tuple-element.64), channel_id=1, source_target_pairs={{0,2},{1,3},{2,0},{3,1},{4,6},{5,7},{6,4},{7,5},{8,10},{9,11},{10,... | collective-permute-start | bytes 135176 | tf_op jit(solution)/shard_map/ppermute | solution.py:366
  91.7 1.9 %collective-permute-done.20.rest_1_ = bf16[11,16,128]{2,1,0:T(8,128)(2,1)S(1)} collective-permute-done((bf16[11,16,128]{2,1,0:T(8,128)(2,1)S(1)}, bf16[11,16,128]{2,1,0:T(8,128)(2,1)S(1)}, u32[]{:S(2)}, u32[]{:S(2)}) %collective-permute-start.20) | collective-permute-done | bytes 45088 | tf_op jit(solution)/shard_map/ppermute | solution.py:366
  93.5 1.6 %collective-permute-start.22 = (bf16[11,16,128]{2,1,0:T(8,128)(2,1)S(1)}, bf16[11,16,128]{2,1,0:T(8,128)(2,1)S(1)}, u32[]{:S(2)}, u32[]{:S(2)}) collective-permute-start(bf16[11,16,128]{2,1,0:T(8,128)(2,1)S(1)} %get-tuple-element.65), channel_id=1, source_target_pairs={{0,3},{1,0},{2,1},{3,2},{4,7},{5,4},{6,5},{7,6},{8,11},{9,8},{10,9... | collective-permute-start | bytes 135176 | tf_op jit(solution)/shard_map/ppermute | solution.py:366
  95.1 2.4 %collective-permute-done.22.rest_3_ = bf16[11,16,128]{2,1,0:T(8,128)(2,1)S(1)} collective-permute-done((bf16[11,16,128]{2,1,0:T(8,128)(2,1)S(1)}, bf16[11,16,128]{2,1,0:T(8,128)(2,1)S(1)}, u32[]{:S(2)}, u32[]{:S(2)}) %collective-permute-start.22) | collective-permute-done | bytes 45088 | tf_op jit(solution)/shard_map/ppermute | solution.py:366
  97.6 1.7 %shard_map.117 = (f32[20,2048]{1,0:T(8,128)}, f32[20,2048]{1,0:T(8,128)}, bf16[20,16,128]{2,1,0:T(8,128)(2,1)S(1)}) custom-call(s32[192]{0:T(256)S(1)} %get-tuple-element.41.table, bf16[20,16,128]{2,1,0:T(8,128)(2,1)S(1)} %get-tuple-element.48.mine, bf16[11,16,128]{2,1,0:T(8,128)(2,1)S(1)} %get-tuple-element.62.rest_0_, ...), custom_call_target="tpu_custom_call" | custom-call | tf_op jit(solution)/shard_map/pallas_call | solution.py:33
  99.3 1.8 %collective-permute-start.31 = (bf16[20,16,128]{2,1,0:T(8,128)(2,1)S(1)}, bf16[20,16,128]{2,1,0:T(8,128)(2,1)S(1)}, u32[]{:S(2)}, u32[]{:S(2)}) collective-permute-start(bf16[20,16,128]{2,1,0:T(8,128)(2,1)S(1)} %get-tuple-element.74.rest_0_), channel_id=1, source_target_pairs={{0,24},{4,28},{8,16},{12,20},{16,8},{20,12},{24,0},{28,4},{1,25},{... | collective-permute-start | bytes 245768 | tf_op jit(solution)/shard_map/ppermute | solution.py:362
  101.0 1.2 %collective-permute-start.29 = (bf16[20,16,128]{2,1,0:T(8,128)(2,1)S(1)}, bf16[20,16,128]{2,1,0:T(8,128)(2,1)S(1)}, u32[]{:S(2)}, u32[]{:S(2)}) collective-permute-start(bf16[20,16,128]{2,1,0:T(8,128)(2,1)S(1)} %get-tuple-element.74.rest_0_), channel_id=1, source_target_pairs={{0,16},{4,20},{8,24},{12,28},{16,0},{20,4},{24,8},{28,12},{1,17},{... | collective-permute-start | bytes 245768 | tf_op jit(solution)/shard_map/ppermute | solution.py:362
  102.2 0.5 collective-permute-start.27
  102.8 1.8 %collective-permute-done.31.rest_6_ = bf16[20,16,128]{2,1,0:T(8,128)(2,1)S(1)} collective-permute-done((bf16[20,16,128]{2,1,0:T(8,128)(2,1)S(1)}, bf16[20,16,128]{2,1,0:T(8,128)(2,1)S(1)}, u32[]{:S(2)}, u32[]{:S(2)}) %collective-permute-start.31) | collective-permute-done | bytes 81952 | tf_op jit(solution)/shard_map/ppermute | solution.py:362
  104.6 0.9 collective-permute-done.29.rest_4_
  105.5 1.2 %collective-permute-done.27.rest_2_ = bf16[20,16,128]{2,1,0:T(8,128)(2,1)S(1)} collective-permute-done((bf16[20,16,128]{2,1,0:T(8,128)(2,1)S(1)}, bf16[20,16,128]{2,1,0:T(8,128)(2,1)S(1)}, u32[]{:S(2)}, u32[]{:S(2)}) %collective-permute-start.27) | collective-permute-done | bytes 81952 | tf_op jit(solution)/shard_map/ppermute | solution.py:362
  106.7 0.9 shard_map.113
  107.6 0.4 collective-permute-done.28.rest_3_
  108.0 1.5 %shard_map.118 = bf16[20,128,128]{2,1,0:T(8,128)(2,1)} custom-call(s32[2]{0:T(128)S(1)} %pad_add_fusion.here, bf16[20,16,128]{2,1,0:T(8,128)(2,1)S(1)} %get-tuple-element.74.rest_0_, bf16[20,16,128]{2,1,0:T(8,128)(2,1)S(1)} %collective-permute-done.26.rest_1_, bf16[20,16,128]{2,1,0:T(8,128)(2,1)S(1)} %collective-permute-done.27.rest_2_, ...), custom_call_target="tpu_custom_call" | custom-call | tf_op jit(solution)/shard_map/pallas_call | solution.py:33
  (27 shorter events, 0.1 us)
Async XLA Ops:
  0.6 1.2 %copy-start = (bf16[28,128,128]{2,1,0:T(8,128)(2,1)S(1)}, bf16[28,128,128]{2,1,0:T(8,128)(2,1)}, u32[]{:S(2)}) copy-start(bf16[28,128,128]{2,1,0:T(8,128)(2,1)} %param.9) | copy-start | bytes 2752516
  0.6 30.5 %copy-start.2 = (bf16[128,2560]{1,0:T(8,128)(2,1)S(1)}, bf16[128,2560]{1,0:T(8,128)(2,1)}, u32[]{:S(2)}) copy-start(bf16[128,2560]{1,0:T(8,128)(2,1)} %cotangent.1) | copy-start | bytes 1966084
  1.8 16.5 %collective-permute-start.2 = (bf16[28,16,128]{2,1,0:T(8,128)(2,1)S(1)}, bf16[28,16,128]{2,1,0:T(8,128)(2,1)S(1)}, u32[]{:S(2)}, u32[]{:S(2)}) collective-permute-start(bf16[28,16,128]{2,1,0:T(8,128)(2,1)S(1)} %constant_dynamic-slice_fusion.rest_0_), channel_id=1, source_target_pairs={{0,3},{1,0},{2,1},{3,2},{4,7},{5,4},{6,5},{7,6},{8,11},{9,8},{10,9... | collective-permute-start | bytes 344072 | tf_op jit(solution)/shard_map/ppermute | solution.py:366
  7.0 11.4 %collective-permute-start.1 = (bf16[28,16,128]{2,1,0:T(8,128)(2,1)S(1)}, bf16[28,16,128]{2,1,0:T(8,128)(2,1)S(1)}, u32[]{:S(2)}, u32[]{:S(2)}) collective-permute-start(bf16[28,16,128]{2,1,0:T(8,128)(2,1)S(1)} %constant_dynamic-slice_fusion.rest_0_), channel_id=1, source_target_pairs={{0,2},{1,3},{2,0},{3,1},{4,6},{5,7},{6,4},{7,5},{8,10},{9,11},{10,... | collective-permute-start | bytes 344072 | tf_op jit(solution)/shard_map/ppermute | solution.py:366
  7.0 11.4 %collective-permute-start = (bf16[28,16,128]{2,1,0:T(8,128)(2,1)S(1)}, bf16[28,16,128]{2,1,0:T(8,128)(2,1)S(1)}, u32[]{:S(2)}, u32[]{:S(2)}) collective-permute-start(bf16[28,16,128]{2,1,0:T(8,128)(2,1)S(1)} %constant_dynamic-slice_fusion.rest_0_), channel_id=1, source_target_pairs={{0,1},{1,2},{2,3},{3,0},{4,5},{5,6},{6,7},{7,4},{8,9},{9,10},{10,1... | collective-permute-start | bytes 344072 | tf_op jit(solution)/shard_map/ppermute | solution.py:366
  8.1 0.9 copy-start.3
  9.0 0.9 copy-start.4
  10.0 0.7 copy-start.5
  10.6 0.7 copy-start.6
  19.2 7.9 %collective-permute-start.8 = (bf16[44,16,128]{2,1,0:T(8,128)(2,1)S(1)}, bf16[44,16,128]{2,1,0:T(8,128)(2,1)S(1)}, u32[]{:S(2)}, u32[]{:S(2)}) collective-permute-start(bf16[44,16,128]{2,1,0:T(8,128)(2,1)S(1)} %get-tuple-element.42.rest_0_), channel_id=1, source_target_pairs={{0,24},{4,28},{8,16},{12,20},{16,8},{20,12},{24,0},{28,4},{1,25},{... | collective-permute-start | bytes 540680 | tf_op jit(solution)/shard_map/ppermute | solution.py:362
  21.7 7.8 %collective-permute-start.6 = (bf16[44,16,128]{2,1,0:T(8,128)(2,1)S(1)}, bf16[44,16,128]{2,1,0:T(8,128)(2,1)S(1)}, u32[]{:S(2)}, u32[]{:S(2)}) collective-permute-start(bf16[44,16,128]{2,1,0:T(8,128)(2,1)S(1)} %get-tuple-element.42.rest_0_), channel_id=1, source_target_pairs={{0,16},{4,20},{8,24},{12,28},{16,0},{20,4},{24,8},{28,12},{1,17},{... | collective-permute-start | bytes 540680 | tf_op jit(solution)/shard_map/ppermute | solution.py:362
  22.3 7.3 %collective-permute-start.4 = (bf16[44,16,128]{2,1,0:T(8,128)(2,1)S(1)}, bf16[44,16,128]{2,1,0:T(8,128)(2,1)S(1)}, u32[]{:S(2)}, u32[]{:S(2)}) collective-permute-start(bf16[44,16,128]{2,1,0:T(8,128)(2,1)S(1)} %get-tuple-element.42.rest_0_), channel_id=1, source_target_pairs={{0,8},{4,12},{8,0},{12,4},{16,24},{20,28},{24,16},{28,20},{1,9},{5... | collective-permute-start | bytes 540680 | tf_op jit(solution)/shard_map/ppermute | solution.py:362
  22.8 7.2 %collective-permute-start.3 = (bf16[44,16,128]{2,1,0:T(8,128)(2,1)S(1)}, bf16[44,16,128]{2,1,0:T(8,128)(2,1)S(1)}, u32[]{:S(2)}, u32[]{:S(2)}) collective-permute-start(bf16[44,16,128]{2,1,0:T(8,128)(2,1)S(1)} %get-tuple-element.42.rest_0_), channel_id=1, source_target_pairs={{0,4},{4,0},{8,12},{12,8},{16,20},{20,16},{24,28},{28,24},{1,5},{5... | collective-permute-start | bytes 540680 | tf_op jit(solution)/shard_map/ppermute | solution.py:362
  27.2 2.9 %collective-permute-start.9 = (bf16[44,16,128]{2,1,0:T(8,128)(2,1)S(1)}, bf16[44,16,128]{2,1,0:T(8,128)(2,1)S(1)}, u32[]{:S(2)}, u32[]{:S(2)}) collective-permute-start(bf16[44,16,128]{2,1,0:T(8,128)(2,1)S(1)} %collective-permute-done.8.rest_6_), channel_id=1, source_target_pairs={{0,4},{4,0},{8,12},{12,8},{16,20},{20,16},{24,28},{28,24},{1,5},{5... | collective-permute-start | bytes 540680 | tf_op jit(solution)/shard_map/ppermute | solution.py:362
  29.5 1.4 %collective-permute-start.7 = (bf16[44,16,128]{2,1,0:T(8,128)(2,1)S(1)}, bf16[44,16,128]{2,1,0:T(8,128)(2,1)S(1)}, u32[]{:S(2)}, u32[]{:S(2)}) collective-permute-start(bf16[44,16,128]{2,1,0:T(8,128)(2,1)S(1)} %collective-permute-done.6.rest_4_), channel_id=1, source_target_pairs={{0,4},{4,0},{8,12},{12,8},{16,20},{20,16},{24,28},{28,24},{1,5},{5... | collective-permute-start | bytes 540680 | tf_op jit(solution)/shard_map/ppermute | solution.py:362
  29.6 1.6 %collective-permute-start.5 = (bf16[44,16,128]{2,1,0:T(8,128)(2,1)S(1)}, bf16[44,16,128]{2,1,0:T(8,128)(2,1)S(1)}, u32[]{:S(2)}, u32[]{:S(2)}) collective-permute-start(bf16[44,16,128]{2,1,0:T(8,128)(2,1)S(1)} %collective-permute-done.4.rest_2_), channel_id=1, source_target_pairs={{0,4},{4,0},{8,12},{12,8},{16,20},{20,16},{24,28},{28,24},{1,5},{5... | collective-permute-start | bytes 540680 | tf_op jit(solution)/shard_map/ppermute | solution.py:362
  31.2 1.3 %copy-start.1 = (bf16[128,5120]{1,0:T(8,128)(2,1)S(1)}, bf16[128,5120]{1,0:T(8,128)(2,1)}, u32[]{:S(2)}) copy-start(bf16[128,5120]{1,0:T(8,128)(2,1)} %tokens.3) | copy-start | bytes 3932164
  41.7 1.5 %collective-permute-start.13 = (bf16[44,16,128]{2,1,0:T(8,128)(2,1)S(1)}, bf16[44,16,128]{2,1,0:T(8,128)(2,1)S(1)}, u32[]{:S(2)}, u32[]{:S(2)}) collective-permute-start(bf16[44,16,128]{2,1,0:T(8,128)(2,1)S(1)} %get-tuple-element.54), channel_id=1, source_target_pairs={{0,4},{4,0},{8,12},{12,8},{16,20},{20,16},{24,28},{28,24},{1,5},{5... | collective-permute-start | bytes 540680 | tf_op jit(solution)/shard_map/ppermute | solution.py:362
  42.0 1.4 %collective-permute-start.14 = (bf16[44,16,128]{2,1,0:T(8,128)(2,1)S(1)}, bf16[44,16,128]{2,1,0:T(8,128)(2,1)S(1)}, u32[]{:S(2)}, u32[]{:S(2)}) collective-permute-start(bf16[44,16,128]{2,1,0:T(8,128)(2,1)S(1)} %get-tuple-element.55), channel_id=1, source_target_pairs={{0,4},{4,0},{8,12},{12,8},{16,20},{20,16},{24,28},{28,24},{1,5},{5... | collective-permute-start | bytes 540680 | tf_op jit(solution)/shard_map/ppermute | solution.py:362
  42.2 1.4 %collective-permute-start.15 = (bf16[44,16,128]{2,1,0:T(8,128)(2,1)S(1)}, bf16[44,16,128]{2,1,0:T(8,128)(2,1)S(1)}, u32[]{:S(2)}, u32[]{:S(2)}) collective-permute-start(bf16[44,16,128]{2,1,0:T(8,128)(2,1)S(1)} %get-tuple-element.56), channel_id=1, source_target_pairs={{0,4},{4,0},{8,12},{12,8},{16,20},{20,16},{24,28},{28,24},{1,5},{5... | collective-permute-start | bytes 540680 | tf_op jit(solution)/shard_map/ppermute | solution.py:362
  42.5 1.4 %collective-permute-start.16 = (bf16[44,16,128]{2,1,0:T(8,128)(2,1)S(1)}, bf16[44,16,128]{2,1,0:T(8,128)(2,1)S(1)}, u32[]{:S(2)}, u32[]{:S(2)}) collective-permute-start(bf16[44,16,128]{2,1,0:T(8,128)(2,1)S(1)} %get-tuple-element.57), channel_id=1, source_target_pairs={{0,4},{4,0},{8,12},{12,8},{16,20},{20,16},{24,28},{28,24},{1,5},{5... | collective-permute-start | bytes 540680 | tf_op jit(solution)/shard_map/ppermute | solution.py:362
  44.1 9.3 %collective-permute-start.17 = (bf16[44,16,128]{2,1,0:T(8,128)(2,1)S(1)}, bf16[44,16,128]{2,1,0:T(8,128)(2,1)S(1)}, u32[]{:S(2)}, u32[]{:S(2)}) collective-permute-start(bf16[44,16,128]{2,1,0:T(8,128)(2,1)S(1)} %get-tuple-element.59), channel_id=1, source_target_pairs={{0,8},{4,12},{8,0},{12,4},{16,24},{20,28},{24,16},{28,20},{1,9},{5... | collective-permute-start | bytes 540680 | tf_op jit(solution)/shard_map/ppermute | solution.py:362
  45.6 7.2 %collective-permute-start.23 = (f32[2,8,2048]{2,1,0:T(8,128)S(1)}, f32[2,8,2048]{2,1,0:T(8,128)S(1)}, u32[]{:S(2)}, u32[]{:S(2)}) collective-permute-start(f32[2,8,2048]{2,1,0:T(8,128)S(1)} %get-tuple-element.71), channel_id=1, source_target_pairs={{0,1},{1,2},{2,3},{3,0},{4,5},{5,6},{6,7},{7,4},{8,9},{9,10},{10,1... | collective-permute-start | bytes 393224 | tf_op jit(solution)/shard_map/ppermute | solution.py:366
  48.1 10.0 %collective-permute-start.18 = (bf16[44,16,128]{2,1,0:T(8,128)(2,1)S(1)}, bf16[44,16,128]{2,1,0:T(8,128)(2,1)S(1)}, u32[]{:S(2)}, u32[]{:S(2)}) collective-permute-start(bf16[44,16,128]{2,1,0:T(8,128)(2,1)S(1)} %get-tuple-element.60), channel_id=1, source_target_pairs={{0,16},{4,20},{8,24},{12,28},{16,0},{20,4},{24,8},{28,12},{1,17},{... | collective-permute-start | bytes 540680 | tf_op jit(solution)/shard_map/ppermute | solution.py:362
  48.9 10.6 %collective-permute-start.19 = (bf16[44,16,128]{2,1,0:T(8,128)(2,1)S(1)}, bf16[44,16,128]{2,1,0:T(8,128)(2,1)S(1)}, u32[]{:S(2)}, u32[]{:S(2)}) collective-permute-start(bf16[44,16,128]{2,1,0:T(8,128)(2,1)S(1)} %get-tuple-element.61), channel_id=1, source_target_pairs={{0,24},{4,28},{8,16},{12,20},{16,8},{20,12},{24,0},{28,4},{1,25},{... | collective-permute-start | bytes 540680 | tf_op jit(solution)/shard_map/ppermute | solution.py:362
  50.1 52.2 %collective-permute-start.10 = (bf16[128,1280]{1,0:T(8,128)(2,1)S(1)}, bf16[128,1280]{1,0:T(8,128)(2,1)S(1)}, u32[]{:S(2)}, u32[]{:S(2)}) collective-permute-start(bf16[128,1280]{1,0:T(8,128)(2,1)S(1)} %get-tuple-element.45), channel_id=1, source_target_pairs={{0,1},{1,2},{2,3},{3,0},{4,5},{5,6},{6,7},{7,4},{8,9},{9,10},{10,1... | collective-permute-start | bytes 983048 | tf_op jit(solution)/shard_map/ppermute | solution.py:366
  52.8 49.9 %collective-permute-start.11 = (bf16[128,1280]{1,0:T(8,128)(2,1)S(1)}, bf16[128,1280]{1,0:T(8,128)(2,1)S(1)}, u32[]{:S(2)}, u32[]{:S(2)}) collective-permute-start(bf16[128,1280]{1,0:T(8,128)(2,1)S(1)} %get-tuple-element.46), channel_id=1, source_target_pairs={{0,2},{1,3},{2,0},{3,1},{4,6},{5,7},{6,4},{7,5},{8,10},{9,11},{10,... | collective-permute-start | bytes 983048 | tf_op jit(solution)/shard_map/ppermute | solution.py:366
  53.4 27.1 %collective-permute-start.24 = (f32[2,8,2048]{2,1,0:T(8,128)S(1)}, f32[2,8,2048]{2,1,0:T(8,128)S(1)}, u32[]{:S(2)}, u32[]{:S(2)}) collective-permute-start(f32[2,8,2048]{2,1,0:T(8,128)S(1)} %get-tuple-element.72), channel_id=1, source_target_pairs={{0,2},{1,3},{2,0},{3,1},{4,6},{5,7},{6,4},{7,5},{8,10},{9,11},{10,... | collective-permute-start | bytes 393224 | tf_op jit(solution)/shard_map/ppermute | solution.py:366
  58.1 30.2 %collective-permute-start.25 = (f32[2,8,2048]{2,1,0:T(8,128)S(1)}, f32[2,8,2048]{2,1,0:T(8,128)S(1)}, u32[]{:S(2)}, u32[]{:S(2)}) collective-permute-start(f32[2,8,2048]{2,1,0:T(8,128)S(1)} %get-tuple-element.73), channel_id=1, source_target_pairs={{0,3},{1,0},{2,1},{3,2},{4,7},{5,4},{6,5},{7,6},{8,11},{9,8},{10,9... | collective-permute-start | bytes 393224 | tf_op jit(solution)/shard_map/ppermute | solution.py:366
  59.5 47.2 %collective-permute-start.12 = (bf16[128,1280]{1,0:T(8,128)(2,1)S(1)}, bf16[128,1280]{1,0:T(8,128)(2,1)S(1)}, u32[]{:S(2)}, u32[]{:S(2)}) collective-permute-start(bf16[128,1280]{1,0:T(8,128)(2,1)S(1)} %get-tuple-element.47), channel_id=1, source_target_pairs={{0,3},{1,0},{2,1},{3,2},{4,7},{5,4},{6,5},{7,6},{8,11},{9,8},{10,9... | collective-permute-start | bytes 983048 | tf_op jit(solution)/shard_map/ppermute | solution.py:366
  80.4 13.1 %collective-permute-start.20 = (bf16[11,16,128]{2,1,0:T(8,128)(2,1)S(1)}, bf16[11,16,128]{2,1,0:T(8,128)(2,1)S(1)}, u32[]{:S(2)}, u32[]{:S(2)}) collective-permute-start(bf16[11,16,128]{2,1,0:T(8,128)(2,1)S(1)} %get-tuple-element.63), channel_id=1, source_target_pairs={{0,1},{1,2},{2,3},{3,0},{4,5},{5,6},{6,7},{7,4},{8,9},{9,10},{10,1... | collective-permute-start | bytes 135176 | tf_op jit(solution)/shard_map/ppermute | solution.py:366
  88.3 6.9 %collective-permute-start.21 = (bf16[11,16,128]{2,1,0:T(8,128)(2,1)S(1)}, bf16[11,16,128]{2,1,0:T(8,128)(2,1)S(1)}, u32[]{:S(2)}, u32[]{:S(2)}) collective-permute-start(bf16[11,16,128]{2,1,0:T(8,128)(2,1)S(1)} %get-tuple-element.64), channel_id=1, source_target_pairs={{0,2},{1,3},{2,0},{3,1},{4,6},{5,7},{6,4},{7,5},{8,10},{9,11},{10,... | collective-permute-start | bytes 135176 | tf_op jit(solution)/shard_map/ppermute | solution.py:366
  93.5 4.0 %collective-permute-start.22 = (bf16[11,16,128]{2,1,0:T(8,128)(2,1)S(1)}, bf16[11,16,128]{2,1,0:T(8,128)(2,1)S(1)}, u32[]{:S(2)}, u32[]{:S(2)}) collective-permute-start(bf16[11,16,128]{2,1,0:T(8,128)(2,1)S(1)} %get-tuple-element.65), channel_id=1, source_target_pairs={{0,3},{1,0},{2,1},{3,2},{4,7},{5,4},{6,5},{7,6},{8,11},{9,8},{10,9... | collective-permute-start | bytes 135176 | tf_op jit(solution)/shard_map/ppermute | solution.py:366
  99.3 5.3 %collective-permute-start.31 = (bf16[20,16,128]{2,1,0:T(8,128)(2,1)S(1)}, bf16[20,16,128]{2,1,0:T(8,128)(2,1)S(1)}, u32[]{:S(2)}, u32[]{:S(2)}) collective-permute-start(bf16[20,16,128]{2,1,0:T(8,128)(2,1)S(1)} %get-tuple-element.74.rest_0_), channel_id=1, source_target_pairs={{0,24},{4,28},{8,16},{12,20},{16,8},{20,12},{24,0},{28,4},{1,25},{... | collective-permute-start | bytes 245768 | tf_op jit(solution)/shard_map/ppermute | solution.py:362
  101.0 4.5 %collective-permute-start.29 = (bf16[20,16,128]{2,1,0:T(8,128)(2,1)S(1)}, bf16[20,16,128]{2,1,0:T(8,128)(2,1)S(1)}, u32[]{:S(2)}, u32[]{:S(2)}) collective-permute-start(bf16[20,16,128]{2,1,0:T(8,128)(2,1)S(1)} %get-tuple-element.74.rest_0_), channel_id=1, source_target_pairs={{0,16},{4,20},{8,24},{12,28},{16,0},{20,4},{24,8},{28,12},{1,17},{... | collective-permute-start | bytes 245768 | tf_op jit(solution)/shard_map/ppermute | solution.py:362
  102.2 4.4 %collective-permute-start.27 = (bf16[20,16,128]{2,1,0:T(8,128)(2,1)S(1)}, bf16[20,16,128]{2,1,0:T(8,128)(2,1)S(1)}, u32[]{:S(2)}, u32[]{:S(2)}) collective-permute-start(bf16[20,16,128]{2,1,0:T(8,128)(2,1)S(1)} %get-tuple-element.74.rest_0_), channel_id=1, source_target_pairs={{0,8},{4,12},{8,0},{12,4},{16,24},{20,28},{24,16},{28,20},{1,9},{5... | collective-permute-start | bytes 245768 | tf_op jit(solution)/shard_map/ppermute | solution.py:362
  102.8 4.8 %collective-permute-start.26 = (bf16[20,16,128]{2,1,0:T(8,128)(2,1)S(1)}, bf16[20,16,128]{2,1,0:T(8,128)(2,1)S(1)}, u32[]{:S(2)}, u32[]{:S(2)}) collective-permute-start(bf16[20,16,128]{2,1,0:T(8,128)(2,1)S(1)} %get-tuple-element.74.rest_0_), channel_id=1, source_target_pairs={{0,4},{4,0},{8,12},{12,8},{16,20},{20,16},{24,28},{28,24},{1,5},{5... | collective-permute-start | bytes 245768 | tf_op jit(solution)/shard_map/ppermute | solution.py:362
  104.6 3.0 %collective-permute-start.32 = (bf16[20,16,128]{2,1,0:T(8,128)(2,1)S(1)}, bf16[20,16,128]{2,1,0:T(8,128)(2,1)S(1)}, u32[]{:S(2)}, u32[]{:S(2)}) collective-permute-start(bf16[20,16,128]{2,1,0:T(8,128)(2,1)S(1)} %collective-permute-done.31.rest_6_), channel_id=1, source_target_pairs={{0,4},{4,0},{8,12},{12,8},{16,20},{20,16},{24,28},{28,24},{1,5},{5... | collective-permute-start | bytes 245768 | tf_op jit(solution)/shard_map/ppermute | solution.py:362
  105.5 2.1 %collective-permute-start.30 = (bf16[20,16,128]{2,1,0:T(8,128)(2,1)S(1)}, bf16[20,16,128]{2,1,0:T(8,128)(2,1)S(1)}, u32[]{:S(2)}, u32[]{:S(2)}) collective-permute-start(bf16[20,16,128]{2,1,0:T(8,128)(2,1)S(1)} %collective-permute-done.29.rest_4_), channel_id=1, source_target_pairs={{0,4},{4,0},{8,12},{12,8},{16,20},{20,16},{24,28},{28,24},{1,5},{5... | collective-permute-start | bytes 245768 | tf_op jit(solution)/shard_map/ppermute | solution.py:362
  106.7 1.3 %collective-permute-start.28 = (bf16[20,16,128]{2,1,0:T(8,128)(2,1)S(1)}, bf16[20,16,128]{2,1,0:T(8,128)(2,1)S(1)}, u32[]{:S(2)}, u32[]{:S(2)}) collective-permute-start(bf16[20,16,128]{2,1,0:T(8,128)(2,1)S(1)} %collective-permute-done.27.rest_2_), channel_id=1, source_target_pairs={{0,4},{4,0},{8,12},{12,8},{16,20},{20,16},{24,28},{28,24},{1,5},{5... | collective-permute-start | bytes 245768 | tf_op jit(solution)/shard_map/ppermute | solution.py:362

commit v2 on v1

--- a/solution.py
+++ b/solution.py
@@ -20,6 +20,11 @@
 
 VMEM = pl.BlockSpec(memory_space=pltpu.VMEM)
 SMEM = pl.BlockSpec(memory_space=pltpu.SMEM)
+ANY = pl.BlockSpec(memory_space=pl.ANY)
+
+
+def in_hbm(value):
+    return pltpu.with_memory_space_constraint(value, pltpu.HBM)
 
 
 def size_of(item):
@@ -29,7 +34,8 @@
 def call(kernel, out_shape, in_specs, out_specs, scratch):
     def run(*args):
         outs = out_shape if isinstance(out_shape, list) else [out_shape]
-        room = sum(size_of(x) for x in (*args, *outs)) + sum(size_of(x) for x in scratch)
+        held = [x for x in scratch if hasattr(x, "shape") and x.dtype in (jnp.int32, jnp.bfloat16, jnp.float32)]
+        room = sum(size_of(x) for x in (*args, *outs, *held))
         return pl.pallas_call(
             kernel,
             out_shape=out_shape,
@@ -46,8 +52,33 @@
     return jax.ShapeDtypeStruct(dims, dtype)
 
 
-def wrap(value, count):
-    return jnp.where(value < 0, value + count, value)
+def paired(n):
+    return n & (n - 1) == 0
+
+
+def rel_to(me, other, n):
+    if paired(n):
+        return me ^ other
+    rel = other - me
+    return jnp.where(rel < 0, rel + n, rel)
+
+
+def rel_from(me, other, n):
+    if paired(n):
+        return me ^ other
+    rel = me - other
+    return jnp.where(rel < 0, rel + n, rel)
+
+
+def target_of(me, step, n):
+    if paired(n):
+        return me ^ step
+    other = me + step
+    return jnp.where(other >= n, other - n, other)
+
+
+def target_of_static(i, step, n):
+    return i ^ step if paired(n) else (i + step) % n
 
 
 def which_group(value, group, count):
@@ -57,13 +88,23 @@
     return found
 
 
-def plan_kernel(cfg, here, coords, moved, first, second, *rest):
+def take_rank(counts, at, live):
+    rank = jnp.int32(0)
+    new = []
+    for i, count in enumerate(counts):
+        hit = jnp.where(jnp.logical_and(live, at == i), 1, 0)
+        rank = rank + hit * count
+        new.append(count + hit)
+    return rank, tuple(new)
+
+
+def plan_kernel(cfg, here, coords, moved, table, src):
     n, per, cap, ms, bs, bw, pad = cfg
-    table = rest[0]
-    packs = rest[1 : 1 + n]
-    src, out_slot, counts = rest[1 + n :]
     total = n * per
     slots = n * bs
+    share, grad, moment = 3 * slots, 3 * slots + per, 3 * slots + 2 * per
+    out = moment + per
+    spare = out + n * ms
     me = here[0]
 
     def fill(ref, base, size, value):
@@ -71,76 +112,77 @@
             ref[base + i] = jnp.int32(value)
             return 0
 
-        lax.fori_loop(0, size, put, 0)
+        lax.fori_loop(0, size, put, 0, unroll=math.gcd(size, 4))
 
     fill(src, 0, total, -1)
-    fill(out_slot, 0, n * ms, 0)
     fill(table, 0, slots, -1)
     fill(table, slots, 2 * slots, 0)
-    fill(table, 3 * slots, 3 * per, -1)
+    fill(table, moment, per, -1)
+    fill(table, out, n * ms, 0)
+    zeros = (jnp.int32(0),) * n
 
     for p in range(n):
-        for i in range(n):
-            counts[i] = jnp.int32(0)
-        rel = wrap(me - p, n)
-
-        def old_slot(j, _):
-            o = p * cap + j
-            t = moved[o]
-
-            @pl.when(t >= 0)
-            def _():
-                dest = which_group(t, per, n)
-                src[t] = rel * cap + j
-                k = counts[dest]
-                counts[dest] = k + 1
-
-                @pl.when(me == p)
-                def _():
-                    out_slot[wrap(dest - me, n) * ms + k] = j
-
-                @pl.when(dest == me)
-                def _():
-                    table[3 * slots + 2 * per + t - me * per] = rel * pad + k
-
-            return 0
-
-        lax.fori_loop(0, cap, old_slot, 0)
+        rel = rel_from(me, p, n)
+
+        def old_slot(j, counts):
+            t = moved[p * cap + j]
+            live = t >= 0
+            dest = which_group(t, per, n)
+            k, counts = take_rank(counts, dest, live)
+            src[jnp.where(live, t, total)] = rel * cap + j
+            gone = jnp.logical_and(live, me == p)
+            table[jnp.where(gone, out + rel_to(me, dest, n) * ms + k, spare)] = j
+            came = jnp.logical_and(live, dest == me)
+            table[jnp.where(came, moment + t - me * per, spare)] = rel * pad + k
+            return counts
+
+        lax.fori_loop(0, cap, old_slot, zeros, unroll=math.gcd(cap, 4))
 
     for w in range(n):
-        for i in range(n):
-            counts[i] = jnp.int32(0)
-
-        def new_slot(j, _):
+
+        def new_slot(j, counts):
             b = w * per + j
+            row = coords[0, b]
             col = coords[1, b]
+            source = src[b]
             band = which_group(col, bw, n)
-            k = counts[band]
-            counts[band] = k + 1
-
-            @pl.when(band == me)
-            def _():
-                q = w * bs + k
-                table[q] = src[b]
-                table[slots + q] = coords[0, b]
-                table[2 * slots + q] = col - me * bw
-
-            @pl.when(me == w)
-            def _():
-                table[3 * slots + j] = src[b]
-                table[3 * slots + per + j] = wrap(me - band, n) * bs + k
-
-            return 0
-
-        lax.fori_loop(0, per, new_slot, 0)
-
+            k, counts = take_rank(counts, band, True)
+            q = w * bs + k
+            near = band == me
+            table[jnp.where(near, q, spare)] = source
+            table[jnp.where(near, slots + q, spare)] = row
+            table[jnp.where(near, 2 * slots + q, spare)] = col - me * bw
+            own = me == w
+            table[jnp.where(own, share + j, spare)] = source
+            table[jnp.where(own, grad + j, spare)] = rel_from(me, band, n) * bs + k
+            return counts
+
+        lax.fori_loop(0, per, new_slot, zeros, unroll=math.gcd(per, 4))
+
+
+def pack_kernel(cfg, table, first, second, tokens, cotangent, *rest):
+    n, ms, pad, out = cfg
+    packs = rest[:n]
+    tokens_out, cotangent_out, first_in, second_in, sems = rest[n:]
+    copies = [
+        pltpu.make_async_copy(first, first_in, sems.at[0]),
+        pltpu.make_async_copy(second, second_in, sems.at[1]),
+        pltpu.make_async_copy(tokens, tokens_out, sems.at[2]),
+        pltpu.make_async_copy(cotangent, cotangent_out, sems.at[3]),
+    ]
+    for copy in copies:
+        copy.start()
+    copies[0].wait()
+    copies[1].wait()
     for s in range(n):
         for k in range(ms):
-            row = out_slot[s * ms + k]
-            packs[s][0, k : k + 1, :] = first[pl.ds(row, 1), :]
-            packs[s][1, k : k + 1, :] = second[pl.ds(row, 1), :]
+            row = table[out + s * ms + k]
+            packs[s][0, k : k + 1, :] = first_in[pl.ds(row, 1), :]
+            packs[s][1, k : k + 1, :] = second_in[pl.ds(row, 1), :]
         if pad > ms:
             packs[s][:, ms:pad, :] = jnp.zeros((2, pad - ms, first.shape[1]), jnp.float32)
+    copies[2].wait()
+    copies[3].wait()
 
 
 def select_kernel(cfg, table, *rest):
@@ -171,7 +213,7 @@
     activated, slopes = rest[:2]
     far = rest[2 : 1 + n]
     own = rest[1 + n]
-    weights, products, hidden, backs, grads = rest[2 + n :]
+    weights, hidden, grads = rest[2 + n :]
     slots = n * bs
     me = here[0]
     if parts == 1:
@@ -185,66 +227,57 @@
     def col_at(index):
         return pl.ds(pl.multiple_of(index * blk, blk), blk)
 
+    hidden[...] = jnp.zeros_like(hidden)
+
     def product(w, _):
         for k in range(bs):
             q = w * bs + k
-            products[q] = jnp.dot(
+            term = jnp.dot(
                 tokens[:, col_at(table[slots + q])],
                 weights[q],
                 preferred_element_type=jnp.float32,
             ).astype(jnp.bfloat16)
+            at = col_at(table[2 * slots + q])
+            hidden[:, at] = hidden[:, at] + term.astype(jnp.float32)
         return 0
 
     lax.fori_loop(0, n, product, 0)
-    hidden[...] = jnp.zeros_like(hidden)
-
-    def gather_hidden(q, _):
-        at = col_at(table[2 * slots + q])
-        hidden[:, at] = hidden[:, at] + products[q].astype(jnp.float32)
-        return 0
-
-    lax.fori_loop(0, slots, gather_hidden, 0)
 
     def pointwise(c, _):
         at = col_at(c)
         v = hidden[:, at]
         square = v * v
-        t = jnp.tanh(SQRT_2_OVER_PI * (v + 0.044715 * (square * v)))
-        half = 0.5 * (1.0 + t)
-        activated[:, at] = (v * half).astype(jnp.bfloat16)
-        slope = half + 0.5 * v * ((1.0 - t) * (1.0 + t)) * (
-            SQRT_2_OVER_PI * (1.0 + (3.0 * 0.044715) * square)
+        t = jnp.tanh(v * (SQRT_2_OVER_PI + (SQRT_2_OVER_PI * 0.044715) * square))
+        half = 0.5 + 0.5 * t
+        value = v * half
+        activated[:, at] = value.astype(jnp.bfloat16)
+        slope = half + value * (1.0 - half) * (
+            2.0 * SQRT_2_OVER_PI + (6.0 * 0.044715 * SQRT_2_OVER_PI) * square
         )
         slopes[:, at] = (cotangent[:, at].astype(jnp.float32) * slope).astype(jnp.bfloat16)
         return 0
 
     lax.fori_loop(0, bw, pointwise, 0)
+    grads[...] = jnp.zeros_like(grads)
 
     def back(w, _):
         for k in range(bs):
             q = w * bs + k
-            backs[q] = lax.dot_general(
+            term = lax.dot_general(
                 slopes[:, col_at(table[2 * slots + q])],
                 weights[q],
                 (((1,), (1,)), ((), ())),
                 preferred_element_type=jnp.float32,
             )
+            at = col_at(table[slots + q])
+            grads[:, at] = grads[:, at] + term
         return 0
 
     lax.fori_loop(0, n, back, 0)
-    grads[...] = jnp.zeros_like(grads)
-
-    def gather_back(q, _):
-        at = col_at(table[slots + q])
-        grads[:, at] = grads[:, at] + backs[q]
-        return 0
-
-    lax.fori_loop(0, slots, gather_back, 0)
     width = own.shape[1]
 
     def band_of(s):
-        band = me + s
-        band = jnp.where(band >= n, band - n, band)
+        band = target_of(me, s, n)
         return grads[:, pl.ds(pl.multiple_of(band * width, blk), width)]
 
     own[...] = band_of(0)
@@ -299,8 +332,7 @@
         total = total + term[...].astype(jnp.float32)
     pool[...] = total.astype(jnp.bfloat16)
     for s in range(n):
-        band = me + s
-        band = jnp.where(band >= n, band - n, band)
+        band = target_of(me, s, n)
         outs[s][...] = pool[pl.ds(band * bs, bs)]
 
 
@@ -363,7 +395,7 @@
 
 
 def shift(value, step, n):
-    return lax.ppermute(value, "mp", [(i, (i + step) % n) for i in range(n)])
+    return lax.ppermute(value, "mp", [(i, target_of_static(i, step, n)) for i in range(n)])
 
 
 def plane_gather(value, parts):
@@ -398,18 +430,14 @@
     share = lax.dynamic_slice_in_dim(old_weights, d * rows, rows, 1)
     shares = [share] + [shift(share, s, n) for s in range(1, n)]
 
-    plan = call(
+    out = 3 * slots + 3 * per
+    table = call(
         functools.partial(plan_kernel, (n, per, cap, ms, bs, bw, pad)),
-        [shape((3 * slots + 3 * per,), jnp.int32)] + [shape((2, pad, shard), f32)] * n,
-        [SMEM, SMEM, SMEM, VMEM, VMEM],
-        [SMEM] + [VMEM] * n,
-        [
-            pltpu.SMEM((total,), jnp.int32),
-            pltpu.SMEM((n * ms,), jnp.int32),
-            pltpu.SMEM((n,), jnp.int32),
-        ],
-    )(here, new_coords.T, moved_to, old_first, old_second)
-    table, packs = plan[0], plan[1:]
+        shape((out + n * ms + 4,), jnp.int32),
+        [SMEM] * 3,
+        SMEM,
+        [pltpu.SMEM((total + 8,), jnp.int32)],
+    )(here, in_hbm(new_coords.T), in_hbm(moved_to))
 
     picked, mine = call(
         functools.partial(select_kernel, (n, per, cap, bs)),
@@ -425,7 +453,20 @@
         gathered = lax.all_gather(picked, "dp", axis=0)
         pieces = [gathered.transpose(1, 0, 2, 3).reshape(slots, blk, blk)]
 
-    packs = list(lax.optimization_barrier(tuple(packs) + (picked,)))[:n]
+    packed = call(
+        functools.partial(pack_kernel, (n, ms, pad, out)),
+        [shape((2, pad, shard), f32)] * n
+        + [shape(tokens_in.shape, bf16), shape(cotangent.shape, bf16)],
+        [SMEM] + [ANY] * 4,
+        [VMEM] * (n + 2),
+        [
+            pltpu.VMEM(old_first.shape, f32),
+            pltpu.VMEM(old_second.shape, f32),
+            pltpu.SemaphoreType.DMA((4,)),
+        ],
+    )(table, *[in_hbm(x) for x in (old_first, old_second, tokens_in, cotangent)])
+    packs = packed[:n]
+    tokens, cotangents = packed[n:]
     moments = [packs[0]] + [shift(packs[s], s, n) for s in range(1, n)]
 
     results = call(
@@ -437,12 +478,10 @@
         [VMEM] * (n + 2),
         [
             pltpu.VMEM((slots, blk, blk), bf16),
-            pltpu.VMEM((slots, tok, blk), bf16),
             pltpu.VMEM((tok, bw * blk), f32),
-            pltpu.VMEM((slots, tok, blk), f32),
             pltpu.VMEM((tok, width), f32),
         ],
-    )(here, table, tokens_in, cotangent, *pieces)
+    )(here, table, tokens, cotangents, *pieces)
     activated, slopes = results[:2]
     far, own = results[2 : 1 + n], results[1 + n]
     back_terms = [shift(far[s - 1], s, n) for s in range(1, n)]
@@ -454,7 +493,7 @@
         [SMEM, SMEM, VMEM, VMEM],
         [VMEM] * count,
         [pltpu.VMEM((slots, blk, blk), bf16)],
-    )(here, table, tokens_in, slopes)
+    )(here, table, tokens, slopes)
 
     if direct:
         half = parts // 2

time: 110 us -> 105 us (0.955)
  waiting for transfers between devices: 41.4 us -> 47.3 us
  starting transfers between devices: 39.5 us -> 33.9 us
  local copies, waits for them, and re-layouts: 5.73 us -> 1.19 us
    ppermute x12, waiting for transfers between devices: 25.7 us -> 35.4 us  [shift(): lax.ppermute(value, 'mp', [(i, target_of_static(i, step, n)) for i in ran...]
    ppermute x12, starting transfers between devices: 27.3 us -> 21.3 us  [shift(): lax.ppermute(value, 'mp', [(i, target_of_static(i, step, n)) for i in ran...]
    unnamed x14 -> x2, local copies, waits for them, and re-layouts: 5.71 us -> 1.17 us
    ppermute x21, waiting for transfers between devices: 15.7 us -> 11.9 us  [swap(): return lax.ppermute(value, 'dp', [(i, i ^ bits) for i in range(parts)])]
    pallas_call x9 -> x10, Pallas kernels: 21.9 us -> 21.3 us  [run(): pl.pallas_call(kernel, out_shape=out_shape, in_specs=in_specs, out_specs=...]
  transfers between devices with their start and end apart: 33 -> 33, of which waited for: 18 -> 15; matrix products, arithmetic and copies ran while one was open for 0% -> 0% of each run, Pallas kernels for 9% -> 11%
where the time goes in v2:
time: 105 us; the launch traced here: 104 us
  waiting for transfers between devices  47.3 us (45%)
  starting transfers between devices  33.9 us (32%)
  Pallas kernels  21.3 us (20%)
  local copies, waits for them, and re-layouts  1.19 us (1%)
    ppermute x12, waiting for transfers between devices, shift(): lax.ppermute(value, 'mp', [(i, target_of_static(i, step, n)) for i in ran...  35.4 us
    pallas_call x10, Pallas kernels, run(): pl.pallas_call(kernel, out_shape=out_shape, in_specs=in_specs, out_specs=...  21.3 us
    ppermute x12, starting transfers between devices, shift(): lax.ppermute(value, 'mp', [(i, target_of_static(i, step, n)) for i in ran...  21.3 us
    ppermute x21, starting transfers between devices, swap(): return lax.ppermute(value, 'dp', [(i, i ^ bits) for i in range(parts)])  12.6 us
    ppermute x21, waiting for transfers between devices, swap(): return lax.ppermute(value, 'dp', [(i, i ^ bits) for i in range(parts)])  11.9 us
  transfers between devices with their start and end apart: 33, of which 15 were waited for; matrix products, arithmetic and copies ran while one was open for 0% of the time, Pallas kernels for 11%

profile of v2, /device:TPU:0, one launch (start us, length us, event | category | flops | bytes accessed | tf_op | source)
XLA Modules:
  0.0 104.5 jit_solution(867400734585715422)
XLA Ops:
  0.6 0.0 copy-start
  0.7 1.2 %copy-done = bf16[28,128,128]{2,1,0:T(8,128)(2,1)S(1)} copy-done((bf16[28,128,128]{2,1,0:T(8,128)(2,1)S(1)}, bf16[28,128,128]{2,1,0:T(8,128)(2,1)}, u32[]{:S(2)}) %copy-start) | copy-done | bytes 917528
  1.8 5.1 %collective-permute-start.2 = (bf16[28,16,128]{2,1,0:T(8,128)(2,1)S(1)}, bf16[28,16,128]{2,1,0:T(8,128)(2,1)S(1)}, u32[]{:S(2)}, u32[]{:S(2)}) collective-permute-start(bf16[28,16,128]{2,1,0:T(8,128)(2,1)S(1)} %constant_dynamic-slice_fusion.rest_0_), channel_id=1, source_target_pairs={{0,3},{1,2},{2,1},{3,0},{4,7},{5,6},{6,5},{7,4},{8,11},{9,10},{10,... | collective-permute-start | bytes 344072 | tf_op jit(solution)/shard_map/ppermute | solution.py:398
  7.0 0.0 collective-permute-start.1
  7.0 0.6 collective-permute-start
  7.6 0.1 pad_add_fusion.here
  7.7 5.6 %shard_map.110.table = s32[224]{0:T(256)S(1)} custom-call(s32[2]{0:T(128)S(1)} %pad_add_fusion.here, s32[2,80]{1,0:T(2,128)} %bitcast.3, s32[112]{0:T(128)} %moved.1), custom_call_target="tpu_custom_call" | custom-call | tf_op jit(solution)/shard_map/pallas_call | solution.py:39
  13.3 0.0 collective-permute-done.2.rest_3_
  13.3 3.3 %collective-permute-done.1.rest_2_ = bf16[28,16,128]{2,1,0:T(8,128)(2,1)S(1)} collective-permute-done((bf16[28,16,128]{2,1,0:T(8,128)(2,1)S(1)}, bf16[28,16,128]{2,1,0:T(8,128)(2,1)S(1)}, u32[]{:S(2)}, u32[]{:S(2)}) %collective-permute-start.1) | collective-permute-done | bytes 114720 | tf_op jit(solution)/shard_map/ppermute | solution.py:398
  16.6 0.0 collective-permute-done.rest_1_
  16.7 0.8 shard_map.112
  17.5 2.5 %collective-permute-start.8 = (bf16[44,16,128]{2,1,0:T(8,128)(2,1)S(1)}, bf16[44,16,128]{2,1,0:T(8,128)(2,1)S(1)}, u32[]{:S(2)}, u32[]{:S(2)}) collective-permute-start(bf16[44,16,128]{2,1,0:T(8,128)(2,1)S(1)} %get-tuple-element.40.rest_0_), channel_id=1, source_target_pairs={{0,24},{4,28},{8,16},{12,20},{16,8},{20,12},{24,0},{28,4},{1,25},{... | collective-permute-start | bytes 540680 | tf_op jit(solution)/shard_map/ppermute | solution.py:394
  20.0 0.5 collective-permute-start.6
  20.5 0.5 collective-permute-start.4
  21.0 0.0 collective-permute-start.3
  21.0 4.4 %collective-permute-done.8.rest_6_ = bf16[44,16,128]{2,1,0:T(8,128)(2,1)S(1)} collective-permute-done((bf16[44,16,128]{2,1,0:T(8,128)(2,1)S(1)}, bf16[44,16,128]{2,1,0:T(8,128)(2,1)S(1)}, u32[]{:S(2)}, u32[]{:S(2)}) %collective-permute-start.8) | collective-permute-done | bytes 180256 | tf_op jit(solution)/shard_map/ppermute | solution.py:394
  25.5 2.4 %collective-permute-done.6.rest_4_ = bf16[44,16,128]{2,1,0:T(8,128)(2,1)S(1)} collective-permute-done((bf16[44,16,128]{2,1,0:T(8,128)(2,1)S(1)}, bf16[44,16,128]{2,1,0:T(8,128)(2,1)S(1)}, u32[]{:S(2)}, u32[]{:S(2)}) %collective-permute-start.6) | collective-permute-done | bytes 180256 | tf_op jit(solution)/shard_map/ppermute | solution.py:394
  27.9 0.0 collective-permute-start.7
  27.9 0.1 collective-permute-done.4.rest_2_
  28.0 0.4 collective-permute-start.5
  28.4 2.2 %shard_map.111 = (f32[2,8,2048]{2,1,0:T(8,128)S(1)}, f32[2,8,2048]{2,1,0:T(8,128)S(1)}, f32[2,8,2048]{2,1,0:T(8,128)S(1)}, f32[2,8,2048]{2,1,0:T(8,128)S(1)}, bf...) custom-call(s32[224]{0:T(256)S(1)} %shard_map.110.table, f32[28,2048]{1,0:T(8,128)} %first.1, ...), custom_call_target="tpu_custom_call" | custom-call | tf_op jit(solution)/shard_map/pallas_call | solution.py:39
  30.7 0.0 collective-permute-done.7.rest_5_
  30.7 5.6 %shard_map.113 = (bf16[128,2560]{1,0:T(8,128)(2,1)}, bf16[128,2560]{1,0:T(8,128)(2,1)S(1)}, bf16[128,1280]{1,0:T(8,128)(2,1)S(1)}, bf16[128,1280]{1,0:T(8,128)(2...) custom-call(s32[2]{0:T(128)S(1)} %pad_add_fusion.here, s32[224]{0:T(256)S(1)} %shard_map.110.table, ...), custom_call_target="tpu_custom_call" | custom-call | tf_op jit(solution)/shard_map/pallas_call | solution.py:39
  36.4 2.1 %shard_map.115 = (bf16[44,16,128]{2,1,0:T(8,128)(2,1)S(1)}, bf16[44,16,128]{2,1,0:T(8,128)(2,1)S(1)}, bf16[44,16,128]{2,1,0:T(8,128)(2,1)S(1)}, bf16[44,16,128]{...) custom-call(s32[2]{0:T(128)S(1)} %pad_add_fusion.here, ...), custom_call_target="tpu_custom_call" | custom-call | tf_op jit(solution)/shard_map/pallas_call | solution.py:39
  38.5 0.2 collective-permute-start.13
  38.6 0.4 collective-permute-start.14
  39.0 0.1 collective-permute-start.15
  39.1 0.4 collective-permute-start.16
  39.6 0.4 collective-permute-done.13.refs_4_
  40.0 0.3 collective-permute-done.14.refs_5_
  40.2 0.3 collective-permute-done.15.refs_6_
  40.5 0.3 collective-permute-done.16.refs_7_
  40.7 0.2 shard_map.116
  40.9 1.6 %collective-permute-start.17 = (bf16[44,16,128]{2,1,0:T(8,128)(2,1)S(1)}, bf16[44,16,128]{2,1,0:T(8,128)(2,1)S(1)}, u32[]{:S(2)}, u32[]{:S(2)}) collective-permute-start(bf16[44,16,128]{2,1,0:T(8,128)(2,1)S(1)} %get-tuple-element.57), channel_id=1, source_target_pairs={{0,8},{4,12},{8,0},{12,4},{16,24},{20,28},{24,16},{28,20},{1,9},{5... | collective-permute-start | bytes 540680 | tf_op jit(solution)/shard_map/ppermute | solution.py:394
  42.5 0.0 collective-permute-start.23
  42.5 0.8 collective-permute-start.18
  43.3 1.2 %collective-permute-start.19 = (bf16[44,16,128]{2,1,0:T(8,128)(2,1)S(1)}, bf16[44,16,128]{2,1,0:T(8,128)(2,1)S(1)}, u32[]{:S(2)}, u32[]{:S(2)}) collective-permute-start(bf16[44,16,128]{2,1,0:T(8,128)(2,1)S(1)} %get-tuple-element.59), channel_id=1, source_target_pairs={{0,24},{4,28},{8,16},{12,20},{16,8},{20,12},{24,0},{28,4},{1,25},{... | collective-permute-start | bytes 540680 | tf_op jit(solution)/shard_map/ppermute | solution.py:394
  44.5 2.0 %collective-permute-start.10 = (bf16[128,1280]{1,0:T(8,128)(2,1)S(1)}, bf16[128,1280]{1,0:T(8,128)(2,1)S(1)}, u32[]{:S(2)}, u32[]{:S(2)}) collective-permute-start(bf16[128,1280]{1,0:T(8,128)(2,1)S(1)} %get-tuple-element.43), channel_id=1, source_target_pairs={{0,1},{1,0},{2,3},{3,2},{4,5},{5,4},{6,7},{7,6},{8,9},{9,8},{10,11... | collective-permute-start | bytes 983048 | tf_op jit(solution)/shard_map/ppermute | solution.py:398
  46.5 2.3 %collective-permute-done.23.rest_5_ = f32[2,8,2048]{2,1,0:T(8,128)S(1)} collective-permute-done((f32[2,8,2048]{2,1,0:T(8,128)S(1)}, f32[2,8,2048]{2,1,0:T(8,128)S(1)}, u32[]{:S(2)}, u32[]{:S(2)}) %collective-permute-start.23) | collective-permute-done | bytes 131104 | tf_op jit(solution)/shard_map/ppermute | solution.py:398
  48.8 0.4 collective-permute-start.11
  49.2 2.6 %collective-permute-start.24 = (f32[2,8,2048]{2,1,0:T(8,128)S(1)}, f32[2,8,2048]{2,1,0:T(8,128)S(1)}, u32[]{:S(2)}, u32[]{:S(2)}) collective-permute-start(f32[2,8,2048]{2,1,0:T(8,128)S(1)} %get-tuple-element.66), channel_id=1, source_target_pairs={{0,2},{1,3},{2,0},{3,1},{4,6},{5,7},{6,4},{7,5},{8,10},{9,11},{10,... | collective-permute-start | bytes 393224 | tf_op jit(solution)/shard_map/ppermute | solution.py:398
  51.8 1.0 collective-permute-done.18.rest_2_
  52.8 2.3 %collective-permute-start.25 = (f32[2,8,2048]{2,1,0:T(8,128)S(1)}, f32[2,8,2048]{2,1,0:T(8,128)S(1)}, u32[]{:S(2)}, u32[]{:S(2)}) collective-permute-start(f32[2,8,2048]{2,1,0:T(8,128)S(1)} %get-tuple-element.67), channel_id=1, source_target_pairs={{0,3},{1,2},{2,1},{3,0},{4,7},{5,6},{6,5},{7,4},{8,11},{9,10},{10,... | collective-permute-start | bytes 393224 | tf_op jit(solution)/shard_map/ppermute | solution.py:398
  55.0 1.5 %collective-permute-start.12 = (bf16[128,1280]{1,0:T(8,128)(2,1)S(1)}, bf16[128,1280]{1,0:T(8,128)(2,1)S(1)}, u32[]{:S(2)}, u32[]{:S(2)}) collective-permute-start(bf16[128,1280]{1,0:T(8,128)(2,1)S(1)} %get-tuple-element.45), channel_id=1, source_target_pairs={{0,3},{1,2},{2,1},{3,0},{4,7},{5,6},{6,5},{7,4},{8,11},{9,10},{10,... | collective-permute-start | bytes 983048 | tf_op jit(solution)/shard_map/ppermute | solution.py:398
  56.6 0.7 shard_map.117
  57.3 25.5 %collective-permute-done.24.rest_6_ = f32[2,8,2048]{2,1,0:T(8,128)S(1)} collective-permute-done((f32[2,8,2048]{2,1,0:T(8,128)S(1)}, f32[2,8,2048]{2,1,0:T(8,128)S(1)}, u32[]{:S(2)}, u32[]{:S(2)}) %collective-permute-start.24) | collective-permute-done | bytes 131104 | tf_op jit(solution)/shard_map/ppermute | solution.py:398
  82.8 0.0 collective-permute-done.25.rest_7_
  82.8 5.0 %collective-permute-start.21 = (bf16[11,16,128]{2,1,0:T(8,128)(2,1)S(1)}, bf16[11,16,128]{2,1,0:T(8,128)(2,1)S(1)}, u32[]{:S(2)}, u32[]{:S(2)}) collective-permute-start(bf16[11,16,128]{2,1,0:T(8,128)(2,1)S(1)} %get-tuple-element.62), channel_id=1, source_target_pairs={{0,2},{1,3},{2,0},{3,1},{4,6},{5,7},{6,4},{7,5},{8,10},{9,11},{10,... | collective-permute-start | bytes 135176 | tf_op jit(solution)/shard_map/ppermute | solution.py:398
  87.8 1.7 %collective-permute-start.22 = (bf16[11,16,128]{2,1,0:T(8,128)(2,1)S(1)}, bf16[11,16,128]{2,1,0:T(8,128)(2,1)S(1)}, u32[]{:S(2)}, u32[]{:S(2)}) collective-permute-start(bf16[11,16,128]{2,1,0:T(8,128)(2,1)S(1)} %get-tuple-element.63), channel_id=1, source_target_pairs={{0,3},{1,2},{2,1},{3,0},{4,7},{5,6},{6,5},{7,4},{8,11},{9,10},{10,... | collective-permute-start | bytes 135176 | tf_op jit(solution)/shard_map/ppermute | solution.py:398
  89.5 3.2 %collective-permute-done.21.rest_2_ = bf16[11,16,128]{2,1,0:T(8,128)(2,1)S(1)} collective-permute-done((bf16[11,16,128]{2,1,0:T(8,128)(2,1)S(1)}, bf16[11,16,128]{2,1,0:T(8,128)(2,1)S(1)}, u32[]{:S(2)}, u32[]{:S(2)}) %collective-permute-start.21) | collective-permute-done | bytes 45088 | tf_op jit(solution)/shard_map/ppermute | solution.py:398
  92.7 1.0 collective-permute-done.22.rest_3_
  93.7 1.7 %shard_map.118 = (f32[20,2048]{1,0:T(8,128)}, f32[20,2048]{1,0:T(8,128)}, bf16[20,16,128]{2,1,0:T(8,128)(2,1)S(1)}) custom-call(s32[224]{0:T(256)S(1)} %shard_map.110.table, bf16[20,16,128]{2,1,0:T(8,128)(2,1)S(1)} %get-tuple-element.46.mine, bf16[11,16,128]{2,1,0:T(8,128)(2,1)S(1)} %get-tuple-element.60.rest_0_, ...), custom_call_target="tpu_custom_call" | custom-call | tf_op jit(solution)/shard_map/pallas_call | solution.py:39
  95.4 1.5 %collective-permute-start.31 = (bf16[20,16,128]{2,1,0:T(8,128)(2,1)S(1)}, bf16[20,16,128]{2,1,0:T(8,128)(2,1)S(1)}, u32[]{:S(2)}, u32[]{:S(2)}) collective-permute-start(bf16[20,16,128]{2,1,0:T(8,128)(2,1)S(1)} %get-tuple-element.68.rest_0_), channel_id=1, source_target_pairs={{0,24},{4,28},{8,16},{12,20},{16,8},{20,12},{24,0},{28,4},{1,25},{... | collective-permute-start | bytes 245768 | tf_op jit(solution)/shard_map/ppermute | solution.py:394
  96.9 0.0 collective-permute-done.10.rest_0_
  96.9 1.9 %collective-permute-start.27 = (bf16[20,16,128]{2,1,0:T(8,128)(2,1)S(1)}, bf16[20,16,128]{2,1,0:T(8,128)(2,1)S(1)}, u32[]{:S(2)}, u32[]{:S(2)}) collective-permute-start(bf16[20,16,128]{2,1,0:T(8,128)(2,1)S(1)} %get-tuple-element.68.rest_0_), channel_id=1, source_target_pairs={{0,8},{4,12},{8,0},{12,4},{16,24},{20,28},{24,16},{28,20},{1,9},{5... | collective-permute-start | bytes 245768 | tf_op jit(solution)/shard_map/ppermute | solution.py:394
  98.9 0.0 collective-permute-done.11.rest_1_
  98.9 1.9 %collective-permute-done.31.rest_6_ = bf16[20,16,128]{2,1,0:T(8,128)(2,1)S(1)} collective-permute-done((bf16[20,16,128]{2,1,0:T(8,128)(2,1)S(1)}, bf16[20,16,128]{2,1,0:T(8,128)(2,1)S(1)}, u32[]{:S(2)}, u32[]{:S(2)}) %collective-permute-start.31) | collective-permute-done | bytes 81952 | tf_op jit(solution)/shard_map/ppermute | solution.py:394
  100.7 0.0 collective-permute-start.32
  100.7 0.9 collective-permute-done.29.rest_4_
  101.6 0.5 collective-permute-start.28
  102.1 0.9 shard_map.114
  103.0 0.0 collective-permute-done.30.rest_5_
  103.0 0.0 collective-permute-done.28.rest_3_
  103.0 1.5 %shard_map.119 = bf16[20,128,128]{2,1,0:T(8,128)(2,1)} custom-call(s32[2]{0:T(128)S(1)} %pad_add_fusion.here, bf16[20,16,128]{2,1,0:T(8,128)(2,1)S(1)} %get-tuple-element.68.rest_0_, bf16[20,16,128]{2,1,0:T(8,128)(2,1)S(1)} %collective-permute-done.26.rest_1_, bf16[20,16,128]{2,1,0:T(8,128)(2,1)S(1)} %collective-permute-done.27.rest_2_, ...), custom_call_target="tpu_custom_call" | custom-call | tf_op jit(solution)/shard_map/pallas_call | solution.py:39
  (16 shorter events, 0.1 us)
Async XLA Ops:
  0.6 1.2 %copy-start = (bf16[28,128,128]{2,1,0:T(8,128)(2,1)S(1)}, bf16[28,128,128]{2,1,0:T(8,128)(2,1)}, u32[]{:S(2)}) copy-start(bf16[28,128,128]{2,1,0:T(8,128)(2,1)} %param.9) | copy-start | bytes 2752516
  1.8 11.5 %collective-permute-start.2 = (bf16[28,16,128]{2,1,0:T(8,128)(2,1)S(1)}, bf16[28,16,128]{2,1,0:T(8,128)(2,1)S(1)}, u32[]{:S(2)}, u32[]{:S(2)}) collective-permute-start(bf16[28,16,128]{2,1,0:T(8,128)(2,1)S(1)} %constant_dynamic-slice_fusion.rest_0_), channel_id=1, source_target_pairs={{0,3},{1,2},{2,1},{3,0},{4,7},{5,6},{6,5},{7,4},{8,11},{9,10},{10,... | collective-permute-start | bytes 344072 | tf_op jit(solution)/shard_map/ppermute | solution.py:398
  7.0 9.7 %collective-permute-start.1 = (bf16[28,16,128]{2,1,0:T(8,128)(2,1)S(1)}, bf16[28,16,128]{2,1,0:T(8,128)(2,1)S(1)}, u32[]{:S(2)}, u32[]{:S(2)}) collective-permute-start(bf16[28,16,128]{2,1,0:T(8,128)(2,1)S(1)} %constant_dynamic-slice_fusion.rest_0_), channel_id=1, source_target_pairs={{0,2},{1,3},{2,0},{3,1},{4,6},{5,7},{6,4},{7,5},{8,10},{9,11},{10,... | collective-permute-start | bytes 344072 | tf_op jit(solution)/shard_map/ppermute | solution.py:398
  7.0 9.7 %collective-permute-start = (bf16[28,16,128]{2,1,0:T(8,128)(2,1)S(1)}, bf16[28,16,128]{2,1,0:T(8,128)(2,1)S(1)}, u32[]{:S(2)}, u32[]{:S(2)}) collective-permute-start(bf16[28,16,128]{2,1,0:T(8,128)(2,1)S(1)} %constant_dynamic-slice_fusion.rest_0_), channel_id=1, source_target_pairs={{0,1},{1,0},{2,3},{3,2},{4,5},{5,4},{6,7},{7,6},{8,9},{9,8},{10,11... | collective-permute-start | bytes 344072 | tf_op jit(solution)/shard_map/ppermute | solution.py:398
  17.5 8.0 %collective-permute-start.8 = (bf16[44,16,128]{2,1,0:T(8,128)(2,1)S(1)}, bf16[44,16,128]{2,1,0:T(8,128)(2,1)S(1)}, u32[]{:S(2)}, u32[]{:S(2)}) collective-permute-start(bf16[44,16,128]{2,1,0:T(8,128)(2,1)S(1)} %get-tuple-element.40.rest_0_), channel_id=1, source_target_pairs={{0,24},{4,28},{8,16},{12,20},{16,8},{20,12},{24,0},{28,4},{1,25},{... | collective-permute-start | bytes 540680 | tf_op jit(solution)/shard_map/ppermute | solution.py:394
  20.0 7.9 %collective-permute-start.6 = (bf16[44,16,128]{2,1,0:T(8,128)(2,1)S(1)}, bf16[44,16,128]{2,1,0:T(8,128)(2,1)S(1)}, u32[]{:S(2)}, u32[]{:S(2)}) collective-permute-start(bf16[44,16,128]{2,1,0:T(8,128)(2,1)S(1)} %get-tuple-element.40.rest_0_), channel_id=1, source_target_pairs={{0,16},{4,20},{8,24},{12,28},{16,0},{20,4},{24,8},{28,12},{1,17},{... | collective-permute-start | bytes 540680 | tf_op jit(solution)/shard_map/ppermute | solution.py:394
  20.5 7.5 %collective-permute-start.4 = (bf16[44,16,128]{2,1,0:T(8,128)(2,1)S(1)}, bf16[44,16,128]{2,1,0:T(8,128)(2,1)S(1)}, u32[]{:S(2)}, u32[]{:S(2)}) collective-permute-start(bf16[44,16,128]{2,1,0:T(8,128)(2,1)S(1)} %get-tuple-element.40.rest_0_), channel_id=1, source_target_pairs={{0,8},{4,12},{8,0},{12,4},{16,24},{20,28},{24,16},{28,20},{1,9},{5... | collective-permute-start | bytes 540680 | tf_op jit(solution)/shard_map/ppermute | solution.py:394
  21.0 9.6 %collective-permute-start.3 = (bf16[44,16,128]{2,1,0:T(8,128)(2,1)S(1)}, bf16[44,16,128]{2,1,0:T(8,128)(2,1)S(1)}, u32[]{:S(2)}, u32[]{:S(2)}) collective-permute-start(bf16[44,16,128]{2,1,0:T(8,128)(2,1)S(1)} %get-tuple-element.40.rest_0_), channel_id=1, source_target_pairs={{0,4},{4,0},{8,12},{12,8},{16,20},{20,16},{24,28},{28,24},{1,5},{5... | collective-permute-start | bytes 540680 | tf_op jit(solution)/shard_map/ppermute | solution.py:394
  25.5 5.2 %collective-permute-start.9 = (bf16[44,16,128]{2,1,0:T(8,128)(2,1)S(1)}, bf16[44,16,128]{2,1,0:T(8,128)(2,1)S(1)}, u32[]{:S(2)}, u32[]{:S(2)}) collective-permute-start(bf16[44,16,128]{2,1,0:T(8,128)(2,1)S(1)} %collective-permute-done.8.rest_6_), channel_id=1, source_target_pairs={{0,4},{4,0},{8,12},{12,8},{16,20},{20,16},{24,28},{28,24},{1,5},{5... | collective-permute-start | bytes 540680 | tf_op jit(solution)/shard_map/ppermute | solution.py:394
  27.9 2.8 %collective-permute-start.7 = (bf16[44,16,128]{2,1,0:T(8,128)(2,1)S(1)}, bf16[44,16,128]{2,1,0:T(8,128)(2,1)S(1)}, u32[]{:S(2)}, u32[]{:S(2)}) collective-permute-start(bf16[44,16,128]{2,1,0:T(8,128)(2,1)S(1)} %collective-permute-done.6.rest_4_), channel_id=1, source_target_pairs={{0,4},{4,0},{8,12},{12,8},{16,20},{20,16},{24,28},{28,24},{1,5},{5... | collective-permute-start | bytes 540680 | tf_op jit(solution)/shard_map/ppermute | solution.py:394
  28.0 2.7 %collective-permute-start.5 = (bf16[44,16,128]{2,1,0:T(8,128)(2,1)S(1)}, bf16[44,16,128]{2,1,0:T(8,128)(2,1)S(1)}, u32[]{:S(2)}, u32[]{:S(2)}) collective-permute-start(bf16[44,16,128]{2,1,0:T(8,128)(2,1)S(1)} %collective-permute-done.4.rest_2_), channel_id=1, source_target_pairs={{0,4},{4,0},{8,12},{12,8},{16,20},{20,16},{24,28},{28,24},{1,5},{5... | collective-permute-start | bytes 540680 | tf_op jit(solution)/shard_map/ppermute | solution.py:394
  38.5 1.5 %collective-permute-start.13 = (bf16[44,16,128]{2,1,0:T(8,128)(2,1)S(1)}, bf16[44,16,128]{2,1,0:T(8,128)(2,1)S(1)}, u32[]{:S(2)}, u32[]{:S(2)}) collective-permute-start(bf16[44,16,128]{2,1,0:T(8,128)(2,1)S(1)} %get-tuple-element.52), channel_id=1, source_target_pairs={{0,4},{4,0},{8,12},{12,8},{16,20},{20,16},{24,28},{28,24},{1,5},{5... | collective-permute-start | bytes 540680 | tf_op jit(solution)/shard_map/ppermute | solution.py:394
  38.6 1.6 %collective-permute-start.14 = (bf16[44,16,128]{2,1,0:T(8,128)(2,1)S(1)}, bf16[44,16,128]{2,1,0:T(8,128)(2,1)S(1)}, u32[]{:S(2)}, u32[]{:S(2)}) collective-permute-start(bf16[44,16,128]{2,1,0:T(8,128)(2,1)S(1)} %get-tuple-element.53), channel_id=1, source_target_pairs={{0,4},{4,0},{8,12},{12,8},{16,20},{20,16},{24,28},{28,24},{1,5},{5... | collective-permute-start | bytes 540680 | tf_op jit(solution)/shard_map/ppermute | solution.py:394
  39.0 1.4 %collective-permute-start.15 = (bf16[44,16,128]{2,1,0:T(8,128)(2,1)S(1)}, bf16[44,16,128]{2,1,0:T(8,128)(2,1)S(1)}, u32[]{:S(2)}, u32[]{:S(2)}) collective-permute-start(bf16[44,16,128]{2,1,0:T(8,128)(2,1)S(1)} %get-tuple-element.54), channel_id=1, source_target_pairs={{0,4},{4,0},{8,12},{12,8},{16,20},{20,16},{24,28},{28,24},{1,5},{5... | collective-permute-start | bytes 540680 | tf_op jit(solution)/shard_map/ppermute | solution.py:394
  39.1 1.6 %collective-permute-start.16 = (bf16[44,16,128]{2,1,0:T(8,128)(2,1)S(1)}, bf16[44,16,128]{2,1,0:T(8,128)(2,1)S(1)}, u32[]{:S(2)}, u32[]{:S(2)}) collective-permute-start(bf16[44,16,128]{2,1,0:T(8,128)(2,1)S(1)} %get-tuple-element.55), channel_id=1, source_target_pairs={{0,4},{4,0},{8,12},{12,8},{16,20},{20,16},{24,28},{28,24},{1,5},{5... | collective-permute-start | bytes 540680 | tf_op jit(solution)/shard_map/ppermute | solution.py:394
  40.9 8.3 %collective-permute-start.17 = (bf16[44,16,128]{2,1,0:T(8,128)(2,1)S(1)}, bf16[44,16,128]{2,1,0:T(8,128)(2,1)S(1)}, u32[]{:S(2)}, u32[]{:S(2)}) collective-permute-start(bf16[44,16,128]{2,1,0:T(8,128)(2,1)S(1)} %get-tuple-element.57), channel_id=1, source_target_pairs={{0,8},{4,12},{8,0},{12,4},{16,24},{20,28},{24,16},{28,20},{1,9},{5... | collective-permute-start | bytes 540680 | tf_op jit(solution)/shard_map/ppermute | solution.py:394
  42.5 6.4 %collective-permute-start.23 = (f32[2,8,2048]{2,1,0:T(8,128)S(1)}, f32[2,8,2048]{2,1,0:T(8,128)S(1)}, u32[]{:S(2)}, u32[]{:S(2)}) collective-permute-start(f32[2,8,2048]{2,1,0:T(8,128)S(1)} %get-tuple-element.65), channel_id=1, source_target_pairs={{0,1},{1,0},{2,3},{3,2},{4,5},{5,4},{6,7},{7,6},{8,9},{9,8},{10,11... | collective-permute-start | bytes 393224 | tf_op jit(solution)/shard_map/ppermute | solution.py:398
  42.5 10.3 %collective-permute-start.18 = (bf16[44,16,128]{2,1,0:T(8,128)(2,1)S(1)}, bf16[44,16,128]{2,1,0:T(8,128)(2,1)S(1)}, u32[]{:S(2)}, u32[]{:S(2)}) collective-permute-start(bf16[44,16,128]{2,1,0:T(8,128)(2,1)S(1)} %get-tuple-element.58), channel_id=1, source_target_pairs={{0,16},{4,20},{8,24},{12,28},{16,0},{20,4},{24,8},{28,12},{1,17},{... | collective-permute-start | bytes 540680 | tf_op jit(solution)/shard_map/ppermute | solution.py:394
  43.3 11.8 %collective-permute-start.19 = (bf16[44,16,128]{2,1,0:T(8,128)(2,1)S(1)}, bf16[44,16,128]{2,1,0:T(8,128)(2,1)S(1)}, u32[]{:S(2)}, u32[]{:S(2)}) collective-permute-start(bf16[44,16,128]{2,1,0:T(8,128)(2,1)S(1)} %get-tuple-element.59), channel_id=1, source_target_pairs={{0,24},{4,28},{8,16},{12,20},{16,8},{20,12},{24,0},{28,4},{1,25},{... | collective-permute-start | bytes 540680 | tf_op jit(solution)/shard_map/ppermute | solution.py:394
  44.5 52.5 %collective-permute-start.10 = (bf16[128,1280]{1,0:T(8,128)(2,1)S(1)}, bf16[128,1280]{1,0:T(8,128)(2,1)S(1)}, u32[]{:S(2)}, u32[]{:S(2)}) collective-permute-start(bf16[128,1280]{1,0:T(8,128)(2,1)S(1)} %get-tuple-element.43), channel_id=1, source_target_pairs={{0,1},{1,0},{2,3},{3,2},{4,5},{5,4},{6,7},{7,6},{8,9},{9,8},{10,11... | collective-permute-start | bytes 983048 | tf_op jit(solution)/shard_map/ppermute | solution.py:398
  48.8 50.0 %collective-permute-start.11 = (bf16[128,1280]{1,0:T(8,128)(2,1)S(1)}, bf16[128,1280]{1,0:T(8,128)(2,1)S(1)}, u32[]{:S(2)}, u32[]{:S(2)}) collective-permute-start(bf16[128,1280]{1,0:T(8,128)(2,1)S(1)} %get-tuple-element.44), channel_id=1, source_target_pairs={{0,2},{1,3},{2,0},{3,1},{4,6},{5,7},{6,4},{7,5},{8,10},{9,11},{10,... | collective-permute-start | bytes 983048 | tf_op jit(solution)/shard_map/ppermute | solution.py:398
  49.2 33.6 %collective-permute-start.24 = (f32[2,8,2048]{2,1,0:T(8,128)S(1)}, f32[2,8,2048]{2,1,0:T(8,128)S(1)}, u32[]{:S(2)}, u32[]{:S(2)}) collective-permute-start(f32[2,8,2048]{2,1,0:T(8,128)S(1)} %get-tuple-element.66), channel_id=1, source_target_pairs={{0,2},{1,3},{2,0},{3,1},{4,6},{5,7},{6,4},{7,5},{8,10},{9,11},{10,... | collective-permute-start | bytes 393224 | tf_op jit(solution)/shard_map/ppermute | solution.py:398
  52.8 30.0 %collective-permute-start.25 = (f32[2,8,2048]{2,1,0:T(8,128)S(1)}, f32[2,8,2048]{2,1,0:T(8,128)S(1)}, u32[]{:S(2)}, u32[]{:S(2)}) collective-permute-start(f32[2,8,2048]{2,1,0:T(8,128)S(1)} %get-tuple-element.67), channel_id=1, source_target_pairs={{0,3},{1,2},{2,1},{3,0},{4,7},{5,6},{6,5},{7,4},{8,11},{9,10},{10,... | collective-permute-start | bytes 393224 | tf_op jit(solution)/shard_map/ppermute | solution.py:398
  55.0 47.1 %collective-permute-start.12 = (bf16[128,1280]{1,0:T(8,128)(2,1)S(1)}, bf16[128,1280]{1,0:T(8,128)(2,1)S(1)}, u32[]{:S(2)}, u32[]{:S(2)}) collective-permute-start(bf16[128,1280]{1,0:T(8,128)(2,1)S(1)} %get-tuple-element.45), channel_id=1, source_target_pairs={{0,3},{1,2},{2,1},{3,0},{4,7},{5,6},{6,5},{7,4},{8,11},{9,10},{10,... | collective-permute-start | bytes 983048 | tf_op jit(solution)/shard_map/ppermute | solution.py:398
  82.8 5.0 %collective-permute-start.20 = (bf16[11,16,128]{2,1,0:T(8,128)(2,1)S(1)}, bf16[11,16,128]{2,1,0:T(8,128)(2,1)S(1)}, u32[]{:S(2)}, u32[]{:S(2)}) collective-permute-start(bf16[11,16,128]{2,1,0:T(8,128)(2,1)S(1)} %get-tuple-element.61), channel_id=1, source_target_pairs={{0,1},{1,0},{2,3},{3,2},{4,5},{5,4},{6,7},{7,6},{8,9},{9,8},{10,11... | collective-permute-start | bytes 135176 | tf_op jit(solution)/shard_map/ppermute | solution.py:398
  82.8 9.9 %collective-permute-start.21 = (bf16[11,16,128]{2,1,0:T(8,128)(2,1)S(1)}, bf16[11,16,128]{2,1,0:T(8,128)(2,1)S(1)}, u32[]{:S(2)}, u32[]{:S(2)}) collective-permute-start(bf16[11,16,128]{2,1,0:T(8,128)(2,1)S(1)} %get-tuple-element.62), channel_id=1, source_target_pairs={{0,2},{1,3},{2,0},{3,1},{4,6},{5,7},{6,4},{7,5},{8,10},{9,11},{10,... | collective-permute-start | bytes 135176 | tf_op jit(solution)/shard_map/ppermute | solution.py:398
  87.8 5.9 %collective-permute-start.22 = (bf16[11,16,128]{2,1,0:T(8,128)(2,1)S(1)}, bf16[11,16,128]{2,1,0:T(8,128)(2,1)S(1)}, u32[]{:S(2)}, u32[]{:S(2)}) collective-permute-start(bf16[11,16,128]{2,1,0:T(8,128)(2,1)S(1)} %get-tuple-element.63), channel_id=1, source_target_pairs={{0,3},{1,2},{2,1},{3,0},{4,7},{5,6},{6,5},{7,4},{8,11},{9,10},{10,... | collective-permute-start | bytes 135176 | tf_op jit(solution)/shard_map/ppermute | solution.py:398
  95.4 5.4 %collective-permute-start.31 = (bf16[20,16,128]{2,1,0:T(8,128)(2,1)S(1)}, bf16[20,16,128]{2,1,0:T(8,128)(2,1)S(1)}, u32[]{:S(2)}, u32[]{:S(2)}) collective-permute-start(bf16[20,16,128]{2,1,0:T(8,128)(2,1)S(1)} %get-tuple-element.68.rest_0_), channel_id=1, source_target_pairs={{0,24},{4,28},{8,16},{12,20},{16,8},{20,12},{24,0},{28,4},{1,25},{... | collective-permute-start | bytes 245768 | tf_op jit(solution)/shard_map/ppermute | solution.py:394
  96.9 4.7 %collective-permute-start.29 = (bf16[20,16,128]{2,1,0:T(8,128)(2,1)S(1)}, bf16[20,16,128]{2,1,0:T(8,128)(2,1)S(1)}, u32[]{:S(2)}, u32[]{:S(2)}) collective-permute-start(bf16[20,16,128]{2,1,0:T(8,128)(2,1)S(1)} %get-tuple-element.68.rest_0_), channel_id=1, source_target_pairs={{0,16},{4,20},{8,24},{12,28},{16,0},{20,4},{24,8},{28,12},{1,17},{... | collective-permute-start | bytes 245768 | tf_op jit(solution)/shard_map/ppermute | solution.py:394
  96.9 4.7 %collective-permute-start.27 = (bf16[20,16,128]{2,1,0:T(8,128)(2,1)S(1)}, bf16[20,16,128]{2,1,0:T(8,128)(2,1)S(1)}, u32[]{:S(2)}, u32[]{:S(2)}) collective-permute-start(bf16[20,16,128]{2,1,0:T(8,128)(2,1)S(1)} %get-tuple-element.68.rest_0_), channel_id=1, source_target_pairs={{0,8},{4,12},{8,0},{12,4},{16,24},{20,28},{24,16},{28,20},{1,9},{5... | collective-permute-start | bytes 245768 | tf_op jit(solution)/shard_map/ppermute | solution.py:394
  98.9 4.1 %collective-permute-start.26 = (bf16[20,16,128]{2,1,0:T(8,128)(2,1)S(1)}, bf16[20,16,128]{2,1,0:T(8,128)(2,1)S(1)}, u32[]{:S(2)}, u32[]{:S(2)}) collective-permute-start(bf16[20,16,128]{2,1,0:T(8,128)(2,1)S(1)} %get-tuple-element.68.rest_0_), channel_id=1, source_target_pairs={{0,4},{4,0},{8,12},{12,8},{16,20},{20,16},{24,28},{28,24},{1,5},{5... | collective-permute-start | bytes 245768 | tf_op jit(solution)/shard_map/ppermute | solution.py:394
  100.7 2.3 %collective-permute-start.32 = (bf16[20,16,128]{2,1,0:T(8,128)(2,1)S(1)}, bf16[20,16,128]{2,1,0:T(8,128)(2,1)S(1)}, u32[]{:S(2)}, u32[]{:S(2)}) collective-permute-start(bf16[20,16,128]{2,1,0:T(8,128)(2,1)S(1)} %collective-permute-done.31.rest_6_), channel_id=1, source_target_pairs={{0,4},{4,0},{8,12},{12,8},{16,20},{20,16},{24,28},{28,24},{1,5},{5... | collective-permute-start | bytes 245768 | tf_op jit(solution)/shard_map/ppermute | solution.py:394
  101.6 1.4 %collective-permute-start.30 = (bf16[20,16,128]{2,1,0:T(8,128)(2,1)S(1)}, bf16[20,16,128]{2,1,0:T(8,128)(2,1)S(1)}, u32[]{:S(2)}, u32[]{:S(2)}) collective-permute-start(bf16[20,16,128]{2,1,0:T(8,128)(2,1)S(1)} %collective-permute-done.29.rest_4_), channel_id=1, source_target_pairs={{0,4},{4,0},{8,12},{12,8},{16,20},{20,16},{24,28},{28,24},{1,5},{5... | collective-permute-start | bytes 245768 | tf_op jit(solution)/shard_map/ppermute | solution.py:394
  101.6 1.4 %collective-permute-start.28 = (bf16[20,16,128]{2,1,0:T(8,128)(2,1)S(1)}, bf16[20,16,128]{2,1,0:T(8,128)(2,1)S(1)}, u32[]{:S(2)}, u32[]{:S(2)}) collective-permute-start(bf16[20,16,128]{2,1,0:T(8,128)(2,1)S(1)} %collective-permute-done.27.rest_2_), channel_id=1, source_target_pairs={{0,4},{4,0},{8,12},{12,8},{16,20},{20,16},{24,28},{28,24},{1,5},{5... | collective-permute-start | bytes 245768 | tf_op jit(solution)/shard_map/ppermute | solution.py:394

commit v3 on v2

--- a/solution.py
+++ b/solution.py
@@ -211,9 +211,13 @@
     weights_in = rest[:parts]
     rest = rest[parts:]
     activated, slopes = rest[:2]
-    far = rest[2 : 1 + n]
-    own = rest[1 + n]
-    weights, hidden, grads = rest[2 + n :]
+    odd, near, even = split_steps(n)
+    relay = rest[2] if odd else None
+    at = 2 + (1 if odd else 0)
+    nears = rest[at : at + len(near)]
+    at += len(near)
+    evens = rest[at : at + len(even)]
+    own, weights, hidden, grads = rest[at + len(even) :]
     slots = n * bs
     me = here[0]
     if parts == 1:
@@ -281,8 +285,12 @@
         return grads[:, pl.ds(pl.multiple_of(band * width, blk), width)]
 
     own[...] = band_of(0)
-    for s in range(1, n):
-        far[s - 1][...] = band_of(s).astype(jnp.bfloat16)
+    for i, s in enumerate(odd):
+        relay[i] = band_of(s).astype(jnp.bfloat16)
+    for i, s in enumerate(near):
+        nears[i][...] = band_of(s).astype(jnp.bfloat16)
+    for i, s in enumerate(even):
+        evens[i][...] = band_of(s)
 
 
 def grad_kernel(cfg, here, table, tokens, slopes, *rest):
@@ -383,11 +391,37 @@
         out[:, pl.ds(pl.multiple_of((d ^ s) * rows, rows), rows), :] = rest[s][...]
 
 
-def sum_kernel(own, *rest):
-    total = own[...]
-    for term in rest[:-1]:
-        total = total + term[...].astype(jnp.float32)
-    rest[-1][...] = total.astype(jnp.bfloat16)
+def split_steps(n):
+    steps = list(range(1, n))
+    if not paired(n):
+        return [], [], steps
+    return steps[2::2], steps[:1], steps[1::2]
+
+
+def relay_kernel(count, *refs):
+    evens, outs = refs[:count], refs[-2 * count :]
+    half = evens[0].shape[0] // 2
+    for i in range(count):
+        total = evens[i][...]
+        if len(refs) > 3 * count:
+            total = total + refs[count][i].astype(jnp.float32)
+        total = total.astype(jnp.bfloat16)
+        outs[2 * i][...] = total[:half]
+        outs[2 * i + 1][...] = total[half:]
+
+
+def sum_kernel(cfg, own, *rest):
+    evens, nears = cfg
+    out = rest[-1]
+    half = own.shape[0] // 2
+    for h in range(2):
+        rows = slice(h * half, (h + 1) * half)
+        total = own[rows]
+        for i in range(evens):
+            total = total + rest[2 * i + h][...].astype(jnp.float32)
+        for i in range(nears):
+            total = total + rest[2 * evens + i][rows].astype(jnp.float32)
+        out[rows] = total.astype(jnp.bfloat16)
 
 
 def swap(value, bits, parts):
@@ -469,13 +503,15 @@
     tokens, cotangents = packed[n:]
     moments = [packs[0]] + [shift(packs[s], s, n) for s in range(1, n)]
 
+    odd, near, even = split_steps(n)
     results = call(
         functools.partial(forward_kernel, (n, bs, bw, blk, len(pieces))),
         [shape((tok, bw * blk), bf16)] * 2
-        + [shape((tok, width // n), bf16)] * (n - 1)
-        + [shape((tok, width // n), f32)],
+        + [shape((len(odd), tok, width // n), bf16)] * min(len(odd), 1)
+        + [shape((tok, width // n), bf16)] * len(near)
+        + [shape((tok, width // n), f32)] * (len(even) + 1),
         [SMEM, SMEM, VMEM, VMEM] + [VMEM] * len(pieces),
-        [VMEM] * (n + 2),
+        [VMEM] * (3 + min(len(odd), 1) + len(near) + len(even)),
         [
             pltpu.VMEM((slots, blk, blk), bf16),
             pltpu.VMEM((tok, bw * blk), f32),
@@ -483,8 +519,10 @@
         ],
     )(here, table, tokens, cotangents, *pieces)
     activated, slopes = results[:2]
-    far, own = results[2 : 1 + n], results[1 + n]
-    back_terms = [shift(far[s - 1], s, n) for s in range(1, n)]
+    rest = list(results[2:])
+    relayed = [shift(rest.pop(0), 1, n)] if odd else []
+    nears = [rest.pop(0) for _ in near]
+    evens, own = rest[:-1], rest[-1]
 
     count = parts if direct else 1
     partials = call(
@@ -495,18 +533,30 @@
         [pltpu.VMEM((slots, blk, blk), bf16)],
     )(here, table, tokens, slopes)
 
+    halves = call(
+        functools.partial(relay_kernel, len(even)),
+        [shape((tok // 2, width // n), bf16)] * (2 * len(even)),
+        [VMEM] * (len(even) + len(relayed)),
+        [VMEM] * (2 * len(even)),
+        [],
+    )(*evens, *relayed)
+    back_terms = []
+    for i, s in enumerate(even):
+        back_terms += [shift(halves[2 * i + h], s, n) for h in range(2)]
+    back_terms += [shift(x, s, n) for x, s in zip(nears, near)]
+
     if direct:
         half = parts // 2
-        even = [partials[2 * j] for j in range(half)]
+        kept = [partials[2 * j] for j in range(half)]
         crossed = [swap(partials[2 * j + 1], 1, parts) for j in range(half)]
-        paired = call(
+        summed = call(
             functools.partial(pair_kernel, half),
             [shape((slots, rows, blk), bf16)] * half,
             [VMEM] * parts,
             [VMEM] * half,
             [],
-        )(*even, *crossed)
-        terms = [paired[0]] + [swap(paired[j], 2 * j, parts) for j in range(1, half)]
+        )(*kept, *crossed)
+        terms = [summed[0]] + [swap(summed[j], 2 * j, parts) for j in range(1, half)]
     else:
         spread = partials[0].reshape(slots, parts, rows, blk).transpose(1, 0, 2, 3)
         spread = lax.all_to_all(spread, "dp", split_axis=0, concat_axis=0, tiled=True)
@@ -550,7 +600,11 @@
         weights_out = lax.all_gather(weight_share, "dp", axis=1, tiled=True)
 
     grad_inputs = call(
-        sum_kernel, shape((tok, width // n), bf16), [VMEM] * n, VMEM, []
+        functools.partial(sum_kernel, (len(even), len(near))),
+        shape((tok, width // n), bf16),
+        [VMEM] * (1 + len(back_terms)),
+        VMEM,
+        [],
     )(own, *back_terms)
     return (activated, grad_inputs, weights_out, first_new, second_new)
 

time: 105 us -> 88.1 us (0.84)
  waiting for transfers between devices: 47.3 us -> 35.5 us
  starting transfers between devices: 33.9 us -> 29 us
    ppermute x12 -> x13, waiting for transfers between devices: 35.4 us -> 22.9 us  [shift(): lax.ppermute(value, 'mp', [(i, target_of_static(i, step, n)) for i in ran...]
    ppermute x12 -> x13, starting transfers between devices: 21.3 us -> 16.4 us  [shift(): lax.ppermute(value, 'mp', [(i, target_of_static(i, step, n)) for i in ran...]
    pallas_call x10 -> x11, Pallas kernels: 21.3 us -> 21.3 us  [run(): pl.pallas_call(kernel, out_shape=out_shape, in_specs=in_specs, out_specs=...]
  transfers between devices with their start and end apart: 33 -> 34, of which waited for: 15 -> 16; matrix products, arithmetic and copies ran while one was open for 0% -> 0% of each run, Pallas kernels for 11% -> 13%
where the time goes in v3:
time: 88.1 us; the launch traced here: 87.9 us
  waiting for transfers between devices  35.5 us (40%)
  starting transfers between devices  29 us (33%)
  Pallas kernels  21.3 us (24%)
  local copies, waits for them, and re-layouts  1.19 us (1%)
    ppermute x13, waiting for transfers between devices, shift(): lax.ppermute(value, 'mp', [(i, target_of_static(i, step, n)) for i in ran...  22.9 us
    pallas_call x11, Pallas kernels, run(): pl.pallas_call(kernel, out_shape=out_shape, in_specs=in_specs, out_specs=...  21.3 us
    ppermute x13, starting transfers between devices, shift(): lax.ppermute(value, 'mp', [(i, target_of_static(i, step, n)) for i in ran...  16.4 us
    ppermute x21, waiting for transfers between devices, swap(): return lax.ppermute(value, 'dp', [(i, i ^ bits) for i in range(parts)])  12.7 us
    ppermute x21, starting transfers between devices, swap(): return lax.ppermute(value, 'dp', [(i, i ^ bits) for i in range(parts)])  12.6 us
  transfers between devices with their start and end apart: 34, of which 16 were waited for; matrix products, arithmetic and copies ran while one was open for 0% of the time, Pallas kernels for 13%

profile of v3, /device:TPU:0, one launch (start us, length us, event | category | flops | bytes accessed | tf_op | source)
XLA Modules:
  0.0 87.9 jit_solution(8519923629505371922)
XLA Ops:
  0.6 0.0 copy-start
  0.7 1.2 %copy-done = bf16[28,128,128]{2,1,0:T(8,128)(2,1)S(1)} copy-done((bf16[28,128,128]{2,1,0:T(8,128)(2,1)S(1)}, bf16[28,128,128]{2,1,0:T(8,128)(2,1)}, u32[]{:S(2)}) %copy-start) | copy-done | bytes 917528
  1.8 5.1 %collective-permute-start.2 = (bf16[28,16,128]{2,1,0:T(8,128)(2,1)S(1)}, bf16[28,16,128]{2,1,0:T(8,128)(2,1)S(1)}, u32[]{:S(2)}, u32[]{:S(2)}) collective-permute-start(bf16[28,16,128]{2,1,0:T(8,128)(2,1)S(1)} %constant_dynamic-slice_fusion.rest_0_), channel_id=1, source_target_pairs={{0,3},{1,2},{2,1},{3,0},{4,7},{5,6},{6,5},{7,4},{8,11},{9,10},{10,... | collective-permute-start | bytes 344072 | tf_op jit(solution)/shard_map/ppermute | solution.py:432
  7.0 0.0 collective-permute-start.1
  7.0 0.6 collective-permute-start
  7.6 0.1 pad_add_fusion.here
  7.7 5.6 %shard_map.110.table = s32[224]{0:T(256)S(1)} custom-call(s32[2]{0:T(128)S(1)} %pad_add_fusion.here, s32[2,80]{1,0:T(2,128)} %bitcast.3, s32[112]{0:T(128)} %moved.1), custom_call_target="tpu_custom_call" | custom-call | tf_op jit(solution)/shard_map/pallas_call | solution.py:39
  13.3 3.3 %collective-permute-done.1.rest_2_ = bf16[28,16,128]{2,1,0:T(8,128)(2,1)S(1)} collective-permute-done((bf16[28,16,128]{2,1,0:T(8,128)(2,1)S(1)}, bf16[28,16,128]{2,1,0:T(8,128)(2,1)S(1)}, u32[]{:S(2)}, u32[]{:S(2)}) %collective-permute-start.1) | collective-permute-done | bytes 114720 | tf_op jit(solution)/shard_map/ppermute | solution.py:432
  16.6 0.0 collective-permute-done.rest_1_
  16.7 0.8 shard_map.112
  17.5 2.5 %collective-permute-start.8 = (bf16[44,16,128]{2,1,0:T(8,128)(2,1)S(1)}, bf16[44,16,128]{2,1,0:T(8,128)(2,1)S(1)}, u32[]{:S(2)}, u32[]{:S(2)}) collective-permute-start(bf16[44,16,128]{2,1,0:T(8,128)(2,1)S(1)} %get-tuple-element.42.rest_0_), channel_id=1, source_target_pairs={{0,24},{4,28},{8,16},{12,20},{16,8},{20,12},{24,0},{28,4},{1,25},{... | collective-permute-start | bytes 540680 | tf_op jit(solution)/shard_map/ppermute | solution.py:428
  20.0 0.5 collective-permute-start.6
  20.5 0.5 collective-permute-start.4
  21.0 0.0 collective-permute-start.3
  21.0 4.4 %collective-permute-done.8.rest_6_ = bf16[44,16,128]{2,1,0:T(8,128)(2,1)S(1)} collective-permute-done((bf16[44,16,128]{2,1,0:T(8,128)(2,1)S(1)}, bf16[44,16,128]{2,1,0:T(8,128)(2,1)S(1)}, u32[]{:S(2)}, u32[]{:S(2)}) %collective-permute-start.8) | collective-permute-done | bytes 180256 | tf_op jit(solution)/shard_map/ppermute | solution.py:428
  25.5 2.4 %collective-permute-done.6.rest_4_ = bf16[44,16,128]{2,1,0:T(8,128)(2,1)S(1)} collective-permute-done((bf16[44,16,128]{2,1,0:T(8,128)(2,1)S(1)}, bf16[44,16,128]{2,1,0:T(8,128)(2,1)S(1)}, u32[]{:S(2)}, u32[]{:S(2)}) %collective-permute-start.6) | collective-permute-done | bytes 180256 | tf_op jit(solution)/shard_map/ppermute | solution.py:428
  27.9 0.0 collective-permute-start.7
  27.9 0.1 collective-permute-done.4.rest_2_
  28.0 0.4 collective-permute-start.5
  28.4 2.2 %shard_map.111 = (f32[2,8,2048]{2,1,0:T(8,128)S(1)}, f32[2,8,2048]{2,1,0:T(8,128)S(1)}, f32[2,8,2048]{2,1,0:T(8,128)S(1)}, f32[2,8,2048]{2,1,0:T(8,128)S(1)}, bf...) custom-call(s32[224]{0:T(256)S(1)} %shard_map.110.table, f32[28,2048]{1,0:T(8,128)} %first.1, ...), custom_call_target="tpu_custom_call" | custom-call | tf_op jit(solution)/shard_map/pallas_call | solution.py:39
  30.7 0.0 collective-permute-done.7.rest_5_
  30.7 5.7 %shard_map.113 = (bf16[128,2560]{1,0:T(8,128)(2,1)}, bf16[128,2560]{1,0:T(8,128)(2,1)S(1)}, bf16[1,128,1280]{2,1,0:T(8,128)(2,1)S(1)}, bf16[128,1280]{1,0:T(8,12...) custom-call(s32[2]{0:T(128)S(1)} %pad_add_fusion.here, s32[224]{0:T(256)S(1)} %shard_map.110.table, ...), custom_call_target="tpu_custom_call" | custom-call | tf_op jit(solution)/shard_map/pallas_call | solution.py:39
  36.4 2.1 %shard_map.116 = (bf16[44,16,128]{2,1,0:T(8,128)(2,1)S(1)}, bf16[44,16,128]{2,1,0:T(8,128)(2,1)S(1)}, bf16[44,16,128]{2,1,0:T(8,128)(2,1)S(1)}, bf16[44,16,128]{...) custom-call(s32[2]{0:T(128)S(1)} %pad_add_fusion.here, ...), custom_call_target="tpu_custom_call" | custom-call | tf_op jit(solution)/shard_map/pallas_call | solution.py:39
  38.5 0.2 collective-permute-start.14
  38.6 0.4 collective-permute-start.15
  39.1 0.1 collective-permute-start.16
  39.1 0.4 collective-permute-start.17
  39.6 0.0 collective-permute-start.10
  39.6 0.4 collective-permute-done.14.refs_4_
  40.0 0.3 collective-permute-done.15.refs_5_
  40.2 0.3 collective-permute-done.16.refs_6_
  40.5 0.3 collective-permute-done.17.refs_7_
  40.7 0.2 shard_map.117
  40.9 1.6 %collective-permute-start.18 = (bf16[44,16,128]{2,1,0:T(8,128)(2,1)S(1)}, bf16[44,16,128]{2,1,0:T(8,128)(2,1)S(1)}, u32[]{:S(2)}, u32[]{:S(2)}) collective-permute-start(bf16[44,16,128]{2,1,0:T(8,128)(2,1)S(1)} %get-tuple-element.61), channel_id=1, source_target_pairs={{0,8},{4,12},{8,0},{12,4},{16,24},{20,28},{24,16},{28,20},{1,9},{5... | collective-permute-start | bytes 540680 | tf_op jit(solution)/shard_map/ppermute | solution.py:428
  42.5 0.8 collective-permute-start.19
  43.3 0.9 %collective-permute-start.13 = (bf16[128,1280]{1,0:T(8,128)(2,1)S(1)}, bf16[128,1280]{1,0:T(8,128)(2,1)S(1)}, u32[]{:S(2)}, u32[]{:S(2)}) collective-permute-start(bf16[128,1280]{1,0:T(8,128)(2,1)S(1)} %get-tuple-element.49), channel_id=1, source_target_pairs={{0,1},{1,0},{2,3},{3,2},{4,5},{5,4},{6,7},{7,6},{8,9},{9,8},{10,11... | collective-permute-start | bytes 983048 | tf_op jit(solution)/shard_map/ppermute | solution.py:432
  44.2 1.2 %collective-permute-start.20 = (bf16[44,16,128]{2,1,0:T(8,128)(2,1)S(1)}, bf16[44,16,128]{2,1,0:T(8,128)(2,1)S(1)}, u32[]{:S(2)}, u32[]{:S(2)}) collective-permute-start(bf16[44,16,128]{2,1,0:T(8,128)(2,1)S(1)} %get-tuple-element.63), channel_id=1, source_target_pairs={{0,24},{4,28},{8,16},{12,20},{16,8},{20,12},{24,0},{28,4},{1,25},{... | collective-permute-start | bytes 540680 | tf_op jit(solution)/shard_map/ppermute | solution.py:428
  45.3 4.8 %collective-permute-done.10.refs_1_ = bf16[1,128,1280]{2,1,0:T(8,128)(2,1)S(1)} collective-permute-done((bf16[1,128,1280]{2,1,0:T(8,128)(2,1)S(1)}, bf16[1,128,1280]{2,1,0:T(8,128)(2,1)S(1)}, u32[]{:S(2)}, u32[]{:S(2)}) %collective-permute-start.10) | collective-permute-done | bytes 327712 | tf_op jit(solution)/shard_map/ppermute | solution.py:432
  50.1 0.0 collective-permute-start.24
  50.2 2.9 %collective-permute-start.25 = (f32[2,8,2048]{2,1,0:T(8,128)S(1)}, f32[2,8,2048]{2,1,0:T(8,128)S(1)}, u32[]{:S(2)}, u32[]{:S(2)}) collective-permute-start(f32[2,8,2048]{2,1,0:T(8,128)S(1)} %get-tuple-element.70), channel_id=1, source_target_pairs={{0,2},{1,3},{2,0},{3,1},{4,6},{5,7},{6,4},{7,5},{8,10},{9,11},{10,... | collective-permute-start | bytes 393224 | tf_op jit(solution)/shard_map/ppermute | solution.py:432
  53.0 0.0 collective-permute-done.19.rest_2_
  53.0 2.0 %collective-permute-start.26 = (f32[2,8,2048]{2,1,0:T(8,128)S(1)}, f32[2,8,2048]{2,1,0:T(8,128)S(1)}, u32[]{:S(2)}, u32[]{:S(2)}) collective-permute-start(f32[2,8,2048]{2,1,0:T(8,128)S(1)} %get-tuple-element.71), channel_id=1, source_target_pairs={{0,3},{1,2},{2,1},{3,0},{4,7},{5,6},{6,5},{7,4},{8,11},{9,10},{10,... | collective-permute-start | bytes 393224 | tf_op jit(solution)/shard_map/ppermute | solution.py:432
  55.0 0.1 shard_map.114
  55.1 0.1 collective-permute-start.11
  55.2 0.7 shard_map.118
  55.9 10.6 %collective-permute-done.24.rest_5_ = f32[2,8,2048]{2,1,0:T(8,128)S(1)} collective-permute-done((f32[2,8,2048]{2,1,0:T(8,128)S(1)}, f32[2,8,2048]{2,1,0:T(8,128)S(1)}, u32[]{:S(2)}, u32[]{:S(2)}) %collective-permute-start.24) | collective-permute-done | bytes 131104 | tf_op jit(solution)/shard_map/ppermute | solution.py:432
  66.5 0.0 collective-permute-start.21
  66.5 0.0 collective-permute-done.25.rest_6_
  66.5 2.7 %collective-permute-start.22 = (bf16[11,16,128]{2,1,0:T(8,128)(2,1)S(1)}, bf16[11,16,128]{2,1,0:T(8,128)(2,1)S(1)}, u32[]{:S(2)}, u32[]{:S(2)}) collective-permute-start(bf16[11,16,128]{2,1,0:T(8,128)(2,1)S(1)} %get-tuple-element.66), channel_id=1, source_target_pairs={{0,2},{1,3},{2,0},{3,1},{4,6},{5,7},{6,4},{7,5},{8,10},{9,11},{10,... | collective-permute-start | bytes 135176 | tf_op jit(solution)/shard_map/ppermute | solution.py:432
  69.2 1.7 %collective-permute-start.23 = (bf16[11,16,128]{2,1,0:T(8,128)(2,1)S(1)}, bf16[11,16,128]{2,1,0:T(8,128)(2,1)S(1)}, u32[]{:S(2)}, u32[]{:S(2)}) collective-permute-start(bf16[11,16,128]{2,1,0:T(8,128)(2,1)S(1)} %get-tuple-element.67), channel_id=1, source_target_pairs={{0,3},{1,2},{2,1},{3,0},{4,7},{5,6},{6,5},{7,4},{8,11},{9,10},{10,... | collective-permute-start | bytes 135176 | tf_op jit(solution)/shard_map/ppermute | solution.py:432
  70.9 2.7 %collective-permute-done.22.rest_2_ = bf16[11,16,128]{2,1,0:T(8,128)(2,1)S(1)} collective-permute-done((bf16[11,16,128]{2,1,0:T(8,128)(2,1)S(1)}, bf16[11,16,128]{2,1,0:T(8,128)(2,1)S(1)}, u32[]{:S(2)}, u32[]{:S(2)}) %collective-permute-start.22) | collective-permute-done | bytes 45088 | tf_op jit(solution)/shard_map/ppermute | solution.py:432
  73.6 1.5 %collective-permute-done.23.rest_3_ = bf16[11,16,128]{2,1,0:T(8,128)(2,1)S(1)} collective-permute-done((bf16[11,16,128]{2,1,0:T(8,128)(2,1)S(1)}, bf16[11,16,128]{2,1,0:T(8,128)(2,1)S(1)}, u32[]{:S(2)}, u32[]{:S(2)}) %collective-permute-start.23) | collective-permute-done | bytes 45088 | tf_op jit(solution)/shard_map/ppermute | solution.py:432
  75.0 1.7 %shard_map.119 = (f32[20,2048]{1,0:T(8,128)}, f32[20,2048]{1,0:T(8,128)}, bf16[20,16,128]{2,1,0:T(8,128)(2,1)S(1)}) custom-call(s32[224]{0:T(256)S(1)} %shard_map.110.table, bf16[20,16,128]{2,1,0:T(8,128)(2,1)S(1)} %get-tuple-element.50.mine, bf16[11,16,128]{2,1,0:T(8,128)(2,1)S(1)} %get-tuple-element.64.rest_0_, ...), custom_call_target="tpu_custom_call" | custom-call | tf_op jit(solution)/shard_map/pallas_call | solution.py:39
  76.7 1.7 %collective-permute-start.32 = (bf16[20,16,128]{2,1,0:T(8,128)(2,1)S(1)}, bf16[20,16,128]{2,1,0:T(8,128)(2,1)S(1)}, u32[]{:S(2)}, u32[]{:S(2)}) collective-permute-start(bf16[20,16,128]{2,1,0:T(8,128)(2,1)S(1)} %get-tuple-element.72.rest_0_), channel_id=1, source_target_pairs={{0,24},{4,28},{8,16},{12,20},{16,8},{20,12},{24,0},{28,4},{1,25},{... | collective-permute-start | bytes 245768 | tf_op jit(solution)/shard_map/ppermute | solution.py:428
  78.5 0.4 collective-permute-start.12
  78.9 1.7 %collective-permute-start.30 = (bf16[20,16,128]{2,1,0:T(8,128)(2,1)S(1)}, bf16[20,16,128]{2,1,0:T(8,128)(2,1)S(1)}, u32[]{:S(2)}, u32[]{:S(2)}) collective-permute-start(bf16[20,16,128]{2,1,0:T(8,128)(2,1)S(1)} %get-tuple-element.72.rest_0_), channel_id=1, source_target_pairs={{0,16},{4,20},{8,24},{12,28},{16,0},{20,4},{24,8},{28,12},{1,17},{... | collective-permute-start | bytes 245768 | tf_op jit(solution)/shard_map/ppermute | solution.py:428
  80.6 0.0 collective-permute-start.28
  80.6 1.5 %collective-permute-done.32.rest_6_ = bf16[20,16,128]{2,1,0:T(8,128)(2,1)S(1)} collective-permute-done((bf16[20,16,128]{2,1,0:T(8,128)(2,1)S(1)}, bf16[20,16,128]{2,1,0:T(8,128)(2,1)S(1)}, u32[]{:S(2)}, u32[]{:S(2)}) %collective-permute-start.32) | collective-permute-done | bytes 81952 | tf_op jit(solution)/shard_map/ppermute | solution.py:428
  82.1 1.2 %collective-permute-done.30.rest_4_ = bf16[20,16,128]{2,1,0:T(8,128)(2,1)S(1)} collective-permute-done((bf16[20,16,128]{2,1,0:T(8,128)(2,1)S(1)}, bf16[20,16,128]{2,1,0:T(8,128)(2,1)S(1)}, u32[]{:S(2)}, u32[]{:S(2)}) %collective-permute-start.30) | collective-permute-done | bytes 81952 | tf_op jit(solution)/shard_map/ppermute | solution.py:428
  83.3 1.7 %collective-permute-done.28.rest_2_ = bf16[20,16,128]{2,1,0:T(8,128)(2,1)S(1)} collective-permute-done((bf16[20,16,128]{2,1,0:T(8,128)(2,1)S(1)}, bf16[20,16,128]{2,1,0:T(8,128)(2,1)S(1)}, u32[]{:S(2)}, u32[]{:S(2)}) %collective-permute-start.28) | collective-permute-done | bytes 81952 | tf_op jit(solution)/shard_map/ppermute | solution.py:428
  85.0 0.5 collective-permute-start.29
  85.6 0.8 shard_map.115
  86.4 0.1 collective-permute-done.29.rest_3_
  86.5 1.5 %shard_map.120 = bf16[20,128,128]{2,1,0:T(8,128)(2,1)} custom-call(s32[2]{0:T(128)S(1)} %pad_add_fusion.here, bf16[20,16,128]{2,1,0:T(8,128)(2,1)S(1)} %get-tuple-element.72.rest_0_, bf16[20,16,128]{2,1,0:T(8,128)(2,1)S(1)} %collective-permute-done.27.rest_1_, bf16[20,16,128]{2,1,0:T(8,128)(2,1)S(1)} %collective-permute-done.28.rest_2_, ...), custom_call_target="tpu_custom_call" | custom-call | tf_op jit(solution)/shard_map/pallas_call | solution.py:39
  (19 shorter events, 0.1 us)
Async XLA Ops:
  0.6 1.2 %copy-start = (bf16[28,128,128]{2,1,0:T(8,128)(2,1)S(1)}, bf16[28,128,128]{2,1,0:T(8,128)(2,1)}, u32[]{:S(2)}) copy-start(bf16[28,128,128]{2,1,0:T(8,128)(2,1)} %param.9) | copy-start | bytes 2752516
  1.8 11.5 %collective-permute-start.2 = (bf16[28,16,128]{2,1,0:T(8,128)(2,1)S(1)}, bf16[28,16,128]{2,1,0:T(8,128)(2,1)S(1)}, u32[]{:S(2)}, u32[]{:S(2)}) collective-permute-start(bf16[28,16,128]{2,1,0:T(8,128)(2,1)S(1)} %constant_dynamic-slice_fusion.rest_0_), channel_id=1, source_target_pairs={{0,3},{1,2},{2,1},{3,0},{4,7},{5,6},{6,5},{7,4},{8,11},{9,10},{10,... | collective-permute-start | bytes 344072 | tf_op jit(solution)/shard_map/ppermute | solution.py:432
  7.0 9.7 %collective-permute-start.1 = (bf16[28,16,128]{2,1,0:T(8,128)(2,1)S(1)}, bf16[28,16,128]{2,1,0:T(8,128)(2,1)S(1)}, u32[]{:S(2)}, u32[]{:S(2)}) collective-permute-start(bf16[28,16,128]{2,1,0:T(8,128)(2,1)S(1)} %constant_dynamic-slice_fusion.rest_0_), channel_id=1, source_target_pairs={{0,2},{1,3},{2,0},{3,1},{4,6},{5,7},{6,4},{7,5},{8,10},{9,11},{10,... | collective-permute-start | bytes 344072 | tf_op jit(solution)/shard_map/ppermute | solution.py:432
  7.0 9.7 %collective-permute-start = (bf16[28,16,128]{2,1,0:T(8,128)(2,1)S(1)}, bf16[28,16,128]{2,1,0:T(8,128)(2,1)S(1)}, u32[]{:S(2)}, u32[]{:S(2)}) collective-permute-start(bf16[28,16,128]{2,1,0:T(8,128)(2,1)S(1)} %constant_dynamic-slice_fusion.rest_0_), channel_id=1, source_target_pairs={{0,1},{1,0},{2,3},{3,2},{4,5},{5,4},{6,7},{7,6},{8,9},{9,8},{10,11... | collective-permute-start | bytes 344072 | tf_op jit(solution)/shard_map/ppermute | solution.py:432
  17.5 8.0 %collective-permute-start.8 = (bf16[44,16,128]{2,1,0:T(8,128)(2,1)S(1)}, bf16[44,16,128]{2,1,0:T(8,128)(2,1)S(1)}, u32[]{:S(2)}, u32[]{:S(2)}) collective-permute-start(bf16[44,16,128]{2,1,0:T(8,128)(2,1)S(1)} %get-tuple-element.42.rest_0_), channel_id=1, source_target_pairs={{0,24},{4,28},{8,16},{12,20},{16,8},{20,12},{24,0},{28,4},{1,25},{... | collective-permute-start | bytes 540680 | tf_op jit(solution)/shard_map/ppermute | solution.py:428
  20.0 7.9 %collective-permute-start.6 = (bf16[44,16,128]{2,1,0:T(8,128)(2,1)S(1)}, bf16[44,16,128]{2,1,0:T(8,128)(2,1)S(1)}, u32[]{:S(2)}, u32[]{:S(2)}) collective-permute-start(bf16[44,16,128]{2,1,0:T(8,128)(2,1)S(1)} %get-tuple-element.42.rest_0_), channel_id=1, source_target_pairs={{0,16},{4,20},{8,24},{12,28},{16,0},{20,4},{24,8},{28,12},{1,17},{... | collective-permute-start | bytes 540680 | tf_op jit(solution)/shard_map/ppermute | solution.py:428
  20.5 7.5 %collective-permute-start.4 = (bf16[44,16,128]{2,1,0:T(8,128)(2,1)S(1)}, bf16[44,16,128]{2,1,0:T(8,128)(2,1)S(1)}, u32[]{:S(2)}, u32[]{:S(2)}) collective-permute-start(bf16[44,16,128]{2,1,0:T(8,128)(2,1)S(1)} %get-tuple-element.42.rest_0_), channel_id=1, source_target_pairs={{0,8},{4,12},{8,0},{12,4},{16,24},{20,28},{24,16},{28,20},{1,9},{5... | collective-permute-start | bytes 540680 | tf_op jit(solution)/shard_map/ppermute | solution.py:428
  21.0 9.6 %collective-permute-start.3 = (bf16[44,16,128]{2,1,0:T(8,128)(2,1)S(1)}, bf16[44,16,128]{2,1,0:T(8,128)(2,1)S(1)}, u32[]{:S(2)}, u32[]{:S(2)}) collective-permute-start(bf16[44,16,128]{2,1,0:T(8,128)(2,1)S(1)} %get-tuple-element.42.rest_0_), channel_id=1, source_target_pairs={{0,4},{4,0},{8,12},{12,8},{16,20},{20,16},{24,28},{28,24},{1,5},{5... | collective-permute-start | bytes 540680 | tf_op jit(solution)/shard_map/ppermute | solution.py:428
  25.5 5.2 %collective-permute-start.9 = (bf16[44,16,128]{2,1,0:T(8,128)(2,1)S(1)}, bf16[44,16,128]{2,1,0:T(8,128)(2,1)S(1)}, u32[]{:S(2)}, u32[]{:S(2)}) collective-permute-start(bf16[44,16,128]{2,1,0:T(8,128)(2,1)S(1)} %collective-permute-done.8.rest_6_), channel_id=1, source_target_pairs={{0,4},{4,0},{8,12},{12,8},{16,20},{20,16},{24,28},{28,24},{1,5},{5... | collective-permute-start | bytes 540680 | tf_op jit(solution)/shard_map/ppermute | solution.py:428
  27.9 2.8 %collective-permute-start.7 = (bf16[44,16,128]{2,1,0:T(8,128)(2,1)S(1)}, bf16[44,16,128]{2,1,0:T(8,128)(2,1)S(1)}, u32[]{:S(2)}, u32[]{:S(2)}) collective-permute-start(bf16[44,16,128]{2,1,0:T(8,128)(2,1)S(1)} %collective-permute-done.6.rest_4_), channel_id=1, source_target_pairs={{0,4},{4,0},{8,12},{12,8},{16,20},{20,16},{24,28},{28,24},{1,5},{5... | collective-permute-start | bytes 540680 | tf_op jit(solution)/shard_map/ppermute | solution.py:428
  28.0 2.7 %collective-permute-start.5 = (bf16[44,16,128]{2,1,0:T(8,128)(2,1)S(1)}, bf16[44,16,128]{2,1,0:T(8,128)(2,1)S(1)}, u32[]{:S(2)}, u32[]{:S(2)}) collective-permute-start(bf16[44,16,128]{2,1,0:T(8,128)(2,1)S(1)} %collective-permute-done.4.rest_2_), channel_id=1, source_target_pairs={{0,4},{4,0},{8,12},{12,8},{16,20},{20,16},{24,28},{28,24},{1,5},{5... | collective-permute-start | bytes 540680 | tf_op jit(solution)/shard_map/ppermute | solution.py:428
  38.5 1.5 %collective-permute-start.14 = (bf16[44,16,128]{2,1,0:T(8,128)(2,1)S(1)}, bf16[44,16,128]{2,1,0:T(8,128)(2,1)S(1)}, u32[]{:S(2)}, u32[]{:S(2)}) collective-permute-start(bf16[44,16,128]{2,1,0:T(8,128)(2,1)S(1)} %get-tuple-element.56), channel_id=1, source_target_pairs={{0,4},{4,0},{8,12},{12,8},{16,20},{20,16},{24,28},{28,24},{1,5},{5... | collective-permute-start | bytes 540680 | tf_op jit(solution)/shard_map/ppermute | solution.py:428
  38.6 1.6 %collective-permute-start.15 = (bf16[44,16,128]{2,1,0:T(8,128)(2,1)S(1)}, bf16[44,16,128]{2,1,0:T(8,128)(2,1)S(1)}, u32[]{:S(2)}, u32[]{:S(2)}) collective-permute-start(bf16[44,16,128]{2,1,0:T(8,128)(2,1)S(1)} %get-tuple-element.57), channel_id=1, source_target_pairs={{0,4},{4,0},{8,12},{12,8},{16,20},{20,16},{24,28},{28,24},{1,5},{5... | collective-permute-start | bytes 540680 | tf_op jit(solution)/shard_map/ppermute | solution.py:428
  39.1 1.4 %collective-permute-start.16 = (bf16[44,16,128]{2,1,0:T(8,128)(2,1)S(1)}, bf16[44,16,128]{2,1,0:T(8,128)(2,1)S(1)}, u32[]{:S(2)}, u32[]{:S(2)}) collective-permute-start(bf16[44,16,128]{2,1,0:T(8,128)(2,1)S(1)} %get-tuple-element.58), channel_id=1, source_target_pairs={{0,4},{4,0},{8,12},{12,8},{16,20},{20,16},{24,28},{28,24},{1,5},{5... | collective-permute-start | bytes 540680 | tf_op jit(solution)/shard_map/ppermute | solution.py:428
  39.1 1.6 %collective-permute-start.17 = (bf16[44,16,128]{2,1,0:T(8,128)(2,1)S(1)}, bf16[44,16,128]{2,1,0:T(8,128)(2,1)S(1)}, u32[]{:S(2)}, u32[]{:S(2)}) collective-permute-start(bf16[44,16,128]{2,1,0:T(8,128)(2,1)S(1)} %get-tuple-element.59), channel_id=1, source_target_pairs={{0,4},{4,0},{8,12},{12,8},{16,20},{20,16},{24,28},{28,24},{1,5},{5... | collective-permute-start | bytes 540680 | tf_op jit(solution)/shard_map/ppermute | solution.py:428
  39.6 10.6 %collective-permute-start.10 = (bf16[1,128,1280]{2,1,0:T(8,128)(2,1)S(1)}, bf16[1,128,1280]{2,1,0:T(8,128)(2,1)S(1)}, u32[]{:S(2)}, u32[]{:S(2)}) collective-permute-start(bf16[1,128,1280]{2,1,0:T(8,128)(2,1)S(1)} %get-tuple-element.46), channel_id=1, source_target_pairs={{0,1},{1,0},{2,3},{3,2},{4,5},{5,4},{6,7},{7,6},{8,9},{9,8},{10,11... | collective-permute-start | bytes 983048 | tf_op jit(solution)/shard_map/ppermute | solution.py:432
  40.9 9.2 %collective-permute-start.18 = (bf16[44,16,128]{2,1,0:T(8,128)(2,1)S(1)}, bf16[44,16,128]{2,1,0:T(8,128)(2,1)S(1)}, u32[]{:S(2)}, u32[]{:S(2)}) collective-permute-start(bf16[44,16,128]{2,1,0:T(8,128)(2,1)S(1)} %get-tuple-element.61), channel_id=1, source_target_pairs={{0,8},{4,12},{8,0},{12,4},{16,24},{20,28},{24,16},{28,20},{1,9},{5... | collective-permute-start | bytes 540680 | tf_op jit(solution)/shard_map/ppermute | solution.py:428
  42.5 10.5 %collective-permute-start.19 = (bf16[44,16,128]{2,1,0:T(8,128)(2,1)S(1)}, bf16[44,16,128]{2,1,0:T(8,128)(2,1)S(1)}, u32[]{:S(2)}, u32[]{:S(2)}) collective-permute-start(bf16[44,16,128]{2,1,0:T(8,128)(2,1)S(1)} %get-tuple-element.62), channel_id=1, source_target_pairs={{0,16},{4,20},{8,24},{12,28},{16,0},{20,4},{24,8},{28,12},{1,17},{... | collective-permute-start | bytes 540680 | tf_op jit(solution)/shard_map/ppermute | solution.py:428
  43.3 37.3 %collective-permute-start.13 = (bf16[128,1280]{1,0:T(8,128)(2,1)S(1)}, bf16[128,1280]{1,0:T(8,128)(2,1)S(1)}, u32[]{:S(2)}, u32[]{:S(2)}) collective-permute-start(bf16[128,1280]{1,0:T(8,128)(2,1)S(1)} %get-tuple-element.49), channel_id=1, source_target_pairs={{0,1},{1,0},{2,3},{3,2},{4,5},{5,4},{6,7},{7,6},{8,9},{9,8},{10,11... | collective-permute-start | bytes 983048 | tf_op jit(solution)/shard_map/ppermute | solution.py:432
  44.2 11.0 %collective-permute-start.20 = (bf16[44,16,128]{2,1,0:T(8,128)(2,1)S(1)}, bf16[44,16,128]{2,1,0:T(8,128)(2,1)S(1)}, u32[]{:S(2)}, u32[]{:S(2)}) collective-permute-start(bf16[44,16,128]{2,1,0:T(8,128)(2,1)S(1)} %get-tuple-element.63), channel_id=1, source_target_pairs={{0,24},{4,28},{8,16},{12,20},{16,8},{20,12},{24,0},{28,4},{1,25},{... | collective-permute-start | bytes 540680 | tf_op jit(solution)/shard_map/ppermute | solution.py:428
  50.1 16.3 %collective-permute-start.24 = (f32[2,8,2048]{2,1,0:T(8,128)S(1)}, f32[2,8,2048]{2,1,0:T(8,128)S(1)}, u32[]{:S(2)}, u32[]{:S(2)}) collective-permute-start(f32[2,8,2048]{2,1,0:T(8,128)S(1)} %get-tuple-element.69), channel_id=1, source_target_pairs={{0,1},{1,0},{2,3},{3,2},{4,5},{5,4},{6,7},{7,6},{8,9},{9,8},{10,11... | collective-permute-start | bytes 393224 | tf_op jit(solution)/shard_map/ppermute | solution.py:432
  50.2 16.3 %collective-permute-start.25 = (f32[2,8,2048]{2,1,0:T(8,128)S(1)}, f32[2,8,2048]{2,1,0:T(8,128)S(1)}, u32[]{:S(2)}, u32[]{:S(2)}) collective-permute-start(f32[2,8,2048]{2,1,0:T(8,128)S(1)} %get-tuple-element.70), channel_id=1, source_target_pairs={{0,2},{1,3},{2,0},{3,1},{4,6},{5,7},{6,4},{7,5},{8,10},{9,11},{10,... | collective-permute-start | bytes 393224 | tf_op jit(solution)/shard_map/ppermute | solution.py:432
  53.0 16.2 %collective-permute-start.26 = (f32[2,8,2048]{2,1,0:T(8,128)S(1)}, f32[2,8,2048]{2,1,0:T(8,128)S(1)}, u32[]{:S(2)}, u32[]{:S(2)}) collective-permute-start(f32[2,8,2048]{2,1,0:T(8,128)S(1)} %get-tuple-element.71), channel_id=1, source_target_pairs={{0,3},{1,2},{2,1},{3,0},{4,7},{5,6},{6,5},{7,4},{8,11},{9,10},{10,... | collective-permute-start | bytes 393224 | tf_op jit(solution)/shard_map/ppermute | solution.py:432
  55.1 29.9 %collective-permute-start.11 = (bf16[64,1280]{1,0:T(8,128)(2,1)S(1)}, bf16[64,1280]{1,0:T(8,128)(2,1)S(1)}, u32[]{:S(2)}, u32[]{:S(2)}) collective-permute-start(bf16[64,1280]{1,0:T(8,128)(2,1)S(1)} %get-tuple-element.47), channel_id=1, source_target_pairs={{0,2},{1,3},{2,0},{3,1},{4,6},{5,7},{6,4},{7,5},{8,10},{9,11},{10,... | collective-permute-start | bytes 491528 | tf_op jit(solution)/shard_map/ppermute | solution.py:432
  66.5 4.4 %collective-permute-start.21 = (bf16[11,16,128]{2,1,0:T(8,128)(2,1)S(1)}, bf16[11,16,128]{2,1,0:T(8,128)(2,1)S(1)}, u32[]{:S(2)}, u32[]{:S(2)}) collective-permute-start(bf16[11,16,128]{2,1,0:T(8,128)(2,1)S(1)} %get-tuple-element.65), channel_id=1, source_target_pairs={{0,1},{1,0},{2,3},{3,2},{4,5},{5,4},{6,7},{7,6},{8,9},{9,8},{10,11... | collective-permute-start | bytes 135176 | tf_op jit(solution)/shard_map/ppermute | solution.py:432
  66.5 7.1 %collective-permute-start.22 = (bf16[11,16,128]{2,1,0:T(8,128)(2,1)S(1)}, bf16[11,16,128]{2,1,0:T(8,128)(2,1)S(1)}, u32[]{:S(2)}, u32[]{:S(2)}) collective-permute-start(bf16[11,16,128]{2,1,0:T(8,128)(2,1)S(1)} %get-tuple-element.66), channel_id=1, source_target_pairs={{0,2},{1,3},{2,0},{3,1},{4,6},{5,7},{6,4},{7,5},{8,10},{9,11},{10,... | collective-permute-start | bytes 135176 | tf_op jit(solution)/shard_map/ppermute | solution.py:432
  69.2 5.8 %collective-permute-start.23 = (bf16[11,16,128]{2,1,0:T(8,128)(2,1)S(1)}, bf16[11,16,128]{2,1,0:T(8,128)(2,1)S(1)}, u32[]{:S(2)}, u32[]{:S(2)}) collective-permute-start(bf16[11,16,128]{2,1,0:T(8,128)(2,1)S(1)} %get-tuple-element.67), channel_id=1, source_target_pairs={{0,3},{1,2},{2,1},{3,0},{4,7},{5,6},{6,5},{7,4},{8,11},{9,10},{10,... | collective-permute-start | bytes 135176 | tf_op jit(solution)/shard_map/ppermute | solution.py:432
  76.7 5.3 %collective-permute-start.32 = (bf16[20,16,128]{2,1,0:T(8,128)(2,1)S(1)}, bf16[20,16,128]{2,1,0:T(8,128)(2,1)S(1)}, u32[]{:S(2)}, u32[]{:S(2)}) collective-permute-start(bf16[20,16,128]{2,1,0:T(8,128)(2,1)S(1)} %get-tuple-element.72.rest_0_), channel_id=1, source_target_pairs={{0,24},{4,28},{8,16},{12,20},{16,8},{20,12},{24,0},{28,4},{1,25},{... | collective-permute-start | bytes 245768 | tf_op jit(solution)/shard_map/ppermute | solution.py:428
  78.5 7.1 %collective-permute-start.12 = (bf16[64,1280]{1,0:T(8,128)(2,1)S(1)}, bf16[64,1280]{1,0:T(8,128)(2,1)S(1)}, u32[]{:S(2)}, u32[]{:S(2)}) collective-permute-start(bf16[64,1280]{1,0:T(8,128)(2,1)S(1)} %get-tuple-element.48), channel_id=1, source_target_pairs={{0,2},{1,3},{2,0},{3,1},{4,6},{5,7},{6,4},{7,5},{8,10},{9,11},{10,... | collective-permute-start | bytes 491528 | tf_op jit(solution)/shard_map/ppermute | solution.py:432
  78.9 4.4 %collective-permute-start.30 = (bf16[20,16,128]{2,1,0:T(8,128)(2,1)S(1)}, bf16[20,16,128]{2,1,0:T(8,128)(2,1)S(1)}, u32[]{:S(2)}, u32[]{:S(2)}) collective-permute-start(bf16[20,16,128]{2,1,0:T(8,128)(2,1)S(1)} %get-tuple-element.72.rest_0_), channel_id=1, source_target_pairs={{0,16},{4,20},{8,24},{12,28},{16,0},{20,4},{24,8},{28,12},{1,17},{... | collective-permute-start | bytes 245768 | tf_op jit(solution)/shard_map/ppermute | solution.py:428
  80.6 4.4 %collective-permute-start.28 = (bf16[20,16,128]{2,1,0:T(8,128)(2,1)S(1)}, bf16[20,16,128]{2,1,0:T(8,128)(2,1)S(1)}, u32[]{:S(2)}, u32[]{:S(2)}) collective-permute-start(bf16[20,16,128]{2,1,0:T(8,128)(2,1)S(1)} %get-tuple-element.72.rest_0_), channel_id=1, source_target_pairs={{0,8},{4,12},{8,0},{12,4},{16,24},{20,28},{24,16},{28,20},{1,9},{5... | collective-permute-start | bytes 245768 | tf_op jit(solution)/shard_map/ppermute | solution.py:428
  82.1 4.3 %collective-permute-start.27 = (bf16[20,16,128]{2,1,0:T(8,128)(2,1)S(1)}, bf16[20,16,128]{2,1,0:T(8,128)(2,1)S(1)}, u32[]{:S(2)}, u32[]{:S(2)}) collective-permute-start(bf16[20,16,128]{2,1,0:T(8,128)(2,1)S(1)} %get-tuple-element.72.rest_0_), channel_id=1, source_target_pairs={{0,4},{4,0},{8,12},{12,8},{16,20},{20,16},{24,28},{28,24},{1,5},{5... | collective-permute-start | bytes 245768 | tf_op jit(solution)/shard_map/ppermute | solution.py:428
  83.3 3.1 %collective-permute-start.33 = (bf16[20,16,128]{2,1,0:T(8,128)(2,1)S(1)}, bf16[20,16,128]{2,1,0:T(8,128)(2,1)S(1)}, u32[]{:S(2)}, u32[]{:S(2)}) collective-permute-start(bf16[20,16,128]{2,1,0:T(8,128)(2,1)S(1)} %collective-permute-done.32.rest_6_), channel_id=1, source_target_pairs={{0,4},{4,0},{8,12},{12,8},{16,20},{20,16},{24,28},{28,24},{1,5},{5... | collective-permute-start | bytes 245768 | tf_op jit(solution)/shard_map/ppermute | solution.py:428
  85.0 1.4 %collective-permute-start.31 = (bf16[20,16,128]{2,1,0:T(8,128)(2,1)S(1)}, bf16[20,16,128]{2,1,0:T(8,128)(2,1)S(1)}, u32[]{:S(2)}, u32[]{:S(2)}) collective-permute-start(bf16[20,16,128]{2,1,0:T(8,128)(2,1)S(1)} %collective-permute-done.30.rest_4_), channel_id=1, source_target_pairs={{0,4},{4,0},{8,12},{12,8},{16,20},{20,16},{24,28},{28,24},{1,5},{5... | collective-permute-start | bytes 245768 | tf_op jit(solution)/shard_map/ppermute | solution.py:428
  85.0 1.4 %collective-permute-start.29 = (bf16[20,16,128]{2,1,0:T(8,128)(2,1)S(1)}, bf16[20,16,128]{2,1,0:T(8,128)(2,1)S(1)}, u32[]{:S(2)}, u32[]{:S(2)}) collective-permute-start(bf16[20,16,128]{2,1,0:T(8,128)(2,1)S(1)} %collective-permute-done.28.rest_2_), channel_id=1, source_target_pairs={{0,4},{4,0},{8,12},{12,8},{16,20},{20,16},{24,28},{28,24},{1,5},{5... | collective-permute-start | bytes 245768 | tf_op jit(solution)/shard_map/ppermute | solution.py:428

commit v4 on v3

--- a/solution.py
+++ b/solution.py
@@ -185,6 +185,14 @@
     copies[3].wait()
 
 
+def share_kernel(weights, out, sem):
+    rows = out.shape[1]
+    at = pl.multiple_of(lax.axis_index("dp") * rows, rows)
+    copy = pltpu.make_async_copy(weights.at[:, pl.ds(at, rows), :], out, sem)
+    copy.start()
+    copy.wait()
+
+
 def select_kernel(cfg, table, *rest):
     n, per, cap, bs = cfg
     shares = rest[:n]
@@ -232,6 +240,7 @@
         return pl.ds(pl.multiple_of(index * blk, blk), blk)
 
     hidden[...] = jnp.zeros_like(hidden)
+    zeros = grads.shape[1] // blk // bw
 
     def product(w, _):
         for k in range(bs):
@@ -259,10 +268,13 @@
             2.0 * SQRT_2_OVER_PI + (6.0 * 0.044715 * SQRT_2_OVER_PI) * square
         )
         slopes[:, at] = (cotangent[:, at].astype(jnp.float32) * slope).astype(jnp.bfloat16)
+        for i in range(zeros):
+            grads[:, col_at(c * zeros + i)] = jnp.zeros_like(v)
         return 0
 
     lax.fori_loop(0, bw, pointwise, 0)
-    grads[...] = jnp.zeros_like(grads)
+    for c in range(bw * zeros, grads.shape[1] // blk):
+        grads[:, c * blk : (c + 1) * blk] = jnp.zeros((grads.shape[0], blk), jnp.float32)
 
     def back(w, _):
         for k in range(bs):
@@ -381,6 +393,28 @@
         )
     for i in range(per):
         weight_out[i] = weight[i * rows : (i + 1) * rows, :].astype(jnp.bfloat16)
+
+
+def flush_kernel(count, *refs):
+    sems = refs[2 * count]
+    copies = [
+        pltpu.make_async_copy(refs[i], refs[count + i], sems.at[i]) for i in range(count)
+    ]
+    for copy in copies:
+        copy.start()
+    for copy in copies:
+        copy.wait()
+
+
+def flush(values):
+    count = len(values)
+    return call(
+        functools.partial(flush_kernel, count),
+        [shape(x.shape, x.dtype) for x in values],
+        [VMEM] * count,
+        [pl.BlockSpec(memory_space=pltpu.HBM)] * count,
+        [pltpu.SemaphoreType.DMA((count,))],
+    )(*values)
 
 
 def join_kernel(parts, here, *rest):
@@ -461,7 +495,9 @@
     bf16, f32 = jnp.bfloat16, jnp.float32
     here = jnp.stack([me, d]).astype(jnp.int32)
 
-    share = lax.dynamic_slice_in_dim(old_weights, d * rows, rows, 1)
+    share = call(
+        share_kernel, shape((cap, rows, blk), bf16), [ANY], VMEM, [pltpu.SemaphoreType.DMA(())]
+    )(in_hbm(old_weights))
     shares = [share] + [shift(share, s, n) for s in range(1, n)]
 
     out = 3 * slots + 3 * per
@@ -506,7 +542,7 @@
     odd, near, even = split_steps(n)
     results = call(
         functools.partial(forward_kernel, (n, bs, bw, blk, len(pieces))),
-        [shape((tok, bw * blk), bf16)] * 2
+        [pltpu.VMEM((tok, bw * blk), bf16), shape((tok, bw * blk), bf16)]
         + [shape((len(odd), tok, width // n), bf16)] * min(len(odd), 1)
         + [shape((tok, width // n), bf16)] * len(near)
         + [shape((tok, width // n), f32)] * (len(even) + 1),
@@ -575,7 +611,7 @@
         functools.partial(
             adam_kernel, (n, per, bs, pad, rows, 1.0 / math.sqrt(tok * parts))
         ),
-        [shape((per, shard), f32)] * 2 + [shape((per, rows, blk), bf16)],
+        [pltpu.VMEM((per, shard), f32)] * 2 + [shape((per, rows, blk), bf16)],
         [SMEM, VMEM] + [VMEM] * (2 * n),
         [VMEM] * 3,
         [
@@ -606,6 +642,8 @@
         VMEM,
         [],
     )(own, *back_terms)
+    (activated,) = flush([activated])
+    first_new, second_new = flush([first_new, second_new])
     return (activated, grad_inputs, weights_out, first_new, second_new)
 
 

time: 88.1 us -> 87.4 us (level)
  local copies, waits for them, and re-layouts: 1.19 us -> 0 us
  Pallas kernels: 21.3 us -> 22.2 us
    unnamed x2 -> x0, local copies, waits for them, and re-layouts: 1.17 us -> none
    pallas_call x11 -> x14, Pallas kernels: 21.3 us -> 22.2 us  [run(): pl.pallas_call(kernel, out_shape=out_shape, in_specs=in_specs, out_specs=...]
  transfers between devices with their start and end apart: 34 -> 34, of which waited for: 16 -> 15; matrix products, arithmetic and copies ran while one was open for 0% -> 0% of each run, Pallas kernels for 13% -> 14%
where the time goes in v4:
time: 87.4 us; the launch traced here: 87.2 us
  waiting for transfers between devices  35 us (40%)
  starting transfers between devices  29.1 us (33%)
  Pallas kernels  22.2 us (25%)
    ppermute x13, waiting for transfers between devices, shift(): lax.ppermute(value, 'mp', [(i, target_of_static(i, step, n)) for i in ran...  22.9 us
    pallas_call x14, Pallas kernels, run(): pl.pallas_call(kernel, out_shape=out_shape, in_specs=in_specs, out_specs=...  22.2 us
    ppermute x13, starting transfers between devices, shift(): lax.ppermute(value, 'mp', [(i, target_of_static(i, step, n)) for i in ran...  16.4 us
    ppermute x21, starting transfers between devices, swap(): return lax.ppermute(value, 'dp', [(i, i ^ bits) for i in range(parts)])  12.7 us
    ppermute x21, waiting for transfers between devices, swap(): return lax.ppermute(value, 'dp', [(i, i ^ bits) for i in range(parts)])  12.1 us
  transfers between devices with their start and end apart: 34, of which 15 were waited for; matrix products, arithmetic and copies ran while one was open for 0% of the time, Pallas kernels for 14%

profile of v4, /device:TPU:0, one launch (start us, length us, event | category | flops | bytes accessed | tf_op | source)
XLA Modules:
  0.0 87.2 jit_solution(15558305949815796946)
XLA Ops:
  0.6 0.9 %shard_map.112.rest_0_ = bf16[28,16,128]{2,1,0:T(8,128)(2,1)S(1)} custom-call(bf16[28,128,128]{2,1,0:T(8,128)(2,1)} %weights.1), custom_call_target="tpu_custom_call" | custom-call | tf_op jit(solution)/shard_map/pallas_call | solution.py:39
  1.6 5.1 %collective-permute-start.2 = (bf16[28,16,128]{2,1,0:T(8,128)(2,1)S(1)}, bf16[28,16,128]{2,1,0:T(8,128)(2,1)S(1)}, u32[]{:S(2)}, u32[]{:S(2)}) collective-permute-start(bf16[28,16,128]{2,1,0:T(8,128)(2,1)S(1)} %shard_map.112.rest_0_), channel_id=1, source_target_pairs={{0,3},{1,2},{2,1},{3,0},{4,7},{5,6},{6,5},{7,4},{8,11},{9,10},{10,... | collective-permute-start | bytes 344072 | tf_op jit(solution)/shard_map/ppermute | solution.py:466
  6.7 0.0 collective-permute-start.1
  6.7 0.6 collective-permute-start
  7.3 0.1 pad_add_fusion.here
  7.4 5.6 %shard_map.110.table = s32[224]{0:T(256)S(1)} custom-call(s32[2]{0:T(128)S(1)} %pad_add_fusion.here, s32[2,80]{1,0:T(2,128)} %bitcast.3, s32[112]{0:T(128)} %moved.1), custom_call_target="tpu_custom_call" | custom-call | tf_op jit(solution)/shard_map/pallas_call | solution.py:39
  13.0 3.3 %collective-permute-done.1.rest_2_ = bf16[28,16,128]{2,1,0:T(8,128)(2,1)S(1)} collective-permute-done((bf16[28,16,128]{2,1,0:T(8,128)(2,1)S(1)}, bf16[28,16,128]{2,1,0:T(8,128)(2,1)S(1)}, u32[]{:S(2)}, u32[]{:S(2)}) %collective-permute-start.1) | collective-permute-done | bytes 114720 | tf_op jit(solution)/shard_map/ppermute | solution.py:466
  16.4 0.0 collective-permute-done.rest_1_
  16.4 0.8 shard_map.113
  17.2 2.5 %collective-permute-start.8 = (bf16[44,16,128]{2,1,0:T(8,128)(2,1)S(1)}, bf16[44,16,128]{2,1,0:T(8,128)(2,1)S(1)}, u32[]{:S(2)}, u32[]{:S(2)}) collective-permute-start(bf16[44,16,128]{2,1,0:T(8,128)(2,1)S(1)} %get-tuple-element.44.rest_0_), channel_id=1, source_target_pairs={{0,24},{4,28},{8,16},{12,20},{16,8},{20,12},{24,0},{28,4},{1,25},{... | collective-permute-start | bytes 540680 | tf_op jit(solution)/shard_map/ppermute | solution.py:462
  19.7 0.5 collective-permute-start.6
  20.2 0.5 collective-permute-start.4
  20.8 0.0 collective-permute-start.3
  20.8 4.4 %collective-permute-done.8.rest_6_ = bf16[44,16,128]{2,1,0:T(8,128)(2,1)S(1)} collective-permute-done((bf16[44,16,128]{2,1,0:T(8,128)(2,1)S(1)}, bf16[44,16,128]{2,1,0:T(8,128)(2,1)S(1)}, u32[]{:S(2)}, u32[]{:S(2)}) %collective-permute-start.8) | collective-permute-done | bytes 180256 | tf_op jit(solution)/shard_map/ppermute | solution.py:462
  25.2 2.4 %collective-permute-done.6.rest_4_ = bf16[44,16,128]{2,1,0:T(8,128)(2,1)S(1)} collective-permute-done((bf16[44,16,128]{2,1,0:T(8,128)(2,1)S(1)}, bf16[44,16,128]{2,1,0:T(8,128)(2,1)S(1)}, u32[]{:S(2)}, u32[]{:S(2)}) %collective-permute-start.6) | collective-permute-done | bytes 180256 | tf_op jit(solution)/shard_map/ppermute | solution.py:462
  27.6 0.0 collective-permute-start.7
  27.7 0.1 collective-permute-done.4.rest_2_
  27.7 0.4 collective-permute-start.5
  28.2 2.2 %shard_map.111 = (f32[2,8,2048]{2,1,0:T(8,128)S(1)}, f32[2,8,2048]{2,1,0:T(8,128)S(1)}, f32[2,8,2048]{2,1,0:T(8,128)S(1)}, f32[2,8,2048]{2,1,0:T(8,128)S(1)}, bf...) custom-call(s32[224]{0:T(256)S(1)} %shard_map.110.table, f32[28,2048]{1,0:T(8,128)} %first.1, ...), custom_call_target="tpu_custom_call" | custom-call | tf_op jit(solution)/shard_map/pallas_call | solution.py:39
  30.4 0.0 collective-permute-done.7.rest_5_
  30.4 0.0 collective-permute-done.5.rest_3_
  30.4 4.7 %shard_map.114 = (bf16[128,2560]{1,0:T(8,128)(2,1)S(1)}, bf16[128,2560]{1,0:T(8,128)(2,1)S(1)}, bf16[1,128,1280]{2,1,0:T(8,128)(2,1)S(1)}, bf16[128,1280]{1,0:T(...) custom-call(s32[2]{0:T(128)S(1)} %pad_add_fusion.here, s32[224]{0:T(256)S(1)} %shard_map.110.table, ...), custom_call_target="tpu_custom_call" | custom-call | tf_op jit(solution)/shard_map/pallas_call | solution.py:39
  35.2 2.1 %shard_map.118 = (bf16[44,16,128]{2,1,0:T(8,128)(2,1)S(1)}, bf16[44,16,128]{2,1,0:T(8,128)(2,1)S(1)}, bf16[44,16,128]{2,1,0:T(8,128)(2,1)S(1)}, bf16[44,16,128]{...) custom-call(s32[2]{0:T(128)S(1)} %pad_add_fusion.here, ...), custom_call_target="tpu_custom_call" | custom-call | tf_op jit(solution)/shard_map/pallas_call | solution.py:39
  37.3 0.2 collective-permute-start.14
  37.5 0.4 collective-permute-start.15
  37.9 0.1 collective-permute-start.16
  38.0 0.4 collective-permute-start.17
  38.4 0.0 collective-permute-start.10
  38.4 0.4 collective-permute-done.14.refs_4_
  38.8 0.3 collective-permute-done.15.refs_5_
  39.0 0.3 collective-permute-done.16.refs_6_
  39.3 0.3 collective-permute-done.17.refs_7_
  39.5 0.2 shard_map.119
  39.7 1.6 %collective-permute-start.18 = (bf16[44,16,128]{2,1,0:T(8,128)(2,1)S(1)}, bf16[44,16,128]{2,1,0:T(8,128)(2,1)S(1)}, u32[]{:S(2)}, u32[]{:S(2)}) collective-permute-start(bf16[44,16,128]{2,1,0:T(8,128)(2,1)S(1)} %get-tuple-element.63), channel_id=1, source_target_pairs={{0,8},{4,12},{8,0},{12,4},{16,24},{20,28},{24,16},{28,20},{1,9},{5... | collective-permute-start | bytes 540680 | tf_op jit(solution)/shard_map/ppermute | solution.py:462
  41.3 0.8 collective-permute-start.19
  42.1 0.9 %collective-permute-start.13 = (bf16[128,1280]{1,0:T(8,128)(2,1)S(1)}, bf16[128,1280]{1,0:T(8,128)(2,1)S(1)}, u32[]{:S(2)}, u32[]{:S(2)}) collective-permute-start(bf16[128,1280]{1,0:T(8,128)(2,1)S(1)} %get-tuple-element.51), channel_id=1, source_target_pairs={{0,1},{1,0},{2,3},{3,2},{4,5},{5,4},{6,7},{7,6},{8,9},{9,8},{10,11... | collective-permute-start | bytes 983048 | tf_op jit(solution)/shard_map/ppermute | solution.py:466
  43.0 1.2 %collective-permute-start.20 = (bf16[44,16,128]{2,1,0:T(8,128)(2,1)S(1)}, bf16[44,16,128]{2,1,0:T(8,128)(2,1)S(1)}, u32[]{:S(2)}, u32[]{:S(2)}) collective-permute-start(bf16[44,16,128]{2,1,0:T(8,128)(2,1)S(1)} %get-tuple-element.65), channel_id=1, source_target_pairs={{0,24},{4,28},{8,16},{12,20},{16,8},{20,12},{24,0},{28,4},{1,25},{... | collective-permute-start | bytes 540680 | tf_op jit(solution)/shard_map/ppermute | solution.py:462
  44.2 4.8 %collective-permute-done.10.refs_1_ = bf16[1,128,1280]{2,1,0:T(8,128)(2,1)S(1)} collective-permute-done((bf16[1,128,1280]{2,1,0:T(8,128)(2,1)S(1)}, bf16[1,128,1280]{2,1,0:T(8,128)(2,1)S(1)}, u32[]{:S(2)}, u32[]{:S(2)}) %collective-permute-start.10) | collective-permute-done | bytes 327712 | tf_op jit(solution)/shard_map/ppermute | solution.py:466
  49.0 2.9 %collective-permute-start.25 = (f32[2,8,2048]{2,1,0:T(8,128)S(1)}, f32[2,8,2048]{2,1,0:T(8,128)S(1)}, u32[]{:S(2)}, u32[]{:S(2)}) collective-permute-start(f32[2,8,2048]{2,1,0:T(8,128)S(1)} %get-tuple-element.72), channel_id=1, source_target_pairs={{0,2},{1,3},{2,0},{3,1},{4,6},{5,7},{6,4},{7,5},{8,10},{9,11},{10,... | collective-permute-start | bytes 393224 | tf_op jit(solution)/shard_map/ppermute | solution.py:466
  51.8 0.0 collective-permute-done.19.rest_2_
  51.8 2.0 %collective-permute-start.26 = (f32[2,8,2048]{2,1,0:T(8,128)S(1)}, f32[2,8,2048]{2,1,0:T(8,128)S(1)}, u32[]{:S(2)}, u32[]{:S(2)}) collective-permute-start(f32[2,8,2048]{2,1,0:T(8,128)S(1)} %get-tuple-element.73), channel_id=1, source_target_pairs={{0,3},{1,2},{2,1},{3,0},{4,7},{5,6},{6,5},{7,4},{8,11},{9,10},{10,... | collective-permute-start | bytes 393224 | tf_op jit(solution)/shard_map/ppermute | solution.py:466
  53.9 0.1 shard_map.116
  53.9 0.0 collective-permute-done.20.rest_3_
  53.9 0.1 collective-permute-start.11
  54.0 0.7 shard_map.120
  54.7 10.6 %collective-permute-done.24.rest_5_ = f32[2,8,2048]{2,1,0:T(8,128)S(1)} collective-permute-done((f32[2,8,2048]{2,1,0:T(8,128)S(1)}, f32[2,8,2048]{2,1,0:T(8,128)S(1)}, u32[]{:S(2)}, u32[]{:S(2)}) %collective-permute-start.24) | collective-permute-done | bytes 131104 | tf_op jit(solution)/shard_map/ppermute | solution.py:466
  65.3 2.7 %collective-permute-start.22 = (bf16[11,16,128]{2,1,0:T(8,128)(2,1)S(1)}, bf16[11,16,128]{2,1,0:T(8,128)(2,1)S(1)}, u32[]{:S(2)}, u32[]{:S(2)}) collective-permute-start(bf16[11,16,128]{2,1,0:T(8,128)(2,1)S(1)} %get-tuple-element.68), channel_id=1, source_target_pairs={{0,2},{1,3},{2,0},{3,1},{4,6},{5,7},{6,4},{7,5},{8,10},{9,11},{10,... | collective-permute-start | bytes 135176 | tf_op jit(solution)/shard_map/ppermute | solution.py:466
  68.0 1.7 %collective-permute-start.23 = (bf16[11,16,128]{2,1,0:T(8,128)(2,1)S(1)}, bf16[11,16,128]{2,1,0:T(8,128)(2,1)S(1)}, u32[]{:S(2)}, u32[]{:S(2)}) collective-permute-start(bf16[11,16,128]{2,1,0:T(8,128)(2,1)S(1)} %get-tuple-element.69), channel_id=1, source_target_pairs={{0,3},{1,2},{2,1},{3,0},{4,7},{5,6},{6,5},{7,4},{8,11},{9,10},{10,... | collective-permute-start | bytes 135176 | tf_op jit(solution)/shard_map/ppermute | solution.py:466
  69.7 0.0 collective-permute-done.21.rest_1_
  69.7 2.7 %collective-permute-done.22.rest_2_ = bf16[11,16,128]{2,1,0:T(8,128)(2,1)S(1)} collective-permute-done((bf16[11,16,128]{2,1,0:T(8,128)(2,1)S(1)}, bf16[11,16,128]{2,1,0:T(8,128)(2,1)S(1)}, u32[]{:S(2)}, u32[]{:S(2)}) %collective-permute-start.22) | collective-permute-done | bytes 45088 | tf_op jit(solution)/shard_map/ppermute | solution.py:466
  72.4 1.5 %collective-permute-done.23.rest_3_ = bf16[11,16,128]{2,1,0:T(8,128)(2,1)S(1)} collective-permute-done((bf16[11,16,128]{2,1,0:T(8,128)(2,1)S(1)}, bf16[11,16,128]{2,1,0:T(8,128)(2,1)S(1)}, u32[]{:S(2)}, u32[]{:S(2)}) %collective-permute-start.23) | collective-permute-done | bytes 45088 | tf_op jit(solution)/shard_map/ppermute | solution.py:466
  73.9 1.0 %shard_map.121 = (f32[20,2048]{1,0:T(8,128)S(1)}, f32[20,2048]{1,0:T(8,128)S(1)}, bf16[20,16,128]{2,1,0:T(8,128)(2,1)S(1)}) custom-call(s32[224]{0:T(256)S(1)} %shard_map.110.table, bf16[20,16,128]{2,1,0:T(8,128)(2,1)S(1)} %get-tuple-element.52.mine, bf16[11,16,128]{2,1,0:T(8,128)(2,1)S(1)} %get-tuple-element.66.rest_0_, ...), custom_call_target="tpu_custom_call" | custom-call | tf_op jit(solution)/shard_map/pallas_call | solution.py:39
  74.9 1.8 %collective-permute-start.32 = (bf16[20,16,128]{2,1,0:T(8,128)(2,1)S(1)}, bf16[20,16,128]{2,1,0:T(8,128)(2,1)S(1)}, u32[]{:S(2)}, u32[]{:S(2)}) collective-permute-start(bf16[20,16,128]{2,1,0:T(8,128)(2,1)S(1)} %get-tuple-element.74.rest_0_), channel_id=1, source_target_pairs={{0,24},{4,28},{8,16},{12,20},{16,8},{20,12},{24,0},{28,4},{1,25},{... | collective-permute-start | bytes 245768 | tf_op jit(solution)/shard_map/ppermute | solution.py:462
  76.7 0.4 collective-permute-start.12
  77.0 1.2 %collective-permute-start.30 = (bf16[20,16,128]{2,1,0:T(8,128)(2,1)S(1)}, bf16[20,16,128]{2,1,0:T(8,128)(2,1)S(1)}, u32[]{:S(2)}, u32[]{:S(2)}) collective-permute-start(bf16[20,16,128]{2,1,0:T(8,128)(2,1)S(1)} %get-tuple-element.74.rest_0_), channel_id=1, source_target_pairs={{0,16},{4,20},{8,24},{12,28},{16,0},{20,4},{24,8},{28,12},{1,17},{... | collective-permute-start | bytes 245768 | tf_op jit(solution)/shard_map/ppermute | solution.py:462
  78.3 0.5 collective-permute-start.28
  78.8 1.5 %collective-permute-done.32.rest_6_ = bf16[20,16,128]{2,1,0:T(8,128)(2,1)S(1)} collective-permute-done((bf16[20,16,128]{2,1,0:T(8,128)(2,1)S(1)}, bf16[20,16,128]{2,1,0:T(8,128)(2,1)S(1)}, u32[]{:S(2)}, u32[]{:S(2)}) %collective-permute-start.32) | collective-permute-done | bytes 81952 | tf_op jit(solution)/shard_map/ppermute | solution.py:462
  80.3 1.2 %collective-permute-done.30.rest_4_ = bf16[20,16,128]{2,1,0:T(8,128)(2,1)S(1)} collective-permute-done((bf16[20,16,128]{2,1,0:T(8,128)(2,1)S(1)}, bf16[20,16,128]{2,1,0:T(8,128)(2,1)S(1)}, u32[]{:S(2)}, u32[]{:S(2)}) %collective-permute-start.30) | collective-permute-done | bytes 81952 | tf_op jit(solution)/shard_map/ppermute | solution.py:462
  81.5 1.2 %collective-permute-done.28.rest_2_ = bf16[20,16,128]{2,1,0:T(8,128)(2,1)S(1)} collective-permute-done((bf16[20,16,128]{2,1,0:T(8,128)(2,1)S(1)}, bf16[20,16,128]{2,1,0:T(8,128)(2,1)S(1)}, u32[]{:S(2)}, u32[]{:S(2)}) %collective-permute-start.28) | collective-permute-done | bytes 81952 | tf_op jit(solution)/shard_map/ppermute | solution.py:462
  82.7 0.5 collective-permute-start.29
  83.2 0.8 shard_map.115
  84.1 0.8 shard_map.123
  84.9 0.8 shard_map.117
  85.7 1.5 %shard_map.122 = bf16[20,128,128]{2,1,0:T(8,128)(2,1)} custom-call(s32[2]{0:T(128)S(1)} %pad_add_fusion.here, bf16[20,16,128]{2,1,0:T(8,128)(2,1)S(1)} %get-tuple-element.74.rest_0_, bf16[20,16,128]{2,1,0:T(8,128)(2,1)S(1)} %collective-permute-done.27.rest_1_, bf16[20,16,128]{2,1,0:T(8,128)(2,1)S(1)} %collective-permute-done.28.rest_2_, ...), custom_call_target="tpu_custom_call" | custom-call | tf_op jit(solution)/shard_map/pallas_call | solution.py:39
  (19 shorter events, 0.0 us)
Async XLA Ops:
  1.6 11.5 %collective-permute-start.2 = (bf16[28,16,128]{2,1,0:T(8,128)(2,1)S(1)}, bf16[28,16,128]{2,1,0:T(8,128)(2,1)S(1)}, u32[]{:S(2)}, u32[]{:S(2)}) collective-permute-start(bf16[28,16,128]{2,1,0:T(8,128)(2,1)S(1)} %shard_map.112.rest_0_), channel_id=1, source_target_pairs={{0,3},{1,2},{2,1},{3,0},{4,7},{5,6},{6,5},{7,4},{8,11},{9,10},{10,... | collective-permute-start | bytes 344072 | tf_op jit(solution)/shard_map/ppermute | solution.py:466
  6.7 9.7 %collective-permute-start.1 = (bf16[28,16,128]{2,1,0:T(8,128)(2,1)S(1)}, bf16[28,16,128]{2,1,0:T(8,128)(2,1)S(1)}, u32[]{:S(2)}, u32[]{:S(2)}) collective-permute-start(bf16[28,16,128]{2,1,0:T(8,128)(2,1)S(1)} %shard_map.112.rest_0_), channel_id=1, source_target_pairs={{0,2},{1,3},{2,0},{3,1},{4,6},{5,7},{6,4},{7,5},{8,10},{9,11},{10,... | collective-permute-start | bytes 344072 | tf_op jit(solution)/shard_map/ppermute | solution.py:466
  6.7 9.7 %collective-permute-start = (bf16[28,16,128]{2,1,0:T(8,128)(2,1)S(1)}, bf16[28,16,128]{2,1,0:T(8,128)(2,1)S(1)}, u32[]{:S(2)}, u32[]{:S(2)}) collective-permute-start(bf16[28,16,128]{2,1,0:T(8,128)(2,1)S(1)} %shard_map.112.rest_0_), channel_id=1, source_target_pairs={{0,1},{1,0},{2,3},{3,2},{4,5},{5,4},{6,7},{7,6},{8,9},{9,8},{10,11... | collective-permute-start | bytes 344072 | tf_op jit(solution)/shard_map/ppermute | solution.py:466
  17.2 8.0 %collective-permute-start.8 = (bf16[44,16,128]{2,1,0:T(8,128)(2,1)S(1)}, bf16[44,16,128]{2,1,0:T(8,128)(2,1)S(1)}, u32[]{:S(2)}, u32[]{:S(2)}) collective-permute-start(bf16[44,16,128]{2,1,0:T(8,128)(2,1)S(1)} %get-tuple-element.44.rest_0_), channel_id=1, source_target_pairs={{0,24},{4,28},{8,16},{12,20},{16,8},{20,12},{24,0},{28,4},{1,25},{... | collective-permute-start | bytes 540680 | tf_op jit(solution)/shard_map/ppermute | solution.py:462
  19.7 7.9 %collective-permute-start.6 = (bf16[44,16,128]{2,1,0:T(8,128)(2,1)S(1)}, bf16[44,16,128]{2,1,0:T(8,128)(2,1)S(1)}, u32[]{:S(2)}, u32[]{:S(2)}) collective-permute-start(bf16[44,16,128]{2,1,0:T(8,128)(2,1)S(1)} %get-tuple-element.44.rest_0_), channel_id=1, source_target_pairs={{0,16},{4,20},{8,24},{12,28},{16,0},{20,4},{24,8},{28,12},{1,17},{... | collective-permute-start | bytes 540680 | tf_op jit(solution)/shard_map/ppermute | solution.py:462
  20.2 7.5 %collective-permute-start.4 = (bf16[44,16,128]{2,1,0:T(8,128)(2,1)S(1)}, bf16[44,16,128]{2,1,0:T(8,128)(2,1)S(1)}, u32[]{:S(2)}, u32[]{:S(2)}) collective-permute-start(bf16[44,16,128]{2,1,0:T(8,128)(2,1)S(1)} %get-tuple-element.44.rest_0_), channel_id=1, source_target_pairs={{0,8},{4,12},{8,0},{12,4},{16,24},{20,28},{24,16},{28,20},{1,9},{5... | collective-permute-start | bytes 540680 | tf_op jit(solution)/shard_map/ppermute | solution.py:462
  20.8 9.6 %collective-permute-start.3 = (bf16[44,16,128]{2,1,0:T(8,128)(2,1)S(1)}, bf16[44,16,128]{2,1,0:T(8,128)(2,1)S(1)}, u32[]{:S(2)}, u32[]{:S(2)}) collective-permute-start(bf16[44,16,128]{2,1,0:T(8,128)(2,1)S(1)} %get-tuple-element.44.rest_0_), channel_id=1, source_target_pairs={{0,4},{4,0},{8,12},{12,8},{16,20},{20,16},{24,28},{28,24},{1,5},{5... | collective-permute-start | bytes 540680 | tf_op jit(solution)/shard_map/ppermute | solution.py:462
  25.2 5.2 %collective-permute-start.9 = (bf16[44,16,128]{2,1,0:T(8,128)(2,1)S(1)}, bf16[44,16,128]{2,1,0:T(8,128)(2,1)S(1)}, u32[]{:S(2)}, u32[]{:S(2)}) collective-permute-start(bf16[44,16,128]{2,1,0:T(8,128)(2,1)S(1)} %collective-permute-done.8.rest_6_), channel_id=1, source_target_pairs={{0,4},{4,0},{8,12},{12,8},{16,20},{20,16},{24,28},{28,24},{1,5},{5... | collective-permute-start | bytes 540680 | tf_op jit(solution)/shard_map/ppermute | solution.py:462
  27.6 2.8 %collective-permute-start.7 = (bf16[44,16,128]{2,1,0:T(8,128)(2,1)S(1)}, bf16[44,16,128]{2,1,0:T(8,128)(2,1)S(1)}, u32[]{:S(2)}, u32[]{:S(2)}) collective-permute-start(bf16[44,16,128]{2,1,0:T(8,128)(2,1)S(1)} %collective-permute-done.6.rest_4_), channel_id=1, source_target_pairs={{0,4},{4,0},{8,12},{12,8},{16,20},{20,16},{24,28},{28,24},{1,5},{5... | collective-permute-start | bytes 540680 | tf_op jit(solution)/shard_map/ppermute | solution.py:462
  27.7 2.7 %collective-permute-start.5 = (bf16[44,16,128]{2,1,0:T(8,128)(2,1)S(1)}, bf16[44,16,128]{2,1,0:T(8,128)(2,1)S(1)}, u32[]{:S(2)}, u32[]{:S(2)}) collective-permute-start(bf16[44,16,128]{2,1,0:T(8,128)(2,1)S(1)} %collective-permute-done.4.rest_2_), channel_id=1, source_target_pairs={{0,4},{4,0},{8,12},{12,8},{16,20},{20,16},{24,28},{28,24},{1,5},{5... | collective-permute-start | bytes 540680 | tf_op jit(solution)/shard_map/ppermute | solution.py:462
  37.3 1.5 %collective-permute-start.14 = (bf16[44,16,128]{2,1,0:T(8,128)(2,1)S(1)}, bf16[44,16,128]{2,1,0:T(8,128)(2,1)S(1)}, u32[]{:S(2)}, u32[]{:S(2)}) collective-permute-start(bf16[44,16,128]{2,1,0:T(8,128)(2,1)S(1)} %get-tuple-element.58), channel_id=1, source_target_pairs={{0,4},{4,0},{8,12},{12,8},{16,20},{20,16},{24,28},{28,24},{1,5},{5... | collective-permute-start | bytes 540680 | tf_op jit(solution)/shard_map/ppermute | solution.py:462
  37.5 1.6 %collective-permute-start.15 = (bf16[44,16,128]{2,1,0:T(8,128)(2,1)S(1)}, bf16[44,16,128]{2,1,0:T(8,128)(2,1)S(1)}, u32[]{:S(2)}, u32[]{:S(2)}) collective-permute-start(bf16[44,16,128]{2,1,0:T(8,128)(2,1)S(1)} %get-tuple-element.59), channel_id=1, source_target_pairs={{0,4},{4,0},{8,12},{12,8},{16,20},{20,16},{24,28},{28,24},{1,5},{5... | collective-permute-start | bytes 540680 | tf_op jit(solution)/shard_map/ppermute | solution.py:462
  37.9 1.4 %collective-permute-start.16 = (bf16[44,16,128]{2,1,0:T(8,128)(2,1)S(1)}, bf16[44,16,128]{2,1,0:T(8,128)(2,1)S(1)}, u32[]{:S(2)}, u32[]{:S(2)}) collective-permute-start(bf16[44,16,128]{2,1,0:T(8,128)(2,1)S(1)} %get-tuple-element.60), channel_id=1, source_target_pairs={{0,4},{4,0},{8,12},{12,8},{16,20},{20,16},{24,28},{28,24},{1,5},{5... | collective-permute-start | bytes 540680 | tf_op jit(solution)/shard_map/ppermute | solution.py:462
  38.0 1.6 %collective-permute-start.17 = (bf16[44,16,128]{2,1,0:T(8,128)(2,1)S(1)}, bf16[44,16,128]{2,1,0:T(8,128)(2,1)S(1)}, u32[]{:S(2)}, u32[]{:S(2)}) collective-permute-start(bf16[44,16,128]{2,1,0:T(8,128)(2,1)S(1)} %get-tuple-element.61), channel_id=1, source_target_pairs={{0,4},{4,0},{8,12},{12,8},{16,20},{20,16},{24,28},{28,24},{1,5},{5... | collective-permute-start | bytes 540680 | tf_op jit(solution)/shard_map/ppermute | solution.py:462
  38.4 10.6 %collective-permute-start.10 = (bf16[1,128,1280]{2,1,0:T(8,128)(2,1)S(1)}, bf16[1,128,1280]{2,1,0:T(8,128)(2,1)S(1)}, u32[]{:S(2)}, u32[]{:S(2)}) collective-permute-start(bf16[1,128,1280]{2,1,0:T(8,128)(2,1)S(1)} %get-tuple-element.48), channel_id=1, source_target_pairs={{0,1},{1,0},{2,3},{3,2},{4,5},{5,4},{6,7},{7,6},{8,9},{9,8},{10,11... | collective-permute-start | bytes 983048 | tf_op jit(solution)/shard_map/ppermute | solution.py:466
  39.7 9.3 %collective-permute-start.18 = (bf16[44,16,128]{2,1,0:T(8,128)(2,1)S(1)}, bf16[44,16,128]{2,1,0:T(8,128)(2,1)S(1)}, u32[]{:S(2)}, u32[]{:S(2)}) collective-permute-start(bf16[44,16,128]{2,1,0:T(8,128)(2,1)S(1)} %get-tuple-element.63), channel_id=1, source_target_pairs={{0,8},{4,12},{8,0},{12,4},{16,24},{20,28},{24,16},{28,20},{1,9},{5... | collective-permute-start | bytes 540680 | tf_op jit(solution)/shard_map/ppermute | solution.py:462
  41.3 10.6 %collective-permute-start.19 = (bf16[44,16,128]{2,1,0:T(8,128)(2,1)S(1)}, bf16[44,16,128]{2,1,0:T(8,128)(2,1)S(1)}, u32[]{:S(2)}, u32[]{:S(2)}) collective-permute-start(bf16[44,16,128]{2,1,0:T(8,128)(2,1)S(1)} %get-tuple-element.64), channel_id=1, source_target_pairs={{0,16},{4,20},{8,24},{12,28},{16,0},{20,4},{24,8},{28,12},{1,17},{... | collective-permute-start | bytes 540680 | tf_op jit(solution)/shard_map/ppermute | solution.py:462
  42.1 36.2 %collective-permute-start.13 = (bf16[128,1280]{1,0:T(8,128)(2,1)S(1)}, bf16[128,1280]{1,0:T(8,128)(2,1)S(1)}, u32[]{:S(2)}, u32[]{:S(2)}) collective-permute-start(bf16[128,1280]{1,0:T(8,128)(2,1)S(1)} %get-tuple-element.51), channel_id=1, source_target_pairs={{0,1},{1,0},{2,3},{3,2},{4,5},{5,4},{6,7},{7,6},{8,9},{9,8},{10,11... | collective-permute-start | bytes 983048 | tf_op jit(solution)/shard_map/ppermute | solution.py:466
  43.0 10.9 %collective-permute-start.20 = (bf16[44,16,128]{2,1,0:T(8,128)(2,1)S(1)}, bf16[44,16,128]{2,1,0:T(8,128)(2,1)S(1)}, u32[]{:S(2)}, u32[]{:S(2)}) collective-permute-start(bf16[44,16,128]{2,1,0:T(8,128)(2,1)S(1)} %get-tuple-element.65), channel_id=1, source_target_pairs={{0,24},{4,28},{8,16},{12,20},{16,8},{20,12},{24,0},{28,4},{1,25},{... | collective-permute-start | bytes 540680 | tf_op jit(solution)/shard_map/ppermute | solution.py:462
  49.0 16.3 %collective-permute-start.24 = (f32[2,8,2048]{2,1,0:T(8,128)S(1)}, f32[2,8,2048]{2,1,0:T(8,128)S(1)}, u32[]{:S(2)}, u32[]{:S(2)}) collective-permute-start(f32[2,8,2048]{2,1,0:T(8,128)S(1)} %get-tuple-element.71), channel_id=1, source_target_pairs={{0,1},{1,0},{2,3},{3,2},{4,5},{5,4},{6,7},{7,6},{8,9},{9,8},{10,11... | collective-permute-start | bytes 393224 | tf_op jit(solution)/shard_map/ppermute | solution.py:466
  49.0 16.3 %collective-permute-start.25 = (f32[2,8,2048]{2,1,0:T(8,128)S(1)}, f32[2,8,2048]{2,1,0:T(8,128)S(1)}, u32[]{:S(2)}, u32[]{:S(2)}) collective-permute-start(f32[2,8,2048]{2,1,0:T(8,128)S(1)} %get-tuple-element.72), channel_id=1, source_target_pairs={{0,2},{1,3},{2,0},{3,1},{4,6},{5,7},{6,4},{7,5},{8,10},{9,11},{10,... | collective-permute-start | bytes 393224 | tf_op jit(solution)/shard_map/ppermute | solution.py:466
  51.8 16.2 %collective-permute-start.26 = (f32[2,8,2048]{2,1,0:T(8,128)S(1)}, f32[2,8,2048]{2,1,0:T(8,128)S(1)}, u32[]{:S(2)}, u32[]{:S(2)}) collective-permute-start(f32[2,8,2048]{2,1,0:T(8,128)S(1)} %get-tuple-element.73), channel_id=1, source_target_pairs={{0,3},{1,2},{2,1},{3,0},{4,7},{5,6},{6,5},{7,4},{8,11},{9,10},{10,... | collective-permute-start | bytes 393224 | tf_op jit(solution)/shard_map/ppermute | solution.py:466
  53.9 28.8 %collective-permute-start.11 = (bf16[64,1280]{1,0:T(8,128)(2,1)S(1)}, bf16[64,1280]{1,0:T(8,128)(2,1)S(1)}, u32[]{:S(2)}, u32[]{:S(2)}) collective-permute-start(bf16[64,1280]{1,0:T(8,128)(2,1)S(1)} %get-tuple-element.49), channel_id=1, source_target_pairs={{0,2},{1,3},{2,0},{3,1},{4,6},{5,7},{6,4},{7,5},{8,10},{9,11},{10,... | collective-permute-start | bytes 491528 | tf_op jit(solution)/shard_map/ppermute | solution.py:466
  65.3 4.4 %collective-permute-start.21 = (bf16[11,16,128]{2,1,0:T(8,128)(2,1)S(1)}, bf16[11,16,128]{2,1,0:T(8,128)(2,1)S(1)}, u32[]{:S(2)}, u32[]{:S(2)}) collective-permute-start(bf16[11,16,128]{2,1,0:T(8,128)(2,1)S(1)} %get-tuple-element.67), channel_id=1, source_target_pairs={{0,1},{1,0},{2,3},{3,2},{4,5},{5,4},{6,7},{7,6},{8,9},{9,8},{10,11... | collective-permute-start | bytes 135176 | tf_op jit(solution)/shard_map/ppermute | solution.py:466
  65.3 7.1 %collective-permute-start.22 = (bf16[11,16,128]{2,1,0:T(8,128)(2,1)S(1)}, bf16[11,16,128]{2,1,0:T(8,128)(2,1)S(1)}, u32[]{:S(2)}, u32[]{:S(2)}) collective-permute-start(bf16[11,16,128]{2,1,0:T(8,128)(2,1)S(1)} %get-tuple-element.68), channel_id=1, source_target_pairs={{0,2},{1,3},{2,0},{3,1},{4,6},{5,7},{6,4},{7,5},{8,10},{9,11},{10,... | collective-permute-start | bytes 135176 | tf_op jit(solution)/shard_map/ppermute | solution.py:466
  68.0 5.8 %collective-permute-start.23 = (bf16[11,16,128]{2,1,0:T(8,128)(2,1)S(1)}, bf16[11,16,128]{2,1,0:T(8,128)(2,1)S(1)}, u32[]{:S(2)}, u32[]{:S(2)}) collective-permute-start(bf16[11,16,128]{2,1,0:T(8,128)(2,1)S(1)} %get-tuple-element.69), channel_id=1, source_target_pairs={{0,3},{1,2},{2,1},{3,0},{4,7},{5,6},{6,5},{7,4},{8,11},{9,10},{10,... | collective-permute-start | bytes 135176 | tf_op jit(solution)/shard_map/ppermute | solution.py:466
  74.9 5.4 %collective-permute-start.32 = (bf16[20,16,128]{2,1,0:T(8,128)(2,1)S(1)}, bf16[20,16,128]{2,1,0:T(8,128)(2,1)S(1)}, u32[]{:S(2)}, u32[]{:S(2)}) collective-permute-start(bf16[20,16,128]{2,1,0:T(8,128)(2,1)S(1)} %get-tuple-element.74.rest_0_), channel_id=1, source_target_pairs={{0,24},{4,28},{8,16},{12,20},{16,8},{20,12},{24,0},{28,4},{1,25},{... | collective-permute-start | bytes 245768 | tf_op jit(solution)/shard_map/ppermute | solution.py:462
  76.7 8.2 %collective-permute-start.12 = (bf16[64,1280]{1,0:T(8,128)(2,1)S(1)}, bf16[64,1280]{1,0:T(8,128)(2,1)S(1)}, u32[]{:S(2)}, u32[]{:S(2)}) collective-permute-start(bf16[64,1280]{1,0:T(8,128)(2,1)S(1)} %get-tuple-element.50), channel_id=1, source_target_pairs={{0,2},{1,3},{2,0},{3,1},{4,6},{5,7},{6,4},{7,5},{8,10},{9,11},{10,... | collective-permute-start | bytes 491528 | tf_op jit(solution)/shard_map/ppermute | solution.py:466
  77.0 4.4 %collective-permute-start.30 = (bf16[20,16,128]{2,1,0:T(8,128)(2,1)S(1)}, bf16[20,16,128]{2,1,0:T(8,128)(2,1)S(1)}, u32[]{:S(2)}, u32[]{:S(2)}) collective-permute-start(bf16[20,16,128]{2,1,0:T(8,128)(2,1)S(1)} %get-tuple-element.74.rest_0_), channel_id=1, source_target_pairs={{0,16},{4,20},{8,24},{12,28},{16,0},{20,4},{24,8},{28,12},{1,17},{... | collective-permute-start | bytes 245768 | tf_op jit(solution)/shard_map/ppermute | solution.py:462
  78.3 4.4 %collective-permute-start.28 = (bf16[20,16,128]{2,1,0:T(8,128)(2,1)S(1)}, bf16[20,16,128]{2,1,0:T(8,128)(2,1)S(1)}, u32[]{:S(2)}, u32[]{:S(2)}) collective-permute-start(bf16[20,16,128]{2,1,0:T(8,128)(2,1)S(1)} %get-tuple-element.74.rest_0_), channel_id=1, source_target_pairs={{0,8},{4,12},{8,0},{12,4},{16,24},{20,28},{24,16},{28,20},{1,9},{5... | collective-permute-start | bytes 245768 | tf_op jit(solution)/shard_map/ppermute | solution.py:462
  80.3 5.4 %collective-permute-start.27 = (bf16[20,16,128]{2,1,0:T(8,128)(2,1)S(1)}, bf16[20,16,128]{2,1,0:T(8,128)(2,1)S(1)}, u32[]{:S(2)}, u32[]{:S(2)}) collective-permute-start(bf16[20,16,128]{2,1,0:T(8,128)(2,1)S(1)} %get-tuple-element.74.rest_0_), channel_id=1, source_target_pairs={{0,4},{4,0},{8,12},{12,8},{16,20},{20,16},{24,28},{28,24},{1,5},{5... | collective-permute-start | bytes 245768 | tf_op jit(solution)/shard_map/ppermute | solution.py:462
  81.5 4.2 %collective-permute-start.33 = (bf16[20,16,128]{2,1,0:T(8,128)(2,1)S(1)}, bf16[20,16,128]{2,1,0:T(8,128)(2,1)S(1)}, u32[]{:S(2)}, u32[]{:S(2)}) collective-permute-start(bf16[20,16,128]{2,1,0:T(8,128)(2,1)S(1)} %collective-permute-done.32.rest_6_), channel_id=1, source_target_pairs={{0,4},{4,0},{8,12},{12,8},{16,20},{20,16},{24,28},{28,24},{1,5},{5... | collective-permute-start | bytes 245768 | tf_op jit(solution)/shard_map/ppermute | solution.py:462
  82.7 3.0 %collective-permute-start.31 = (bf16[20,16,128]{2,1,0:T(8,128)(2,1)S(1)}, bf16[20,16,128]{2,1,0:T(8,128)(2,1)S(1)}, u32[]{:S(2)}, u32[]{:S(2)}) collective-permute-start(bf16[20,16,128]{2,1,0:T(8,128)(2,1)S(1)} %collective-permute-done.30.rest_4_), channel_id=1, source_target_pairs={{0,4},{4,0},{8,12},{12,8},{16,20},{20,16},{24,28},{28,24},{1,5},{5... | collective-permute-start | bytes 245768 | tf_op jit(solution)/shard_map/ppermute | solution.py:462
  82.7 3.0 %collective-permute-start.29 = (bf16[20,16,128]{2,1,0:T(8,128)(2,1)S(1)}, bf16[20,16,128]{2,1,0:T(8,128)(2,1)S(1)}, u32[]{:S(2)}, u32[]{:S(2)}) collective-permute-start(bf16[20,16,128]{2,1,0:T(8,128)(2,1)S(1)} %collective-permute-done.28.rest_2_), channel_id=1, source_target_pairs={{0,4},{4,0},{8,12},{12,8},{16,20},{20,16},{24,28},{28,24},{1,5},{5... | collective-permute-start | bytes 245768 | tf_op jit(solution)/shard_map/ppermute | solution.py:462

commit v5 on v4

--- a/solution.py
+++ b/solution.py
@@ -98,8 +98,14 @@
     return rank, tuple(new)
 
 
-def plan_kernel(cfg, here, coords, moved, table, src):
+def plan_kernel(cfg, here, coords, moved, *rest):
     n, per, cap, ms, bs, bw, pad = cfg
+    sources, table, targets, src, sems = rest[:4], rest[4], rest[5:9], rest[9], rest[10]
+    copies = [
+        pltpu.make_async_copy(sources[i], targets[i], sems.at[i]) for i in range(len(sources))
+    ]
+    for copy in copies:
+        copy.start()
     total = n * per
     slots = n * bs
     share, grad, moment = 3 * slots, 3 * slots + per, 3 * slots + 2 * per
@@ -159,30 +165,19 @@
 
         lax.fori_loop(0, per, new_slot, zeros, unroll=math.gcd(per, 4))
 
-
-def pack_kernel(cfg, table, first, second, tokens, cotangent, *rest):
+    for copy in copies:
+        copy.wait()
+
+
+def pack_kernel(cfg, table, first, second, *packs):
     n, ms, pad, out = cfg
-    packs = rest[:n]
-    tokens_out, cotangent_out, first_in, second_in, sems = rest[n:]
-    copies = [
-        pltpu.make_async_copy(first, first_in, sems.at[0]),
-        pltpu.make_async_copy(second, second_in, sems.at[1]),
-        pltpu.make_async_copy(tokens, tokens_out, sems.at[2]),
-        pltpu.make_async_copy(cotangent, cotangent_out, sems.at[3]),
-    ]
-    for copy in copies:
-        copy.start()
-    copies[0].wait()
-    copies[1].wait()
     for s in range(n):
         for k in range(ms):
             row = table[out + s * ms + k]
-            packs[s][0, k : k + 1, :] = first_in[pl.ds(row, 1), :]
-            packs[s][1, k : k + 1, :] = second_in[pl.ds(row, 1), :]
+            packs[s][0, k : k + 1, :] = first[pl.ds(row, 1), :]
+            packs[s][1, k : k + 1, :] = second[pl.ds(row, 1), :]
         if pad > ms:
             packs[s][:, ms:pad, :] = jnp.zeros((2, pad - ms, first.shape[1]), jnp.float32)
-    copies[2].wait()
-    copies[3].wait()
 
 
 def share_kernel(weights, out, sem):
@@ -501,13 +496,14 @@
     shares = [share] + [shift(share, s, n) for s in range(1, n)]
 
     out = 3 * slots + 3 * per
-    table = call(
+    big = (old_first, old_second, tokens_in, cotangent)
+    table, first, second, tokens, cotangents = call(
         functools.partial(plan_kernel, (n, per, cap, ms, bs, bw, pad)),
-        shape((out + n * ms + 4,), jnp.int32),
-        [SMEM] * 3,
-        SMEM,
-        [pltpu.SMEM((total + 8,), jnp.int32)],
-    )(here, in_hbm(new_coords.T), in_hbm(moved_to))
+        [shape((out + n * ms + 4,), jnp.int32)] + [shape(x.shape, x.dtype) for x in big],
+        [SMEM] * 3 + [ANY] * 4,
+        [SMEM] + [VMEM] * 4,
+        [pltpu.SMEM((total + 8,), jnp.int32), pltpu.SemaphoreType.DMA((4,))],
+    )(here, *[in_hbm(x) for x in (new_coords.T, moved_to, *big)])
 
     picked, mine = call(
         functools.partial(select_kernel, (n, per, cap, bs)),
@@ -523,20 +519,13 @@
         gathered = lax.all_gather(picked, "dp", axis=0)
         pieces = [gathered.transpose(1, 0, 2, 3).reshape(slots, blk, blk)]
 
-    packed = call(
+    packs = call(
         functools.partial(pack_kernel, (n, ms, pad, out)),
-        [shape((2, pad, shard), f32)] * n
-        + [shape(tokens_in.shape, bf16), shape(cotangent.shape, bf16)],
-        [SMEM] + [ANY] * 4,
-        [VMEM] * (n + 2),
-        [
-            pltpu.VMEM(old_first.shape, f32),
-            pltpu.VMEM(old_second.shape, f32),
-            pltpu.SemaphoreType.DMA((4,)),
-        ],
-    )(table, *[in_hbm(x) for x in (old_first, old_second, tokens_in, cotangent)])
-    packs = packed[:n]
-    tokens, cotangents = packed[n:]
+        [shape((2, pad, shard), f32)] * n,
+        [SMEM] + [VMEM] * 2,
+        [VMEM] * n,
+        [],
+    )(table, first, second)
     moments = [packs[0]] + [shift(packs[s], s, n) for s in range(1, n)]
 
     odd, near, even = split_steps(n)

time: 87.4 us -> 87 us (level)
  Pallas kernels: 22.2 us -> 20.7 us
  starting transfers between devices: 29.1 us -> 30 us
    pallas_call x14, Pallas kernels: 22.2 us -> 20.7 us  [run(): pl.pallas_call(kernel, out_shape=out_shape, in_specs=in_specs, out_specs=...]
    ppermute x21, waiting for transfers between devices: 12.1 us -> 13.2 us  [swap(): return lax.ppermute(value, 'dp', [(i, i ^ bits) for i in range(parts)])]
    ppermute x13, starting transfers between devices: 16.4 us -> 17.3 us  [shift(): lax.ppermute(value, 'mp', [(i, target_of_static(i, step, n)) for i in ran...]
  transfers between devices with their start and end apart: 34 -> 34, of which waited for: 15 -> 17; matrix products, arithmetic and copies ran while one was open for 0% -> 0% of each run, Pallas kernels for 14% -> 12%
where the time goes in v5:
time: 87 us; the launch traced here: 86.9 us
  waiting for transfers between devices  35.3 us (41%)
  starting transfers between devices  30 us (34%)
  Pallas kernels  20.7 us (24%)
    ppermute x13, waiting for transfers between devices, shift(): lax.ppermute(value, 'mp', [(i, target_of_static(i, step, n)) for i in ran...  22.1 us
    pallas_call x14, Pallas kernels, run(): pl.pallas_call(kernel, out_shape=out_shape, in_specs=in_specs, out_specs=...  20.7 us
    ppermute x13, starting transfers between devices, shift(): lax.ppermute(value, 'mp', [(i, target_of_static(i, step, n)) for i in ran...  17.3 us
    ppermute x21, waiting for transfers between devices, swap(): return lax.ppermute(value, 'dp', [(i, i ^ bits) for i in range(parts)])  13.2 us
    ppermute x21, starting transfers between devices, swap(): return lax.ppermute(value, 'dp', [(i, i ^ bits) for i in range(parts)])  12.7 us
  transfers between devices with their start and end apart: 34, of which 17 were waited for; matrix products, arithmetic and copies ran while one was open for 0% of the time, Pallas kernels for 12%

profile of v5, /device:TPU:0, one launch (start us, length us, event | category | flops | bytes accessed | tf_op | source)
XLA Modules:
  0.0 86.9 jit_solution(784397296411046298)
XLA Ops:
  0.6 0.9 %shard_map.111.rest_0_ = bf16[28,16,128]{2,1,0:T(8,128)(2,1)S(1)} custom-call(bf16[28,128,128]{2,1,0:T(8,128)(2,1)} %weights.1), custom_call_target="tpu_custom_call" | custom-call | tf_op jit(solution)/shard_map/pallas_call | solution.py:39
  1.6 5.1 %collective-permute-start.2 = (bf16[28,16,128]{2,1,0:T(8,128)(2,1)S(1)}, bf16[28,16,128]{2,1,0:T(8,128)(2,1)S(1)}, u32[]{:S(2)}, u32[]{:S(2)}) collective-permute-start(bf16[28,16,128]{2,1,0:T(8,128)(2,1)S(1)} %shard_map.111.rest_0_), channel_id=1, source_target_pairs={{0,3},{1,2},{2,1},{3,0},{4,7},{5,6},{6,5},{7,4},{8,11},{9,10},{10,... | collective-permute-start | bytes 344072 | tf_op jit(solution)/shard_map/ppermute | solution.py:461
  6.7 0.0 collective-permute-start.1
  6.7 0.6 collective-permute-start
  7.3 0.1 pad_add_fusion.here
  7.4 5.6 %shard_map.110 = (s32[224]{0:T(256)S(1)}, f32[28,2048]{1,0:T(8,128)S(1)}, f32[28,2048]{1,0:T(8,128)S(1)}, bf16[128,5120]{1,0:T(8,128)(2,1)S(1)}, bf16[128,2560]{1,0:T(8,128)(2,1)S(1)}) custom-call(s32[2]{0:T(128)S(1)} %pad_add_fusion.here, s32[2,80]{1,0:T(2,128)} %bitcast.3, s32[112]{0:T(128)} %moved.1, f32[28,2048]{1,0:T(8,128)} %rest_0_.1, ...), custom_call_target="tpu_custom_call" | custom-call | tf_op jit(solution)/shard_map/pallas_call | solution.py:39
  13.1 3.3 %collective-permute-done.1.rest_2_ = bf16[28,16,128]{2,1,0:T(8,128)(2,1)S(1)} collective-permute-done((bf16[28,16,128]{2,1,0:T(8,128)(2,1)S(1)}, bf16[28,16,128]{2,1,0:T(8,128)(2,1)S(1)}, u32[]{:S(2)}, u32[]{:S(2)}) %collective-permute-start.1) | collective-permute-done | bytes 114720 | tf_op jit(solution)/shard_map/ppermute | solution.py:461
  16.4 0.0 collective-permute-done.rest_1_
  16.4 0.8 shard_map.112
  17.2 2.5 %collective-permute-start.8 = (bf16[44,16,128]{2,1,0:T(8,128)(2,1)S(1)}, bf16[44,16,128]{2,1,0:T(8,128)(2,1)S(1)}, u32[]{:S(2)}, u32[]{:S(2)}) collective-permute-start(bf16[44,16,128]{2,1,0:T(8,128)(2,1)S(1)} %get-tuple-element.48.rest_0_), channel_id=1, source_target_pairs={{0,24},{4,28},{8,16},{12,20},{16,8},{20,12},{24,0},{28,4},{1,25},{... | collective-permute-start | bytes 540680 | tf_op jit(solution)/shard_map/ppermute | solution.py:457
  19.7 0.5 collective-permute-start.6
  20.2 0.5 collective-permute-start.4
  20.8 0.0 collective-permute-start.3
  20.8 4.4 %collective-permute-done.8.rest_6_ = bf16[44,16,128]{2,1,0:T(8,128)(2,1)S(1)} collective-permute-done((bf16[44,16,128]{2,1,0:T(8,128)(2,1)S(1)}, bf16[44,16,128]{2,1,0:T(8,128)(2,1)S(1)}, u32[]{:S(2)}, u32[]{:S(2)}) %collective-permute-start.8) | collective-permute-done | bytes 180256 | tf_op jit(solution)/shard_map/ppermute | solution.py:457
  25.2 2.4 %collective-permute-done.6.rest_4_ = bf16[44,16,128]{2,1,0:T(8,128)(2,1)S(1)} collective-permute-done((bf16[44,16,128]{2,1,0:T(8,128)(2,1)S(1)}, bf16[44,16,128]{2,1,0:T(8,128)(2,1)S(1)}, u32[]{:S(2)}, u32[]{:S(2)}) %collective-permute-start.6) | collective-permute-done | bytes 180256 | tf_op jit(solution)/shard_map/ppermute | solution.py:457
  27.6 0.0 collective-permute-start.7
  27.7 0.1 collective-permute-done.4.rest_2_
  27.7 0.4 collective-permute-start.5
  28.2 0.0 collective-permute-done.3.rest_1_
  28.2 0.9 %collective-permute-done.7.rest_5_ = bf16[44,16,128]{2,1,0:T(8,128)(2,1)S(1)} collective-permute-done((bf16[44,16,128]{2,1,0:T(8,128)(2,1)S(1)}, bf16[44,16,128]{2,1,0:T(8,128)(2,1)S(1)}, u32[]{:S(2)}, u32[]{:S(2)}) %collective-permute-start.7) | collective-permute-done | bytes 180256 | tf_op jit(solution)/shard_map/ppermute | solution.py:457
  29.1 0.3 collective-permute-done.5.rest_3_
  29.3 4.7 %shard_map.113 = (bf16[128,2560]{1,0:T(8,128)(2,1)S(1)}, bf16[128,2560]{1,0:T(8,128)(2,1)S(1)}, bf16[1,128,1280]{2,1,0:T(8,128)(2,1)S(1)}, bf16[128,1280]{1,0:T(...) custom-call(s32[2]{0:T(128)S(1)} %pad_add_fusion.here, s32[224]{0:T(256)S(1)} %get-tuple-element.45.table, ...), custom_call_target="tpu_custom_call" | custom-call | tf_op jit(solution)/shard_map/pallas_call | solution.py:39
  34.1 2.1 %shard_map.117 = (bf16[44,16,128]{2,1,0:T(8,128)(2,1)S(1)}, bf16[44,16,128]{2,1,0:T(8,128)(2,1)S(1)}, bf16[44,16,128]{2,1,0:T(8,128)(2,1)S(1)}, bf16[44,16,128]{...) custom-call(s32[2]{0:T(128)S(1)} %pad_add_fusion.here, ...), custom_call_target="tpu_custom_call" | custom-call | tf_op jit(solution)/shard_map/pallas_call | solution.py:39
  36.2 0.3 collective-permute-start.14
  36.5 0.3 collective-permute-start.15
  36.7 0.3 collective-permute-start.16
  37.0 0.3 collective-permute-start.17
  37.3 0.0 collective-permute-start.10
  37.3 0.4 collective-permute-done.14.refs_4_
  37.7 0.3 collective-permute-done.15.refs_5_
  37.9 0.3 collective-permute-done.16.refs_6_
  38.2 0.3 collective-permute-done.17.refs_7_
  38.4 0.2 shard_map.118
  38.6 1.6 %collective-permute-start.18 = (bf16[44,16,128]{2,1,0:T(8,128)(2,1)S(1)}, bf16[44,16,128]{2,1,0:T(8,128)(2,1)S(1)}, u32[]{:S(2)}, u32[]{:S(2)}) collective-permute-start(bf16[44,16,128]{2,1,0:T(8,128)(2,1)S(1)} %get-tuple-element.67), channel_id=1, source_target_pairs={{0,8},{4,12},{8,0},{12,4},{16,24},{20,28},{24,16},{28,20},{1,9},{5... | collective-permute-start | bytes 540680 | tf_op jit(solution)/shard_map/ppermute | solution.py:457
  40.1 0.8 collective-permute-start.19
  41.0 0.9 %collective-permute-start.13 = (bf16[128,1280]{1,0:T(8,128)(2,1)S(1)}, bf16[128,1280]{1,0:T(8,128)(2,1)S(1)}, u32[]{:S(2)}, u32[]{:S(2)}) collective-permute-start(bf16[128,1280]{1,0:T(8,128)(2,1)S(1)} %get-tuple-element.55), channel_id=1, source_target_pairs={{0,1},{1,0},{2,3},{3,2},{4,5},{5,4},{6,7},{7,6},{8,9},{9,8},{10,11... | collective-permute-start | bytes 983048 | tf_op jit(solution)/shard_map/ppermute | solution.py:461
  41.9 1.2 %collective-permute-start.20 = (bf16[44,16,128]{2,1,0:T(8,128)(2,1)S(1)}, bf16[44,16,128]{2,1,0:T(8,128)(2,1)S(1)}, u32[]{:S(2)}, u32[]{:S(2)}) collective-permute-start(bf16[44,16,128]{2,1,0:T(8,128)(2,1)S(1)} %get-tuple-element.69), channel_id=1, source_target_pairs={{0,24},{4,28},{8,16},{12,20},{16,8},{20,12},{24,0},{28,4},{1,25},{... | collective-permute-start | bytes 540680 | tf_op jit(solution)/shard_map/ppermute | solution.py:457
  43.0 0.7 shard_map.120
  43.8 4.1 %collective-permute-done.10.refs_1_ = bf16[1,128,1280]{2,1,0:T(8,128)(2,1)S(1)} collective-permute-done((bf16[1,128,1280]{2,1,0:T(8,128)(2,1)S(1)}, bf16[1,128,1280]{2,1,0:T(8,128)(2,1)S(1)}, u32[]{:S(2)}, u32[]{:S(2)}) %collective-permute-start.10) | collective-permute-done | bytes 327712 | tf_op jit(solution)/shard_map/ppermute | solution.py:461
  47.8 0.0 collective-permute-start.24
  47.8 2.9 %collective-permute-start.25 = (f32[2,8,2048]{2,1,0:T(8,128)S(1)}, f32[2,8,2048]{2,1,0:T(8,128)S(1)}, u32[]{:S(2)}, u32[]{:S(2)}) collective-permute-start(f32[2,8,2048]{2,1,0:T(8,128)S(1)} %get-tuple-element.78), channel_id=1, source_target_pairs={{0,2},{1,3},{2,0},{3,1},{4,6},{5,7},{6,4},{7,5},{8,10},{9,11},{10,... | collective-permute-start | bytes 393224 | tf_op jit(solution)/shard_map/ppermute | solution.py:461
  50.7 2.0 %collective-permute-start.26 = (f32[2,8,2048]{2,1,0:T(8,128)S(1)}, f32[2,8,2048]{2,1,0:T(8,128)S(1)}, u32[]{:S(2)}, u32[]{:S(2)}) collective-permute-start(f32[2,8,2048]{2,1,0:T(8,128)S(1)} %get-tuple-element.79), channel_id=1, source_target_pairs={{0,3},{1,2},{2,1},{3,0},{4,7},{5,6},{6,5},{7,4},{8,11},{9,10},{10,... | collective-permute-start | bytes 393224 | tf_op jit(solution)/shard_map/ppermute | solution.py:461
  52.7 0.1 shard_map.115
  52.8 0.1 collective-permute-start.11
  52.9 0.7 shard_map.119
  53.6 10.7 %collective-permute-done.24.rest_5_ = f32[2,8,2048]{2,1,0:T(8,128)S(1)} collective-permute-done((f32[2,8,2048]{2,1,0:T(8,128)S(1)}, f32[2,8,2048]{2,1,0:T(8,128)S(1)}, u32[]{:S(2)}, u32[]{:S(2)}) %collective-permute-start.24) | collective-permute-done | bytes 131104 | tf_op jit(solution)/shard_map/ppermute | solution.py:461
  64.3 2.5 %collective-permute-start.22 = (bf16[11,16,128]{2,1,0:T(8,128)(2,1)S(1)}, bf16[11,16,128]{2,1,0:T(8,128)(2,1)S(1)}, u32[]{:S(2)}, u32[]{:S(2)}) collective-permute-start(bf16[11,16,128]{2,1,0:T(8,128)(2,1)S(1)} %get-tuple-element.72), channel_id=1, source_target_pairs={{0,2},{1,3},{2,0},{3,1},{4,6},{5,7},{6,4},{7,5},{8,10},{9,11},{10,... | collective-permute-start | bytes 135176 | tf_op jit(solution)/shard_map/ppermute | solution.py:461
  66.8 1.9 %collective-permute-start.23 = (bf16[11,16,128]{2,1,0:T(8,128)(2,1)S(1)}, bf16[11,16,128]{2,1,0:T(8,128)(2,1)S(1)}, u32[]{:S(2)}, u32[]{:S(2)}) collective-permute-start(bf16[11,16,128]{2,1,0:T(8,128)(2,1)S(1)} %get-tuple-element.73), channel_id=1, source_target_pairs={{0,3},{1,2},{2,1},{3,0},{4,7},{5,6},{6,5},{7,4},{8,11},{9,10},{10,... | collective-permute-start | bytes 135176 | tf_op jit(solution)/shard_map/ppermute | solution.py:461
  68.7 0.0 collective-permute-done.21.rest_1_
  68.8 2.8 %collective-permute-done.22.rest_2_ = bf16[11,16,128]{2,1,0:T(8,128)(2,1)S(1)} collective-permute-done((bf16[11,16,128]{2,1,0:T(8,128)(2,1)S(1)}, bf16[11,16,128]{2,1,0:T(8,128)(2,1)S(1)}, u32[]{:S(2)}, u32[]{:S(2)}) %collective-permute-start.22) | collective-permute-done | bytes 45088 | tf_op jit(solution)/shard_map/ppermute | solution.py:461
  71.6 1.1 %collective-permute-done.23.rest_3_ = bf16[11,16,128]{2,1,0:T(8,128)(2,1)S(1)} collective-permute-done((bf16[11,16,128]{2,1,0:T(8,128)(2,1)S(1)}, bf16[11,16,128]{2,1,0:T(8,128)(2,1)S(1)}, u32[]{:S(2)}, u32[]{:S(2)}) %collective-permute-start.23) | collective-permute-done | bytes 45088 | tf_op jit(solution)/shard_map/ppermute | solution.py:461
  72.7 1.0 %shard_map.121 = (f32[20,2048]{1,0:T(8,128)S(1)}, f32[20,2048]{1,0:T(8,128)S(1)}, bf16[20,16,128]{2,1,0:T(8,128)(2,1)S(1)}) custom-call(s32[224]{0:T(256)S(1)} %get-tuple-element.45.table, bf16[20,16,128]{2,1,0:T(8,128)(2,1)S(1)} %get-tuple-element.56.mine, bf16[11,16,128]{2,1,0:T(8,128)(2,1)S(1)} %get-tuple-element.70.rest_0_, ...), custom_call_target="tpu_custom_call" | custom-call | tf_op jit(solution)/shard_map/pallas_call | solution.py:39
  73.7 1.8 %collective-permute-start.32 = (bf16[20,16,128]{2,1,0:T(8,128)(2,1)S(1)}, bf16[20,16,128]{2,1,0:T(8,128)(2,1)S(1)}, u32[]{:S(2)}, u32[]{:S(2)}) collective-permute-start(bf16[20,16,128]{2,1,0:T(8,128)(2,1)S(1)} %get-tuple-element.80.rest_0_), channel_id=1, source_target_pairs={{0,24},{4,28},{8,16},{12,20},{16,8},{20,12},{24,0},{28,4},{1,25},{... | collective-permute-start | bytes 245768 | tf_op jit(solution)/shard_map/ppermute | solution.py:457
  75.5 1.3 %collective-permute-start.12 = (bf16[64,1280]{1,0:T(8,128)(2,1)S(1)}, bf16[64,1280]{1,0:T(8,128)(2,1)S(1)}, u32[]{:S(2)}, u32[]{:S(2)}) collective-permute-start(bf16[64,1280]{1,0:T(8,128)(2,1)S(1)} %get-tuple-element.54), channel_id=1, source_target_pairs={{0,2},{1,3},{2,0},{3,1},{4,6},{5,7},{6,4},{7,5},{8,10},{9,11},{10,... | collective-permute-start | bytes 491528 | tf_op jit(solution)/shard_map/ppermute | solution.py:461
  76.7 1.2 %collective-permute-start.30 = (bf16[20,16,128]{2,1,0:T(8,128)(2,1)S(1)}, bf16[20,16,128]{2,1,0:T(8,128)(2,1)S(1)}, u32[]{:S(2)}, u32[]{:S(2)}) collective-permute-start(bf16[20,16,128]{2,1,0:T(8,128)(2,1)S(1)} %get-tuple-element.80.rest_0_), channel_id=1, source_target_pairs={{0,16},{4,20},{8,24},{12,28},{16,0},{20,4},{24,8},{28,12},{1,17},{... | collective-permute-start | bytes 245768 | tf_op jit(solution)/shard_map/ppermute | solution.py:457
  78.0 0.5 collective-permute-start.28
  78.5 0.6 collective-permute-done.32.rest_6_
  79.1 2.1 %collective-permute-done.30.rest_4_ = bf16[20,16,128]{2,1,0:T(8,128)(2,1)S(1)} collective-permute-done((bf16[20,16,128]{2,1,0:T(8,128)(2,1)S(1)}, bf16[20,16,128]{2,1,0:T(8,128)(2,1)S(1)}, u32[]{:S(2)}, u32[]{:S(2)}) %collective-permute-start.30) | collective-permute-done | bytes 81952 | tf_op jit(solution)/shard_map/ppermute | solution.py:457
  81.2 1.2 %collective-permute-done.28.rest_2_ = bf16[20,16,128]{2,1,0:T(8,128)(2,1)S(1)} collective-permute-done((bf16[20,16,128]{2,1,0:T(8,128)(2,1)S(1)}, bf16[20,16,128]{2,1,0:T(8,128)(2,1)S(1)}, u32[]{:S(2)}, u32[]{:S(2)}) %collective-permute-start.28) | collective-permute-done | bytes 81952 | tf_op jit(solution)/shard_map/ppermute | solution.py:457
  82.4 0.5 collective-permute-start.29
  82.9 0.8 shard_map.114
  83.8 0.8 shard_map.123
  84.5 0.8 shard_map.116
  85.4 1.5 %shard_map.122 = bf16[20,128,128]{2,1,0:T(8,128)(2,1)} custom-call(s32[2]{0:T(128)S(1)} %pad_add_fusion.here, bf16[20,16,128]{2,1,0:T(8,128)(2,1)S(1)} %get-tuple-element.80.rest_0_, bf16[20,16,128]{2,1,0:T(8,128)(2,1)S(1)} %collective-permute-done.27.rest_1_, bf16[20,16,128]{2,1,0:T(8,128)(2,1)S(1)} %collective-permute-done.28.rest_2_, ...), custom_call_target="tpu_custom_call" | custom-call | tf_op jit(solution)/shard_map/pallas_call | solution.py:39
  (19 shorter events, 0.1 us)
Async XLA Ops:
  1.6 11.5 %collective-permute-start.2 = (bf16[28,16,128]{2,1,0:T(8,128)(2,1)S(1)}, bf16[28,16,128]{2,1,0:T(8,128)(2,1)S(1)}, u32[]{:S(2)}, u32[]{:S(2)}) collective-permute-start(bf16[28,16,128]{2,1,0:T(8,128)(2,1)S(1)} %shard_map.111.rest_0_), channel_id=1, source_target_pairs={{0,3},{1,2},{2,1},{3,0},{4,7},{5,6},{6,5},{7,4},{8,11},{9,10},{10,... | collective-permute-start | bytes 344072 | tf_op jit(solution)/shard_map/ppermute | solution.py:461
  6.7 9.7 %collective-permute-start.1 = (bf16[28,16,128]{2,1,0:T(8,128)(2,1)S(1)}, bf16[28,16,128]{2,1,0:T(8,128)(2,1)S(1)}, u32[]{:S(2)}, u32[]{:S(2)}) collective-permute-start(bf16[28,16,128]{2,1,0:T(8,128)(2,1)S(1)} %shard_map.111.rest_0_), channel_id=1, source_target_pairs={{0,2},{1,3},{2,0},{3,1},{4,6},{5,7},{6,4},{7,5},{8,10},{9,11},{10,... | collective-permute-start | bytes 344072 | tf_op jit(solution)/shard_map/ppermute | solution.py:461
  6.7 9.7 %collective-permute-start = (bf16[28,16,128]{2,1,0:T(8,128)(2,1)S(1)}, bf16[28,16,128]{2,1,0:T(8,128)(2,1)S(1)}, u32[]{:S(2)}, u32[]{:S(2)}) collective-permute-start(bf16[28,16,128]{2,1,0:T(8,128)(2,1)S(1)} %shard_map.111.rest_0_), channel_id=1, source_target_pairs={{0,1},{1,0},{2,3},{3,2},{4,5},{5,4},{6,7},{7,6},{8,9},{9,8},{10,11... | collective-permute-start | bytes 344072 | tf_op jit(solution)/shard_map/ppermute | solution.py:461
  17.2 8.0 %collective-permute-start.8 = (bf16[44,16,128]{2,1,0:T(8,128)(2,1)S(1)}, bf16[44,16,128]{2,1,0:T(8,128)(2,1)S(1)}, u32[]{:S(2)}, u32[]{:S(2)}) collective-permute-start(bf16[44,16,128]{2,1,0:T(8,128)(2,1)S(1)} %get-tuple-element.48.rest_0_), channel_id=1, source_target_pairs={{0,24},{4,28},{8,16},{12,20},{16,8},{20,12},{24,0},{28,4},{1,25},{... | collective-permute-start | bytes 540680 | tf_op jit(solution)/shard_map/ppermute | solution.py:457
  19.7 7.9 %collective-permute-start.6 = (bf16[44,16,128]{2,1,0:T(8,128)(2,1)S(1)}, bf16[44,16,128]{2,1,0:T(8,128)(2,1)S(1)}, u32[]{:S(2)}, u32[]{:S(2)}) collective-permute-start(bf16[44,16,128]{2,1,0:T(8,128)(2,1)S(1)} %get-tuple-element.48.rest_0_), channel_id=1, source_target_pairs={{0,16},{4,20},{8,24},{12,28},{16,0},{20,4},{24,8},{28,12},{1,17},{... | collective-permute-start | bytes 540680 | tf_op jit(solution)/shard_map/ppermute | solution.py:457
  20.2 7.5 %collective-permute-start.4 = (bf16[44,16,128]{2,1,0:T(8,128)(2,1)S(1)}, bf16[44,16,128]{2,1,0:T(8,128)(2,1)S(1)}, u32[]{:S(2)}, u32[]{:S(2)}) collective-permute-start(bf16[44,16,128]{2,1,0:T(8,128)(2,1)S(1)} %get-tuple-element.48.rest_0_), channel_id=1, source_target_pairs={{0,8},{4,12},{8,0},{12,4},{16,24},{20,28},{24,16},{28,20},{1,9},{5... | collective-permute-start | bytes 540680 | tf_op jit(solution)/shard_map/ppermute | solution.py:457
  20.8 7.4 %collective-permute-start.3 = (bf16[44,16,128]{2,1,0:T(8,128)(2,1)S(1)}, bf16[44,16,128]{2,1,0:T(8,128)(2,1)S(1)}, u32[]{:S(2)}, u32[]{:S(2)}) collective-permute-start(bf16[44,16,128]{2,1,0:T(8,128)(2,1)S(1)} %get-tuple-element.48.rest_0_), channel_id=1, source_target_pairs={{0,4},{4,0},{8,12},{12,8},{16,20},{20,16},{24,28},{28,24},{1,5},{5... | collective-permute-start | bytes 540680 | tf_op jit(solution)/shard_map/ppermute | solution.py:457
  25.2 3.0 %collective-permute-start.9 = (bf16[44,16,128]{2,1,0:T(8,128)(2,1)S(1)}, bf16[44,16,128]{2,1,0:T(8,128)(2,1)S(1)}, u32[]{:S(2)}, u32[]{:S(2)}) collective-permute-start(bf16[44,16,128]{2,1,0:T(8,128)(2,1)S(1)} %collective-permute-done.8.rest_6_), channel_id=1, source_target_pairs={{0,4},{4,0},{8,12},{12,8},{16,20},{20,16},{24,28},{28,24},{1,5},{5... | collective-permute-start | bytes 540680 | tf_op jit(solution)/shard_map/ppermute | solution.py:457
  27.6 1.4 %collective-permute-start.7 = (bf16[44,16,128]{2,1,0:T(8,128)(2,1)S(1)}, bf16[44,16,128]{2,1,0:T(8,128)(2,1)S(1)}, u32[]{:S(2)}, u32[]{:S(2)}) collective-permute-start(bf16[44,16,128]{2,1,0:T(8,128)(2,1)S(1)} %collective-permute-done.6.rest_4_), channel_id=1, source_target_pairs={{0,4},{4,0},{8,12},{12,8},{16,20},{20,16},{24,28},{28,24},{1,5},{5... | collective-permute-start | bytes 540680 | tf_op jit(solution)/shard_map/ppermute | solution.py:457
  27.7 1.6 %collective-permute-start.5 = (bf16[44,16,128]{2,1,0:T(8,128)(2,1)S(1)}, bf16[44,16,128]{2,1,0:T(8,128)(2,1)S(1)}, u32[]{:S(2)}, u32[]{:S(2)}) collective-permute-start(bf16[44,16,128]{2,1,0:T(8,128)(2,1)S(1)} %collective-permute-done.4.rest_2_), channel_id=1, source_target_pairs={{0,4},{4,0},{8,12},{12,8},{16,20},{20,16},{24,28},{28,24},{1,5},{5... | collective-permute-start | bytes 540680 | tf_op jit(solution)/shard_map/ppermute | solution.py:457
  36.2 1.5 %collective-permute-start.14 = (bf16[44,16,128]{2,1,0:T(8,128)(2,1)S(1)}, bf16[44,16,128]{2,1,0:T(8,128)(2,1)S(1)}, u32[]{:S(2)}, u32[]{:S(2)}) collective-permute-start(bf16[44,16,128]{2,1,0:T(8,128)(2,1)S(1)} %get-tuple-element.62), channel_id=1, source_target_pairs={{0,4},{4,0},{8,12},{12,8},{16,20},{20,16},{24,28},{28,24},{1,5},{5... | collective-permute-start | bytes 540680 | tf_op jit(solution)/shard_map/ppermute | solution.py:457
  36.5 1.4 %collective-permute-start.15 = (bf16[44,16,128]{2,1,0:T(8,128)(2,1)S(1)}, bf16[44,16,128]{2,1,0:T(8,128)(2,1)S(1)}, u32[]{:S(2)}, u32[]{:S(2)}) collective-permute-start(bf16[44,16,128]{2,1,0:T(8,128)(2,1)S(1)} %get-tuple-element.63), channel_id=1, source_target_pairs={{0,4},{4,0},{8,12},{12,8},{16,20},{20,16},{24,28},{28,24},{1,5},{5... | collective-permute-start | bytes 540680 | tf_op jit(solution)/shard_map/ppermute | solution.py:457
  36.7 1.4 %collective-permute-start.16 = (bf16[44,16,128]{2,1,0:T(8,128)(2,1)S(1)}, bf16[44,16,128]{2,1,0:T(8,128)(2,1)S(1)}, u32[]{:S(2)}, u32[]{:S(2)}) collective-permute-start(bf16[44,16,128]{2,1,0:T(8,128)(2,1)S(1)} %get-tuple-element.64), channel_id=1, source_target_pairs={{0,4},{4,0},{8,12},{12,8},{16,20},{20,16},{24,28},{28,24},{1,5},{5... | collective-permute-start | bytes 540680 | tf_op jit(solution)/shard_map/ppermute | solution.py:457
  37.0 1.4 %collective-permute-start.17 = (bf16[44,16,128]{2,1,0:T(8,128)(2,1)S(1)}, bf16[44,16,128]{2,1,0:T(8,128)(2,1)S(1)}, u32[]{:S(2)}, u32[]{:S(2)}) collective-permute-start(bf16[44,16,128]{2,1,0:T(8,128)(2,1)S(1)} %get-tuple-element.65), channel_id=1, source_target_pairs={{0,4},{4,0},{8,12},{12,8},{16,20},{20,16},{24,28},{28,24},{1,5},{5... | collective-permute-start | bytes 540680 | tf_op jit(solution)/shard_map/ppermute | solution.py:457
  37.3 10.6 %collective-permute-start.10 = (bf16[1,128,1280]{2,1,0:T(8,128)(2,1)S(1)}, bf16[1,128,1280]{2,1,0:T(8,128)(2,1)S(1)}, u32[]{:S(2)}, u32[]{:S(2)}) collective-permute-start(bf16[1,128,1280]{2,1,0:T(8,128)(2,1)S(1)} %get-tuple-element.52), channel_id=1, source_target_pairs={{0,1},{1,0},{2,3},{3,2},{4,5},{5,4},{6,7},{7,6},{8,9},{9,8},{10,11... | collective-permute-start | bytes 983048 | tf_op jit(solution)/shard_map/ppermute | solution.py:461
  38.6 9.2 %collective-permute-start.18 = (bf16[44,16,128]{2,1,0:T(8,128)(2,1)S(1)}, bf16[44,16,128]{2,1,0:T(8,128)(2,1)S(1)}, u32[]{:S(2)}, u32[]{:S(2)}) collective-permute-start(bf16[44,16,128]{2,1,0:T(8,128)(2,1)S(1)} %get-tuple-element.67), channel_id=1, source_target_pairs={{0,8},{4,12},{8,0},{12,4},{16,24},{20,28},{24,16},{28,20},{1,9},{5... | collective-permute-start | bytes 540680 | tf_op jit(solution)/shard_map/ppermute | solution.py:457
  40.1 10.6 %collective-permute-start.19 = (bf16[44,16,128]{2,1,0:T(8,128)(2,1)S(1)}, bf16[44,16,128]{2,1,0:T(8,128)(2,1)S(1)}, u32[]{:S(2)}, u32[]{:S(2)}) collective-permute-start(bf16[44,16,128]{2,1,0:T(8,128)(2,1)S(1)} %get-tuple-element.68), channel_id=1, source_target_pairs={{0,16},{4,20},{8,24},{12,28},{16,0},{20,4},{24,8},{28,12},{1,17},{... | collective-permute-start | bytes 540680 | tf_op jit(solution)/shard_map/ppermute | solution.py:457
  41.0 37.0 %collective-permute-start.13 = (bf16[128,1280]{1,0:T(8,128)(2,1)S(1)}, bf16[128,1280]{1,0:T(8,128)(2,1)S(1)}, u32[]{:S(2)}, u32[]{:S(2)}) collective-permute-start(bf16[128,1280]{1,0:T(8,128)(2,1)S(1)} %get-tuple-element.55), channel_id=1, source_target_pairs={{0,1},{1,0},{2,3},{3,2},{4,5},{5,4},{6,7},{7,6},{8,9},{9,8},{10,11... | collective-permute-start | bytes 983048 | tf_op jit(solution)/shard_map/ppermute | solution.py:461
  41.9 10.9 %collective-permute-start.20 = (bf16[44,16,128]{2,1,0:T(8,128)(2,1)S(1)}, bf16[44,16,128]{2,1,0:T(8,128)(2,1)S(1)}, u32[]{:S(2)}, u32[]{:S(2)}) collective-permute-start(bf16[44,16,128]{2,1,0:T(8,128)(2,1)S(1)} %get-tuple-element.69), channel_id=1, source_target_pairs={{0,24},{4,28},{8,16},{12,20},{16,8},{20,12},{24,0},{28,4},{1,25},{... | collective-permute-start | bytes 540680 | tf_op jit(solution)/shard_map/ppermute | solution.py:457
  47.8 16.5 %collective-permute-start.24 = (f32[2,8,2048]{2,1,0:T(8,128)S(1)}, f32[2,8,2048]{2,1,0:T(8,128)S(1)}, u32[]{:S(2)}, u32[]{:S(2)}) collective-permute-start(f32[2,8,2048]{2,1,0:T(8,128)S(1)} %get-tuple-element.77), channel_id=1, source_target_pairs={{0,1},{1,0},{2,3},{3,2},{4,5},{5,4},{6,7},{7,6},{8,9},{9,8},{10,11... | collective-permute-start | bytes 393224 | tf_op jit(solution)/shard_map/ppermute | solution.py:461
  47.8 16.5 %collective-permute-start.25 = (f32[2,8,2048]{2,1,0:T(8,128)S(1)}, f32[2,8,2048]{2,1,0:T(8,128)S(1)}, u32[]{:S(2)}, u32[]{:S(2)}) collective-permute-start(f32[2,8,2048]{2,1,0:T(8,128)S(1)} %get-tuple-element.78), channel_id=1, source_target_pairs={{0,2},{1,3},{2,0},{3,1},{4,6},{5,7},{6,4},{7,5},{8,10},{9,11},{10,... | collective-permute-start | bytes 393224 | tf_op jit(solution)/shard_map/ppermute | solution.py:461
  50.7 16.1 %collective-permute-start.26 = (f32[2,8,2048]{2,1,0:T(8,128)S(1)}, f32[2,8,2048]{2,1,0:T(8,128)S(1)}, u32[]{:S(2)}, u32[]{:S(2)}) collective-permute-start(f32[2,8,2048]{2,1,0:T(8,128)S(1)} %get-tuple-element.79), channel_id=1, source_target_pairs={{0,3},{1,2},{2,1},{3,0},{4,7},{5,6},{6,5},{7,4},{8,11},{9,10},{10,... | collective-permute-start | bytes 393224 | tf_op jit(solution)/shard_map/ppermute | solution.py:461
  52.8 29.6 %collective-permute-start.11 = (bf16[64,1280]{1,0:T(8,128)(2,1)S(1)}, bf16[64,1280]{1,0:T(8,128)(2,1)S(1)}, u32[]{:S(2)}, u32[]{:S(2)}) collective-permute-start(bf16[64,1280]{1,0:T(8,128)(2,1)S(1)} %get-tuple-element.53), channel_id=1, source_target_pairs={{0,2},{1,3},{2,0},{3,1},{4,6},{5,7},{6,4},{7,5},{8,10},{9,11},{10,... | collective-permute-start | bytes 491528 | tf_op jit(solution)/shard_map/ppermute | solution.py:461
  64.3 4.4 %collective-permute-start.21 = (bf16[11,16,128]{2,1,0:T(8,128)(2,1)S(1)}, bf16[11,16,128]{2,1,0:T(8,128)(2,1)S(1)}, u32[]{:S(2)}, u32[]{:S(2)}) collective-permute-start(bf16[11,16,128]{2,1,0:T(8,128)(2,1)S(1)} %get-tuple-element.71), channel_id=1, source_target_pairs={{0,1},{1,0},{2,3},{3,2},{4,5},{5,4},{6,7},{7,6},{8,9},{9,8},{10,11... | collective-permute-start | bytes 135176 | tf_op jit(solution)/shard_map/ppermute | solution.py:461
  64.3 7.2 %collective-permute-start.22 = (bf16[11,16,128]{2,1,0:T(8,128)(2,1)S(1)}, bf16[11,16,128]{2,1,0:T(8,128)(2,1)S(1)}, u32[]{:S(2)}, u32[]{:S(2)}) collective-permute-start(bf16[11,16,128]{2,1,0:T(8,128)(2,1)S(1)} %get-tuple-element.72), channel_id=1, source_target_pairs={{0,2},{1,3},{2,0},{3,1},{4,6},{5,7},{6,4},{7,5},{8,10},{9,11},{10,... | collective-permute-start | bytes 135176 | tf_op jit(solution)/shard_map/ppermute | solution.py:461
  66.8 5.8 %collective-permute-start.23 = (bf16[11,16,128]{2,1,0:T(8,128)(2,1)S(1)}, bf16[11,16,128]{2,1,0:T(8,128)(2,1)S(1)}, u32[]{:S(2)}, u32[]{:S(2)}) collective-permute-start(bf16[11,16,128]{2,1,0:T(8,128)(2,1)S(1)} %get-tuple-element.73), channel_id=1, source_target_pairs={{0,3},{1,2},{2,1},{3,0},{4,7},{5,6},{6,5},{7,4},{8,11},{9,10},{10,... | collective-permute-start | bytes 135176 | tf_op jit(solution)/shard_map/ppermute | solution.py:461
  73.7 5.4 %collective-permute-start.32 = (bf16[20,16,128]{2,1,0:T(8,128)(2,1)S(1)}, bf16[20,16,128]{2,1,0:T(8,128)(2,1)S(1)}, u32[]{:S(2)}, u32[]{:S(2)}) collective-permute-start(bf16[20,16,128]{2,1,0:T(8,128)(2,1)S(1)} %get-tuple-element.80.rest_0_), channel_id=1, source_target_pairs={{0,24},{4,28},{8,16},{12,20},{16,8},{20,12},{24,0},{28,4},{1,25},{... | collective-permute-start | bytes 245768 | tf_op jit(solution)/shard_map/ppermute | solution.py:457
  75.5 9.1 %collective-permute-start.12 = (bf16[64,1280]{1,0:T(8,128)(2,1)S(1)}, bf16[64,1280]{1,0:T(8,128)(2,1)S(1)}, u32[]{:S(2)}, u32[]{:S(2)}) collective-permute-start(bf16[64,1280]{1,0:T(8,128)(2,1)S(1)} %get-tuple-element.54), channel_id=1, source_target_pairs={{0,2},{1,3},{2,0},{3,1},{4,6},{5,7},{6,4},{7,5},{8,10},{9,11},{10,... | collective-permute-start | bytes 491528 | tf_op jit(solution)/shard_map/ppermute | solution.py:461
  76.7 4.4 %collective-permute-start.30 = (bf16[20,16,128]{2,1,0:T(8,128)(2,1)S(1)}, bf16[20,16,128]{2,1,0:T(8,128)(2,1)S(1)}, u32[]{:S(2)}, u32[]{:S(2)}) collective-permute-start(bf16[20,16,128]{2,1,0:T(8,128)(2,1)S(1)} %get-tuple-element.80.rest_0_), channel_id=1, source_target_pairs={{0,16},{4,20},{8,24},{12,28},{16,0},{20,4},{24,8},{28,12},{1,17},{... | collective-permute-start | bytes 245768 | tf_op jit(solution)/shard_map/ppermute | solution.py:457
  78.0 4.4 %collective-permute-start.28 = (bf16[20,16,128]{2,1,0:T(8,128)(2,1)S(1)}, bf16[20,16,128]{2,1,0:T(8,128)(2,1)S(1)}, u32[]{:S(2)}, u32[]{:S(2)}) collective-permute-start(bf16[20,16,128]{2,1,0:T(8,128)(2,1)S(1)} %get-tuple-element.80.rest_0_), channel_id=1, source_target_pairs={{0,8},{4,12},{8,0},{12,4},{16,24},{20,28},{24,16},{28,20},{1,9},{5... | collective-permute-start | bytes 245768 | tf_op jit(solution)/shard_map/ppermute | solution.py:457
  79.1 6.3 %collective-permute-start.27 = (bf16[20,16,128]{2,1,0:T(8,128)(2,1)S(1)}, bf16[20,16,128]{2,1,0:T(8,128)(2,1)S(1)}, u32[]{:S(2)}, u32[]{:S(2)}) collective-permute-start(bf16[20,16,128]{2,1,0:T(8,128)(2,1)S(1)} %get-tuple-element.80.rest_0_), channel_id=1, source_target_pairs={{0,4},{4,0},{8,12},{12,8},{16,20},{20,16},{24,28},{28,24},{1,5},{5... | collective-permute-start | bytes 245768 | tf_op jit(solution)/shard_map/ppermute | solution.py:457
  81.2 4.2 %collective-permute-start.33 = (bf16[20,16,128]{2,1,0:T(8,128)(2,1)S(1)}, bf16[20,16,128]{2,1,0:T(8,128)(2,1)S(1)}, u32[]{:S(2)}, u32[]{:S(2)}) collective-permute-start(bf16[20,16,128]{2,1,0:T(8,128)(2,1)S(1)} %collective-permute-done.32.rest_6_), channel_id=1, source_target_pairs={{0,4},{4,0},{8,12},{12,8},{16,20},{20,16},{24,28},{28,24},{1,5},{5... | collective-permute-start | bytes 245768 | tf_op jit(solution)/shard_map/ppermute | solution.py:457
  82.4 3.0 %collective-permute-start.31 = (bf16[20,16,128]{2,1,0:T(8,128)(2,1)S(1)}, bf16[20,16,128]{2,1,0:T(8,128)(2,1)S(1)}, u32[]{:S(2)}, u32[]{:S(2)}) collective-permute-start(bf16[20,16,128]{2,1,0:T(8,128)(2,1)S(1)} %collective-permute-done.30.rest_4_), channel_id=1, source_target_pairs={{0,4},{4,0},{8,12},{12,8},{16,20},{20,16},{24,28},{28,24},{1,5},{5... | collective-permute-start | bytes 245768 | tf_op jit(solution)/shard_map/ppermute | solution.py:457
  82.4 3.0 %collective-permute-start.29 = (bf16[20,16,128]{2,1,0:T(8,128)(2,1)S(1)}, bf16[20,16,128]{2,1,0:T(8,128)(2,1)S(1)}, u32[]{:S(2)}, u32[]{:S(2)}) collective-permute-start(bf16[20,16,128]{2,1,0:T(8,128)(2,1)S(1)} %collective-permute-done.28.rest_2_), channel_id=1, source_target_pairs={{0,4},{4,0},{8,12},{12,8},{16,20},{20,16},{24,28},{28,24},{1,5},{5... | collective-permute-start | bytes 245768 | tf_op jit(solution)/shard_map/ppermute | solution.py:457
